TPU v7x, 512 devices: a whole 4x8x8 slice. The times are simulated.
512 devices in a mesh: flow: 64 (over y, z), lat: 8 (over x, core).
Axes of the slice: x: 4, y: 8, z: 8, core: 2. Of those that a mesh axis runs over, the one named last changes fastest.
Arguments:
- concentration: float32 [3, 1024, 256, 128], P(None, 'flow', 'lat'), may hold values from 0 to 2
- courant: float32 [3, 1024, 256, 128], P(None, 'flow', 'lat'), may hold values from 500 to 4000
- rates: float32 [2, 1024, 256, 128], P(None, 'flow', 'lat'), may hold values from 0.2 to 3
- spread: float32 [256, 128], P('lat'), may hold values from 0.02 to 0.2
- inlet: float32 [3, 256, 128], P(None, 'lat'), may hold values from 200 to 2000
Outputs:
- fresh: float32 [3, 1024, 256, 128], P(None, 'flow', 'lat')
All inputs are finite; a program needn't handle non-finite values.
Results may differ from a plain program's by a relative error of at most 0.000066.
Values sent between devices are 32-bit elements; how exact they have to be, the bound alone decides.
No kernel may reach another device: no remote copies, remote signals or barrier semaphores. Data moves between devices by JAX's collectives and lax.ppermute only.
A program may use at most 64 MiB of HBM per device.

v0:
```python
import jax
import jax.numpy as jnp
from jax import lax
from jax.sharding import PartitionSpec as P


def padded_2(block, sides, width):
    for axis, dim in sides:
        count = lax.axis_size(axis)
        forward = [(i, i + 1) for i in range(count - 1)]
        backward = [(target, source) for source, target in forward]
        low = lax.ppermute(
            lax.slice_in_dim(block, block.shape[dim] - width, None, axis=dim), axis, forward
        )
        high = lax.ppermute(lax.slice_in_dim(block, 0, width, axis=dim), axis, backward)
        block = jnp.concatenate([low, block, high], axis=dim)
    return block


def from_behind(block, axis, distance):
    devices = range(lax.axis_size(axis))
    route = [(i - distance, i) for i in devices if i - distance in devices]
    return lax.ppermute(block, axis, route)


def cell_values(flux, src, coeffs):
    cour_a, cour_p, cour_v, rate_ap, rate_pv = coeffs
    first = (src[0] + flux[0]) / (1.0 + cour_a + rate_ap)
    second = (src[1] + flux[1] + rate_ap * first) / (1.0 + cour_p + rate_pv)
    third = (src[2] + flux[2] + rate_pv * second) / (1.0 + cour_v)
    return (first, second, third)


def cell_flux(flux, src, coeffs):
    first, second, third = cell_values(flux, src, coeffs)
    return (coeffs[0] * first, coeffs[1] * second, coeffs[2] * third)


def apply_map(matrix, offset, flux):
    out_a = matrix[0] * flux[0] + offset[0]
    out_p = matrix[1] * flux[0] + matrix[2] * flux[1] + offset[1]
    out_v = matrix[3] * flux[0] + matrix[4] * flux[1] + matrix[5] * flux[2] + offset[2]
    return jnp.stack([out_a, out_p, out_v])


def per_device(concentration, courant, rates, spread, inlet):
    padded = padded_2(concentration, (("lat", 2),), 1)
    zpadded = jnp.pad(concentration, ((0, 0), (0, 0), (0, 0), (1, 1)))
    beside = padded[:, :, 2:, :] + padded[:, :, :-2, :] + zpadded[..., 2:] + zpadded[..., :-2]
    source = concentration + spread[None, None] * (beside - 4.0 * concentration)
    cells = concentration.shape[1]
    ones = jnp.ones_like(spread)
    zeros = jnp.zeros_like(spread)
    nothing = (0.0, 0.0, 0.0)

    def coeffs_at(index):
        return (
            courant[0, index],
            courant[1, index],
            courant[2, index],
            rates[0, index],
            rates[1, index],
        )

    col_a = (ones, zeros, zeros)
    col_p = (zeros, ones, zeros)
    col_v = (zeros, zeros, ones)
    shifted = (zeros, zeros, zeros)
    for index in range(cells):
        coeffs = coeffs_at(index)
        col_a = cell_flux(col_a, nothing, coeffs)
        col_p = cell_flux(col_p, nothing, coeffs)
        col_v = cell_flux(col_v, nothing, coeffs)
        shifted = cell_flux(shifted, source[:, index], coeffs)
    matrix = jnp.stack([col_a[0], col_a[1], col_p[1], col_a[2], col_p[2], col_v[2]])
    offset = jnp.stack(shifted)
    position = lax.axis_index("flow")
    start = jnp.where(position == 0, inlet, jnp.zeros_like(inlet))

    def relay_step(turn, incoming):
        outgoing = apply_map(matrix, offset, incoming)
        arrived = from_behind(outgoing, "flow", 1)
        return jnp.where(position == 0, inlet, arrived)

    incoming = lax.fori_loop(0, lax.axis_size("flow") - 1, relay_step, start)
    flux = (incoming[0], incoming[1], incoming[2])
    values = []
    for index in range(cells):
        coeffs = coeffs_at(index)
        first, second, third = cell_values(flux, source[:, index], coeffs)
        values.append(jnp.stack([first, second, third]))
        flux = (coeffs[0] * first, coeffs[1] * second, coeffs[2] * third)
    return jnp.stack(values, axis=1)


def solution(mesh):
    in_specs = (
        P(None, "flow", "lat", None),
        P(None, "flow", "lat", None),
        P(None, "flow", "lat", None),
        P("lat", None),
        P(None, "lat", None),
    )
    out_specs = P(None, "flow", "lat", None)
    return jax.shard_map(
        per_device, mesh=mesh, in_specs=in_specs, out_specs=out_specs, check_vma=False
    )
```

profile of v0, /device:TPU:36, one launch (start us, length us, event | category | flops | bytes accessed | tf_op | source)
XLA Modules:
  0.0 610.1 jit_solution(5488121151248385184)
XLA Ops:
  12.9 595.2 %while.12 = (s32[]{:T(128)}, f32[3,32,128]{2,1,0:T(8,128)S(1)}, pred[]{:T(512)}, f32[32,128]{1,0:T(8,128)S(1)}, f32[32,128]{1,0:T(8,128)S(1)}, /*index=5*/f32[32...) while((s32[]{:T(128)}, f32[3,32,128]{2,1,0:T(8,128)S(1)}, ...), condition=%wide.region_1.2_spmd, body=%wide.region_0.1_spmd.sunk | while | flops 86018 | bytes 688302 | solution.py:85
  17.2 8.6 %collective-permute-done = f32[3,32,128]{2,1,0:T(8,128)S(1)} collective-permute-done((f32[3,32,128]{2,1,0:T(8,128)S(1)}, f32[3,32,128]{2,1,0:T(8,128)S(1)}, u32[]{:S(2)}, u32[]{:S(2)}) %collective-permute-start) | collective-permute-done | bytes 49184 | tf_op jit(solution)/shard_map/while/body/eval_jaxpr/ppermute | solution.py:23
  27.8 7.4 %collective-permute-done = f32[3,32,128]{2,1,0:T(8,128)S(1)} collective-permute-done((f32[3,32,128]{2,1,0:T(8,128)S(1)}, f32[3,32,128]{2,1,0:T(8,128)S(1)}, u32[]{:S(2)}, u32[]{:S(2)}) %collective-permute-start) | collective-permute-done | bytes 49184 | tf_op jit(solution)/shard_map/while/body/eval_jaxpr/ppermute | solution.py:23
  37.2 7.4 %collective-permute-done = f32[3,32,128]{2,1,0:T(8,128)S(1)} collective-permute-done((f32[3,32,128]{2,1,0:T(8,128)S(1)}, f32[3,32,128]{2,1,0:T(8,128)S(1)}, u32[]{:S(2)}, u32[]{:S(2)}) %collective-permute-start) | collective-permute-done | bytes 49184 | tf_op jit(solution)/shard_map/while/body/eval_jaxpr/ppermute | solution.py:23
  46.6 7.4 %collective-permute-done = f32[3,32,128]{2,1,0:T(8,128)S(1)} collective-permute-done((f32[3,32,128]{2,1,0:T(8,128)S(1)}, f32[3,32,128]{2,1,0:T(8,128)S(1)}, u32[]{:S(2)}, u32[]{:S(2)}) %collective-permute-start) | collective-permute-done | bytes 49184 | tf_op jit(solution)/shard_map/while/body/eval_jaxpr/ppermute | solution.py:23
  55.9 7.4 %collective-permute-done = f32[3,32,128]{2,1,0:T(8,128)S(1)} collective-permute-done((f32[3,32,128]{2,1,0:T(8,128)S(1)}, f32[3,32,128]{2,1,0:T(8,128)S(1)}, u32[]{:S(2)}, u32[]{:S(2)}) %collective-permute-start) | collective-permute-done | bytes 49184 | tf_op jit(solution)/shard_map/while/body/eval_jaxpr/ppermute | solution.py:23
  65.3 7.4 %collective-permute-done = f32[3,32,128]{2,1,0:T(8,128)S(1)} collective-permute-done((f32[3,32,128]{2,1,0:T(8,128)S(1)}, f32[3,32,128]{2,1,0:T(8,128)S(1)}, u32[]{:S(2)}, u32[]{:S(2)}) %collective-permute-start) | collective-permute-done | bytes 49184 | tf_op jit(solution)/shard_map/while/body/eval_jaxpr/ppermute | solution.py:23
  74.7 7.8 %collective-permute-done = f32[3,32,128]{2,1,0:T(8,128)S(1)} collective-permute-done((f32[3,32,128]{2,1,0:T(8,128)S(1)}, f32[3,32,128]{2,1,0:T(8,128)S(1)}, u32[]{:S(2)}, u32[]{:S(2)}) %collective-permute-start) | collective-permute-done | bytes 49184 | tf_op jit(solution)/shard_map/while/body/eval_jaxpr/ppermute | solution.py:23
  140.7 7.5 %collective-permute-done = f32[3,32,128]{2,1,0:T(8,128)S(1)} collective-permute-done((f32[3,32,128]{2,1,0:T(8,128)S(1)}, f32[3,32,128]{2,1,0:T(8,128)S(1)}, u32[]{:S(2)}, u32[]{:S(2)}) %collective-permute-start) | collective-permute-done | bytes 49184 | tf_op jit(solution)/shard_map/while/body/eval_jaxpr/ppermute | solution.py:23
  178.3 7.4 %collective-permute-done = f32[3,32,128]{2,1,0:T(8,128)S(1)} collective-permute-done((f32[3,32,128]{2,1,0:T(8,128)S(1)}, f32[3,32,128]{2,1,0:T(8,128)S(1)}, u32[]{:S(2)}, u32[]{:S(2)}) %collective-permute-start) | collective-permute-done | bytes 49184 | tf_op jit(solution)/shard_map/while/body/eval_jaxpr/ppermute | solution.py:23
  206.5 7.4 %collective-permute-done = f32[3,32,128]{2,1,0:T(8,128)S(1)} collective-permute-done((f32[3,32,128]{2,1,0:T(8,128)S(1)}, f32[3,32,128]{2,1,0:T(8,128)S(1)}, u32[]{:S(2)}, u32[]{:S(2)}) %collective-permute-start) | collective-permute-done | bytes 49184 | tf_op jit(solution)/shard_map/while/body/eval_jaxpr/ppermute | solution.py:23
  234.6 7.4 %collective-permute-done = f32[3,32,128]{2,1,0:T(8,128)S(1)} collective-permute-done((f32[3,32,128]{2,1,0:T(8,128)S(1)}, f32[3,32,128]{2,1,0:T(8,128)S(1)}, u32[]{:S(2)}, u32[]{:S(2)}) %collective-permute-start) | collective-permute-done | bytes 49184 | tf_op jit(solution)/shard_map/while/body/eval_jaxpr/ppermute | solution.py:23
  281.4 7.5 %collective-permute-done = f32[3,32,128]{2,1,0:T(8,128)S(1)} collective-permute-done((f32[3,32,128]{2,1,0:T(8,128)S(1)}, f32[3,32,128]{2,1,0:T(8,128)S(1)}, u32[]{:S(2)}, u32[]{:S(2)}) %collective-permute-start) | collective-permute-done | bytes 49184 | tf_op jit(solution)/shard_map/while/body/eval_jaxpr/ppermute | solution.py:23
  300.3 7.4 %collective-permute-done = f32[3,32,128]{2,1,0:T(8,128)S(1)} collective-permute-done((f32[3,32,128]{2,1,0:T(8,128)S(1)}, f32[3,32,128]{2,1,0:T(8,128)S(1)}, u32[]{:S(2)}, u32[]{:S(2)}) %collective-permute-start) | collective-permute-done | bytes 49184 | tf_op jit(solution)/shard_map/while/body/eval_jaxpr/ppermute | solution.py:23
  328.4 7.4 %collective-permute-done = f32[3,32,128]{2,1,0:T(8,128)S(1)} collective-permute-done((f32[3,32,128]{2,1,0:T(8,128)S(1)}, f32[3,32,128]{2,1,0:T(8,128)S(1)}, u32[]{:S(2)}, u32[]{:S(2)}) %collective-permute-start) | collective-permute-done | bytes 49184 | tf_op jit(solution)/shard_map/while/body/eval_jaxpr/ppermute | solution.py:23
  347.1 7.9 %collective-permute-done = f32[3,32,128]{2,1,0:T(8,128)S(1)} collective-permute-done((f32[3,32,128]{2,1,0:T(8,128)S(1)}, f32[3,32,128]{2,1,0:T(8,128)S(1)}, u32[]{:S(2)}, u32[]{:S(2)}) %collective-permute-start) | collective-permute-done | bytes 49184 | tf_op jit(solution)/shard_map/while/body/eval_jaxpr/ppermute | solution.py:23
  357.0 7.4 %collective-permute-done = f32[3,32,128]{2,1,0:T(8,128)S(1)} collective-permute-done((f32[3,32,128]{2,1,0:T(8,128)S(1)}, f32[3,32,128]{2,1,0:T(8,128)S(1)}, u32[]{:S(2)}, u32[]{:S(2)}) %collective-permute-start) | collective-permute-done | bytes 49184 | tf_op jit(solution)/shard_map/while/body/eval_jaxpr/ppermute | solution.py:23
  413.2 7.4 %collective-permute-done = f32[3,32,128]{2,1,0:T(8,128)S(1)} collective-permute-done((f32[3,32,128]{2,1,0:T(8,128)S(1)}, f32[3,32,128]{2,1,0:T(8,128)S(1)}, u32[]{:S(2)}, u32[]{:S(2)}) %collective-permute-start) | collective-permute-done | bytes 49184 | tf_op jit(solution)/shard_map/while/body/eval_jaxpr/ppermute | solution.py:23
  422.6 7.4 %collective-permute-done = f32[3,32,128]{2,1,0:T(8,128)S(1)} collective-permute-done((f32[3,32,128]{2,1,0:T(8,128)S(1)}, f32[3,32,128]{2,1,0:T(8,128)S(1)}, u32[]{:S(2)}, u32[]{:S(2)}) %collective-permute-start) | collective-permute-done | bytes 49184 | tf_op jit(solution)/shard_map/while/body/eval_jaxpr/ppermute | solution.py:23
  450.7 7.4 %collective-permute-done = f32[3,32,128]{2,1,0:T(8,128)S(1)} collective-permute-done((f32[3,32,128]{2,1,0:T(8,128)S(1)}, f32[3,32,128]{2,1,0:T(8,128)S(1)}, u32[]{:S(2)}, u32[]{:S(2)}) %collective-permute-start) | collective-permute-done | bytes 49184 | tf_op jit(solution)/shard_map/while/body/eval_jaxpr/ppermute | solution.py:23
  488.2 7.4 %collective-permute-done = f32[3,32,128]{2,1,0:T(8,128)S(1)} collective-permute-done((f32[3,32,128]{2,1,0:T(8,128)S(1)}, f32[3,32,128]{2,1,0:T(8,128)S(1)}, u32[]{:S(2)}, u32[]{:S(2)}) %collective-permute-start) | collective-permute-done | bytes 49184 | tf_op jit(solution)/shard_map/while/body/eval_jaxpr/ppermute | solution.py:23
  497.6 7.4 %collective-permute-done = f32[3,32,128]{2,1,0:T(8,128)S(1)} collective-permute-done((f32[3,32,128]{2,1,0:T(8,128)S(1)}, f32[3,32,128]{2,1,0:T(8,128)S(1)}, u32[]{:S(2)}, u32[]{:S(2)}) %collective-permute-start) | collective-permute-done | bytes 49184 | tf_op jit(solution)/shard_map/while/body/eval_jaxpr/ppermute | solution.py:23
  525.7 7.4 %collective-permute-done = f32[3,32,128]{2,1,0:T(8,128)S(1)} collective-permute-done((f32[3,32,128]{2,1,0:T(8,128)S(1)}, f32[3,32,128]{2,1,0:T(8,128)S(1)}, u32[]{:S(2)}, u32[]{:S(2)}) %collective-permute-start) | collective-permute-done | bytes 49184 | tf_op jit(solution)/shard_map/while/body/eval_jaxpr/ppermute | solution.py:23
  553.8 7.4 %collective-permute-done = f32[3,32,128]{2,1,0:T(8,128)S(1)} collective-permute-done((f32[3,32,128]{2,1,0:T(8,128)S(1)}, f32[3,32,128]{2,1,0:T(8,128)S(1)}, u32[]{:S(2)}, u32[]{:S(2)}) %collective-permute-start) | collective-permute-done | bytes 49184 | tf_op jit(solution)/shard_map/while/body/eval_jaxpr/ppermute | solution.py:23
  (336 shorter events, 435.2 us)
Async XLA Ops:
  12.9 12.9 %collective-permute-start = (f32[3,32,128]{2,1,0:T(8,128)S(1)}, f32[3,32,128]{2,1,0:T(8,128)S(1)}, u32[]{:S(2)}, u32[]{:S(2)}) collective-permute-start(f32[3,32,128]{2,1,0:T(8,128)S(1)} %pad_maximum_fusion.4), channel_id=1, source_target_pairs={{0,8},{8,16},{16,24},{24,32},{32,40},{40,48},{48,56},{56,64},{64,7... | collective-permute-start | bytes 147464 | tf_op jit(solution)/shard_map/while/body/eval_jaxpr/ppermute | solution.py:23
  25.9 9.3 %collective-permute-start = (f32[3,32,128]{2,1,0:T(8,128)S(1)}, f32[3,32,128]{2,1,0:T(8,128)S(1)}, u32[]{:S(2)}, u32[]{:S(2)}) collective-permute-start(f32[3,32,128]{2,1,0:T(8,128)S(1)} %pad_maximum_fusion.4), channel_id=1, source_target_pairs={{0,8},{8,16},{16,24},{24,32},{32,40},{40,48},{48,56},{56,64},{64,7... | collective-permute-start | bytes 147464 | tf_op jit(solution)/shard_map/while/body/eval_jaxpr/ppermute | solution.py:23
  35.3 9.3 %collective-permute-start = (f32[3,32,128]{2,1,0:T(8,128)S(1)}, f32[3,32,128]{2,1,0:T(8,128)S(1)}, u32[]{:S(2)}, u32[]{:S(2)}) collective-permute-start(f32[3,32,128]{2,1,0:T(8,128)S(1)} %pad_maximum_fusion.4), channel_id=1, source_target_pairs={{0,8},{8,16},{16,24},{24,32},{32,40},{40,48},{48,56},{56,64},{64,7... | collective-permute-start | bytes 147464 | tf_op jit(solution)/shard_map/while/body/eval_jaxpr/ppermute | solution.py:23
  44.6 9.3 %collective-permute-start = (f32[3,32,128]{2,1,0:T(8,128)S(1)}, f32[3,32,128]{2,1,0:T(8,128)S(1)}, u32[]{:S(2)}, u32[]{:S(2)}) collective-permute-start(f32[3,32,128]{2,1,0:T(8,128)S(1)} %pad_maximum_fusion.4), channel_id=1, source_target_pairs={{0,8},{8,16},{16,24},{24,32},{32,40},{40,48},{48,56},{56,64},{64,7... | collective-permute-start | bytes 147464 | tf_op jit(solution)/shard_map/while/body/eval_jaxpr/ppermute | solution.py:23
  54.0 9.3 %collective-permute-start = (f32[3,32,128]{2,1,0:T(8,128)S(1)}, f32[3,32,128]{2,1,0:T(8,128)S(1)}, u32[]{:S(2)}, u32[]{:S(2)}) collective-permute-start(f32[3,32,128]{2,1,0:T(8,128)S(1)} %pad_maximum_fusion.4), channel_id=1, source_target_pairs={{0,8},{8,16},{16,24},{24,32},{32,40},{40,48},{48,56},{56,64},{64,7... | collective-permute-start | bytes 147464 | tf_op jit(solution)/shard_map/while/body/eval_jaxpr/ppermute | solution.py:23
  72.8 9.7 %collective-permute-start = (f32[3,32,128]{2,1,0:T(8,128)S(1)}, f32[3,32,128]{2,1,0:T(8,128)S(1)}, u32[]{:S(2)}, u32[]{:S(2)}) collective-permute-start(f32[3,32,128]{2,1,0:T(8,128)S(1)} %pad_maximum_fusion.4), channel_id=1, source_target_pairs={{0,8},{8,16},{16,24},{24,32},{32,40},{40,48},{48,56},{56,64},{64,7... | collective-permute-start | bytes 147464 | tf_op jit(solution)/shard_map/while/body/eval_jaxpr/ppermute | solution.py:23
  129.4 9.3 %collective-permute-start = (f32[3,32,128]{2,1,0:T(8,128)S(1)}, f32[3,32,128]{2,1,0:T(8,128)S(1)}, u32[]{:S(2)}, u32[]{:S(2)}) collective-permute-start(f32[3,32,128]{2,1,0:T(8,128)S(1)} %pad_maximum_fusion.4), channel_id=1, source_target_pairs={{0,8},{8,16},{16,24},{24,32},{32,40},{40,48},{48,56},{56,64},{64,7... | collective-permute-start | bytes 147464 | tf_op jit(solution)/shard_map/while/body/eval_jaxpr/ppermute | solution.py:23
  138.8 9.5 %collective-permute-start = (f32[3,32,128]{2,1,0:T(8,128)S(1)}, f32[3,32,128]{2,1,0:T(8,128)S(1)}, u32[]{:S(2)}, u32[]{:S(2)}) collective-permute-start(f32[3,32,128]{2,1,0:T(8,128)S(1)} %pad_maximum_fusion.4), channel_id=1, source_target_pairs={{0,8},{8,16},{16,24},{24,32},{32,40},{40,48},{48,56},{56,64},{64,7... | collective-permute-start | bytes 147464 | tf_op jit(solution)/shard_map/while/body/eval_jaxpr/ppermute | solution.py:23
  148.3 9.3 %collective-permute-start = (f32[3,32,128]{2,1,0:T(8,128)S(1)}, f32[3,32,128]{2,1,0:T(8,128)S(1)}, u32[]{:S(2)}, u32[]{:S(2)}) collective-permute-start(f32[3,32,128]{2,1,0:T(8,128)S(1)} %pad_maximum_fusion.4), channel_id=1, source_target_pairs={{0,8},{8,16},{16,24},{24,32},{32,40},{40,48},{48,56},{56,64},{64,7... | collective-permute-start | bytes 147464 | tf_op jit(solution)/shard_map/while/body/eval_jaxpr/ppermute | solution.py:23
  176.4 9.3 %collective-permute-start = (f32[3,32,128]{2,1,0:T(8,128)S(1)}, f32[3,32,128]{2,1,0:T(8,128)S(1)}, u32[]{:S(2)}, u32[]{:S(2)}) collective-permute-start(f32[3,32,128]{2,1,0:T(8,128)S(1)} %pad_maximum_fusion.4), channel_id=1, source_target_pairs={{0,8},{8,16},{16,24},{24,32},{32,40},{40,48},{48,56},{56,64},{64,7... | collective-permute-start | bytes 147464 | tf_op jit(solution)/shard_map/while/body/eval_jaxpr/ppermute | solution.py:23
  204.5 9.3 %collective-permute-start = (f32[3,32,128]{2,1,0:T(8,128)S(1)}, f32[3,32,128]{2,1,0:T(8,128)S(1)}, u32[]{:S(2)}, u32[]{:S(2)}) collective-permute-start(f32[3,32,128]{2,1,0:T(8,128)S(1)} %pad_maximum_fusion.4), channel_id=1, source_target_pairs={{0,8},{8,16},{16,24},{24,32},{32,40},{40,48},{48,56},{56,64},{64,7... | collective-permute-start | bytes 147464 | tf_op jit(solution)/shard_map/while/body/eval_jaxpr/ppermute | solution.py:23
  232.6 9.3 %collective-permute-start = (f32[3,32,128]{2,1,0:T(8,128)S(1)}, f32[3,32,128]{2,1,0:T(8,128)S(1)}, u32[]{:S(2)}, u32[]{:S(2)}) collective-permute-start(f32[3,32,128]{2,1,0:T(8,128)S(1)} %pad_maximum_fusion.4), channel_id=1, source_target_pairs={{0,8},{8,16},{16,24},{24,32},{32,40},{40,48},{48,56},{56,64},{64,7... | collective-permute-start | bytes 147464 | tf_op jit(solution)/shard_map/while/body/eval_jaxpr/ppermute | solution.py:23
  279.5 9.4 %collective-permute-start = (f32[3,32,128]{2,1,0:T(8,128)S(1)}, f32[3,32,128]{2,1,0:T(8,128)S(1)}, u32[]{:S(2)}, u32[]{:S(2)}) collective-permute-start(f32[3,32,128]{2,1,0:T(8,128)S(1)} %pad_maximum_fusion.4), channel_id=1, source_target_pairs={{0,8},{8,16},{16,24},{24,32},{32,40},{40,48},{48,56},{56,64},{64,7... | collective-permute-start | bytes 147464 | tf_op jit(solution)/shard_map/while/body/eval_jaxpr/ppermute | solution.py:23
  298.3 9.3 %collective-permute-start = (f32[3,32,128]{2,1,0:T(8,128)S(1)}, f32[3,32,128]{2,1,0:T(8,128)S(1)}, u32[]{:S(2)}, u32[]{:S(2)}) collective-permute-start(f32[3,32,128]{2,1,0:T(8,128)S(1)} %pad_maximum_fusion.4), channel_id=1, source_target_pairs={{0,8},{8,16},{16,24},{24,32},{32,40},{40,48},{48,56},{56,64},{64,7... | collective-permute-start | bytes 147464 | tf_op jit(solution)/shard_map/while/body/eval_jaxpr/ppermute | solution.py:23
  326.4 9.3 %collective-permute-start = (f32[3,32,128]{2,1,0:T(8,128)S(1)}, f32[3,32,128]{2,1,0:T(8,128)S(1)}, u32[]{:S(2)}, u32[]{:S(2)}) collective-permute-start(f32[3,32,128]{2,1,0:T(8,128)S(1)} %pad_maximum_fusion.4), channel_id=1, source_target_pairs={{0,8},{8,16},{16,24},{24,32},{32,40},{40,48},{48,56},{56,64},{64,7... | collective-permute-start | bytes 147464 | tf_op jit(solution)/shard_map/while/body/eval_jaxpr/ppermute | solution.py:23
  345.2 9.8 %collective-permute-start = (f32[3,32,128]{2,1,0:T(8,128)S(1)}, f32[3,32,128]{2,1,0:T(8,128)S(1)}, u32[]{:S(2)}, u32[]{:S(2)}) collective-permute-start(f32[3,32,128]{2,1,0:T(8,128)S(1)} %pad_maximum_fusion.4), channel_id=1, source_target_pairs={{0,8},{8,16},{16,24},{24,32},{32,40},{40,48},{48,56},{56,64},{64,7... | collective-permute-start | bytes 147464 | tf_op jit(solution)/shard_map/while/body/eval_jaxpr/ppermute | solution.py:23
  355.0 9.3 %collective-permute-start = (f32[3,32,128]{2,1,0:T(8,128)S(1)}, f32[3,32,128]{2,1,0:T(8,128)S(1)}, u32[]{:S(2)}, u32[]{:S(2)}) collective-permute-start(f32[3,32,128]{2,1,0:T(8,128)S(1)} %pad_maximum_fusion.4), channel_id=1, source_target_pairs={{0,8},{8,16},{16,24},{24,32},{32,40},{40,48},{48,56},{56,64},{64,7... | collective-permute-start | bytes 147464 | tf_op jit(solution)/shard_map/while/body/eval_jaxpr/ppermute | solution.py:23
  411.3 9.4 %collective-permute-start = (f32[3,32,128]{2,1,0:T(8,128)S(1)}, f32[3,32,128]{2,1,0:T(8,128)S(1)}, u32[]{:S(2)}, u32[]{:S(2)}) collective-permute-start(f32[3,32,128]{2,1,0:T(8,128)S(1)} %pad_maximum_fusion.4), channel_id=1, source_target_pairs={{0,8},{8,16},{16,24},{24,32},{32,40},{40,48},{48,56},{56,64},{64,7... | collective-permute-start | bytes 147464 | tf_op jit(solution)/shard_map/while/body/eval_jaxpr/ppermute | solution.py:23
  420.7 9.3 %collective-permute-start = (f32[3,32,128]{2,1,0:T(8,128)S(1)}, f32[3,32,128]{2,1,0:T(8,128)S(1)}, u32[]{:S(2)}, u32[]{:S(2)}) collective-permute-start(f32[3,32,128]{2,1,0:T(8,128)S(1)} %pad_maximum_fusion.4), channel_id=1, source_target_pairs={{0,8},{8,16},{16,24},{24,32},{32,40},{40,48},{48,56},{56,64},{64,7... | collective-permute-start | bytes 147464 | tf_op jit(solution)/shard_map/while/body/eval_jaxpr/ppermute | solution.py:23
  448.8 9.3 %collective-permute-start = (f32[3,32,128]{2,1,0:T(8,128)S(1)}, f32[3,32,128]{2,1,0:T(8,128)S(1)}, u32[]{:S(2)}, u32[]{:S(2)}) collective-permute-start(f32[3,32,128]{2,1,0:T(8,128)S(1)} %pad_maximum_fusion.4), channel_id=1, source_target_pairs={{0,8},{8,16},{16,24},{24,32},{32,40},{40,48},{48,56},{56,64},{64,7... | collective-permute-start | bytes 147464 | tf_op jit(solution)/shard_map/while/body/eval_jaxpr/ppermute | solution.py:23
  486.3 9.3 %collective-permute-start = (f32[3,32,128]{2,1,0:T(8,128)S(1)}, f32[3,32,128]{2,1,0:T(8,128)S(1)}, u32[]{:S(2)}, u32[]{:S(2)}) collective-permute-start(f32[3,32,128]{2,1,0:T(8,128)S(1)} %pad_maximum_fusion.4), channel_id=1, source_target_pairs={{0,8},{8,16},{16,24},{24,32},{32,40},{40,48},{48,56},{56,64},{64,7... | collective-permute-start | bytes 147464 | tf_op jit(solution)/shard_map/while/body/eval_jaxpr/ppermute | solution.py:23
  495.7 9.3 %collective-permute-start = (f32[3,32,128]{2,1,0:T(8,128)S(1)}, f32[3,32,128]{2,1,0:T(8,128)S(1)}, u32[]{:S(2)}, u32[]{:S(2)}) collective-permute-start(f32[3,32,128]{2,1,0:T(8,128)S(1)} %pad_maximum_fusion.4), channel_id=1, source_target_pairs={{0,8},{8,16},{16,24},{24,32},{32,40},{40,48},{48,56},{56,64},{64,7... | collective-permute-start | bytes 147464 | tf_op jit(solution)/shard_map/while/body/eval_jaxpr/ppermute | solution.py:23
  523.8 9.3 %collective-permute-start = (f32[3,32,128]{2,1,0:T(8,128)S(1)}, f32[3,32,128]{2,1,0:T(8,128)S(1)}, u32[]{:S(2)}, u32[]{:S(2)}) collective-permute-start(f32[3,32,128]{2,1,0:T(8,128)S(1)} %pad_maximum_fusion.4), channel_id=1, source_target_pairs={{0,8},{8,16},{16,24},{24,32},{32,40},{40,48},{48,56},{56,64},{64,7... | collective-permute-start | bytes 147464 | tf_op jit(solution)/shard_map/while/body/eval_jaxpr/ppermute | solution.py:23
  551.9 9.3 %collective-permute-start = (f32[3,32,128]{2,1,0:T(8,128)S(1)}, f32[3,32,128]{2,1,0:T(8,128)S(1)}, u32[]{:S(2)}, u32[]{:S(2)}) collective-permute-start(f32[3,32,128]{2,1,0:T(8,128)S(1)} %pad_maximum_fusion.4), channel_id=1, source_target_pairs={{0,8},{8,16},{16,24},{24,32},{32,40},{40,48},{48,56},{56,64},{64,7... | collective-permute-start | bytes 147464 | tf_op jit(solution)/shard_map/while/body/eval_jaxpr/ppermute | solution.py:23
  (45 other events, 385.4 us)
where the time goes:
time: 612 us; the launch traced here: 610 us
  waiting for transfers between devices  470 us (77%)
  starting transfers between devices  128 us (21%)
  other arithmetic  7.23 us (1%)
    ppermute x63, waiting for transfers between devices, from_behind(): return lax.ppermute(block, axis, route)  467 us
    ppermute x63, starting transfers between devices, from_behind(): return lax.ppermute(block, axis, route)  123 us
  transfers between devices with their start and end apart: 65, of which 64 were waited for; matrix products, arithmetic and copies ran while one was open for 0% of the time, Pallas kernels for 0%

commit v1 on v0

v1 whole, which is shorter than its diff:
```python
import functools

import jax
import jax.numpy as jnp
from jax import lax
from jax.experimental import pallas as pl
from jax.experimental.pallas import tpu as pltpu
from jax.sharding import PartitionSpec as P

VMEM = pl.BlockSpec(memory_space=pltpu.VMEM)
SMEM = pl.BlockSpec(memory_space=pltpu.SMEM)
PARAMS = pltpu.CompilerParams(vmem_limit_bytes=16 * 1024 * 1024)
SLOTS = 8


def shifted(value, distance, axis, edge):
    size = value.shape[axis]
    position = lax.broadcasted_iota(jnp.int32, value.shape, axis)
    moved = pltpu.roll(value, distance % size, axis)
    return jnp.where(position == (0 if distance == 1 else size - 1), edge, moved)


def halves(low, high):
    lane = lax.broadcasted_iota(jnp.int32, low.shape, 1)
    half = low.shape[1] // 2
    first = jnp.where(lane < half, low, pltpu.roll(high, half, 1))
    second = jnp.where(lane < half, pltpu.roll(low, half, 1), high)
    return first, second


def maps_kernel(
    core_ref, conc_ref, cour_ref, rate_ref, spread_ref, chip_ref, link_ref, src_ref, inv_ref, out_ref
):
    cells = conc_ref.shape[1]
    rows = conc_ref.shape[2]
    spread = spread_ref[...]
    even = core_ref[0] == 0
    maps = None
    for i in range(cells):
        src = []
        for c in range(3):
            x = conc_ref[c, i]
            chip = chip_ref[pl.ds(c * cells + i, 1), :]
            link = link_ref[pl.ds(c * cells + i, 1), :]
            below = jnp.broadcast_to(jnp.where(even, link, chip), x.shape)
            above = jnp.broadcast_to(jnp.where(even, chip, link), x.shape)
            beside = shifted(x, -1, 0, above) + shifted(x, 1, 0, below)
            beside = beside + shifted(x, -1, 1, 0.0) + shifted(x, 1, 1, 0.0)
            value = x + spread * (beside - 4.0 * x)
            src_ref[c, i] = value
            src.append(value)
        cour = [cour_ref[c, i] for c in range(3)]
        rate = [rate_ref[c, i] for c in range(2)]
        inv = [
            1.0 / (1.0 + cour[0] + rate[0]),
            1.0 / (1.0 + cour[1] + rate[1]),
            1.0 / (1.0 + cour[2]),
        ]
        for c in range(3):
            inv_ref[c, i] = inv[c]
        gain = [cour[c] * inv[c] for c in range(3)]
        if maps is None:
            u0 = inv[0]
            u1 = inv[1] * (rate[0] * u0)
            v1 = inv[1]
            aa = gain[0]
            pa = cour[1] * u1
            pp = gain[1]
            va = gain[2] * (rate[1] * u1)
            vp = gain[2] * (rate[1] * v1)
            vv = gain[2]
            u0 = inv[0] * src[0]
            u1 = inv[1] * (src[1] + rate[0] * u0)
            off_a = cour[0] * u0
            off_p = cour[1] * u1
            off_v = gain[2] * (src[2] + rate[1] * u1)
        else:
            aa, pa, pp, va, vp, vv, off_a, off_p, off_v = maps
            u0 = inv[0] * aa
            u1 = inv[1] * (pa + rate[0] * u0)
            v1 = inv[1] * pp
            aa = cour[0] * u0
            pa = cour[1] * u1
            pp = cour[1] * v1
            va = gain[2] * (va + rate[1] * u1)
            vp = gain[2] * (vp + rate[1] * v1)
            vv = gain[2] * vv
            u0 = inv[0] * (src[0] + off_a)
            u1 = inv[1] * (src[1] + off_p + rate[0] * u0)
            off_a = cour[0] * u0
            off_p = cour[1] * u1
            off_v = gain[2] * (src[2] + off_v + rate[1] * u1)
        maps = (aa, pa, pp, va, vp, vv, off_a, off_p, off_v)
    listed = list(maps)
    listed.append(jnp.zeros_like(spread))
    for j in range(5):
        first, second = halves(listed[2 * j], listed[2 * j + 1])
        out_ref[pl.ds(j, rows, stride=2 * SLOTS), :] = first
        out_ref[pl.ds(SLOTS + j, rows, stride=2 * SLOTS), :] = second
    for j in range(5, SLOTS):
        out_ref[pl.ds(j, rows, stride=2 * SLOTS), :] = listed[-1]
        out_ref[pl.ds(SLOTS + j, rows, stride=2 * SLOTS), :] = listed[-1]


def relay_kernel(place_ref, maps_ref, inlet_ref, out_ref, map_scr, flux_scr):
    count = out_ref.shape[0] // 2
    lanes = out_ref.shape[1]
    half = lanes // 2
    for j in range(5):
        pair = maps_ref[pl.ds(j, count, stride=SLOTS), :]
        map_scr[2 * j] = pair
        if 2 * j + 1 < 9:
            map_scr[2 * j + 1] = pltpu.roll(pair, half, 1)
    place = place_ref[0]
    row = place // 2
    odd = place - 2 * row
    flux = []
    for c in range(3):
        line = inlet_ref[c, pl.ds(row, 1), :]
        flux.append(jnp.where(odd == 1, pltpu.roll(line, half, 1), line))
    for f in range(count):
        for c in range(3):
            flux_scr[c, pl.ds(f, 1), :] = flux[c]
        m = [map_scr[j, pl.ds(f, 1), :] for j in range(9)]
        flux = [
            m[0] * flux[0] + m[6],
            (m[1] * flux[0] + m[7]) + m[2] * flux[1],
            (m[3] * flux[0] + m[8]) + (m[4] * flux[1] + m[5] * flux[2]),
        ]
    lane = lax.broadcasted_iota(jnp.int32, (count, lanes), 1)
    first = jnp.where(lane < half, flux_scr[0], pltpu.roll(flux_scr[1], half, 1))
    out_ref[pl.ds(0, count, stride=2), :] = first
    out_ref[pl.ds(1, count, stride=2), :] = flux_scr[2]


def fresh_kernel(flux_ref, src_ref, inv_ref, cour_ref, rate_ref, out_ref):
    cells, rows, lanes = src_ref.shape[1:]
    half = lanes // 2
    lane = lax.broadcasted_iota(jnp.int32, (rows, lanes), 1)

    def half_row(h, j):
        return flux_ref[pl.ds(2 * h + j, rows, stride=4), :]

    pair_l, pair_h = half_row(0, 0), half_row(1, 0)
    third_l, third_h = half_row(0, 1), half_row(1, 1)
    flux = [
        jnp.where(lane < half, pair_l, pltpu.roll(pair_h, half, 1)),
        jnp.where(lane < half, pltpu.roll(pair_l, half, 1), pair_h),
        jnp.where(lane < half, third_l, pltpu.roll(third_h, half, 1)),
    ]
    for i in range(cells):
        first = inv_ref[0, i] * (src_ref[0, i] + flux[0])
        second = inv_ref[1, i] * (src_ref[1, i] + flux[1] + rate_ref[0, i] * first)
        third = inv_ref[2, i] * (src_ref[2, i] + flux[2] + rate_ref[1, i] * second)
        values = (first, second, third)
        for c in range(3):
            out_ref[c, i] = values[c]
        flux = [cour_ref[c, i] * values[c] for c in range(3)]


def halo(concentration):
    _, cells, rows, lanes = concentration.shape
    count = lax.axis_size("lat")
    core = lax.axis_index("lat") % 2
    low = concentration[:, :, 0, :].reshape(3 * cells, lanes)
    high = concentration[:, :, rows - 1, :].reshape(3 * cells, lanes)
    to_chip = jnp.where(core == 0, high, low)
    to_link = jnp.where(core == 0, low, high)
    links = [(i, i + 1) for i in range(1, count - 1, 2)]
    links = links + [(b, a) for a, b in links]
    link = lax.ppermute(to_link, "lat", links)
    chip = lax.ppermute(to_chip, "lat", [(i, i ^ 1) for i in range(count)])
    return core, chip, link


def per_device(concentration, courant, rates, spread, inlet):
    _, cells, rows, lanes = concentration.shape
    count = lax.axis_size("flow")
    f32 = jnp.float32
    core, chip, link = halo(concentration)
    block = jax.ShapeDtypeStruct(concentration.shape, f32)
    src, inv, maps = pl.pallas_call(
        maps_kernel,
        out_shape=(block, block, jax.ShapeDtypeStruct((count * SLOTS, lanes), f32)),
        in_specs=[SMEM] + [VMEM] * 6,
        out_specs=(VMEM,) * 3,
        compiler_params=PARAMS,
        name="maps",
    )(core.reshape(1), concentration, courant, rates, spread, chip, link)
    maps = lax.all_to_all(maps.reshape(count, SLOTS, lanes), "flow", 0, 0)
    place = lax.axis_index("flow").reshape(1)
    flux = pl.pallas_call(
        relay_kernel,
        out_shape=jax.ShapeDtypeStruct((count * 2, lanes), f32),
        in_specs=[SMEM] + [VMEM] * 2,
        out_specs=VMEM,
        scratch_shapes=[pltpu.VMEM((10, count, lanes), f32), pltpu.VMEM((3, count, lanes), f32)],
        compiler_params=PARAMS,
        name="relay",
    )(place, maps.reshape(count * SLOTS, lanes), inlet)
    flux = lax.all_to_all(flux.reshape(count, 2, lanes), "flow", 0, 0)
    return pl.pallas_call(
        fresh_kernel,
        out_shape=block,
        in_specs=[VMEM] * 5,
        out_specs=VMEM,
        compiler_params=PARAMS,
        name="fresh",
    )(flux.reshape(count * 2, lanes), src, inv, courant, rates)


def solution(mesh):
    in_specs = (
        P(None, "flow", "lat", None),
        P(None, "flow", "lat", None),
        P(None, "flow", "lat", None),
        P("lat", None),
        P(None, "lat", None),
    )
    out_specs = P(None, "flow", "lat", None)
    return jax.shard_map(
        per_device, mesh=mesh, in_specs=in_specs, out_specs=out_specs, check_vma=False
    )
```

time: 612 us -> 63.3 us (0.10)
  the two profiles are of different devices: /device:TPU:36 before, /device:TPU:2 now
where the time goes in v1:
time: 63.3 us; the launch traced here: 63 us
  starting transfers between devices  22.3 us (35%)
  waiting for transfers between devices  16.9 us (27%)
  blocking collectives  16.4 us (26%)
  local copies, waits for them, and re-layouts  3.32 us (5%)
  Pallas kernels  2.99 us (5%)
  other arithmetic  1.07 us (2%)
    all_to_all x1, blocking collectives, per_device(): flux = lax.all_to_all(flux.reshape(count, 2, lanes), 'flow', 0, 0)  16.4 us
    all_to_all x1, waiting for transfers between devices, per_device(): maps = lax.all_to_all(maps.reshape(count, SLOTS, lanes), 'flow', 0, 0)  15.4 us
    all_to_all x1, starting transfers between devices, per_device(): maps = lax.all_to_all(maps.reshape(count, SLOTS, lanes), 'flow', 0, 0)  12.5 us
    ppermute x1, starting transfers between devices, halo(): link = lax.ppermute(to_link, 'lat', links)  7.89 us
    unnamed x14, local copies, waits for them, and re-layouts  3.32 us
    ppermute x1, starting transfers between devices, halo(): chip = lax.ppermute(to_chip, 'lat', [(i, i ^ 1) for i in range(count)])  1.92 us
    pallas_call x1, Pallas kernels, per_device(): pl.pallas_call(maps_kernel, out_shape=(block, block, jax.ShapeDtypeStruct...  1.61 us
    ppermute x1, waiting for transfers between devices, halo(): link = lax.ppermute(to_link, 'lat', links)  1.49 us
  transfers between devices with their start and end apart: 3, of which 2 were waited for; matrix products, arithmetic and copies ran while one was open for 0% of the time, Pallas kernels for 0%

profile of v1, /device:TPU:2, one launch (start us, length us, event | category | flops | bytes accessed | tf_op | source)
XLA Modules:
  0.0 63.0 jit_solution(16789735780778333283)
XLA Ops:
  0.0 0.0 copy-start.6
  0.0 1.1 %broadcast_select_fusion = (f32[3,16,1,128]{3,2,1,0:T(1,128)S(1)}, f32[3,16,1,128]{3,2,1,0:T(1,128)S(1)}) fusion(pred[]{:T(512)S(6)} %eq.6, f32[3,16,32,128]{3,2,1,0:T(8,128)} %conc_ref.1), kind=kLoop, calls=%fused_computation | loop fusion | flops 12288 | bytes 98305 | tf_op jit(solution)/shard_map/jit(_where)/select_n | solution.py:168
  1.1 1.9 %collective-permute-start = (f32[48,128]{1,0:T(8,128)S(1)}, f32[48,128]{1,0:T(8,128)S(1)}, u32[]{:S(2)}, u32[]{:S(2)}) collective-permute-start(f32[48,128]{1,0:T(8,128)S(1)} %bitcast.12), channel_id=1, source_target_pairs={{0,1},{1,0},{2,3},{3,2},{4,5},{5,4},{6,7},{7,6},{8,9},{9,8},{10,11... | collective-permute-start | bytes 73736 | tf_op jit(solution)/shard_map/ppermute | solution.py:172
  3.0 7.9 %collective-permute-start.1 = (f32[48,128]{1,0:T(8,128)S(1)}, f32[48,128]{1,0:T(8,128)S(1)}, u32[]{:S(2)}, u32[]{:S(2)}) collective-permute-start(f32[48,128]{1,0:T(8,128)S(1)} %bitcast.11), channel_id=1, source_target_pairs={{1,2},{3,4},{5,6},{2,1},{4,3},{6,5},{9,10},{11,12},{13,14},{10,9},... | collective-permute-start | bytes 73736 | tf_op jit(solution)/shard_map/ppermute | solution.py:171
  10.9 0.0 collective-permute-done.chip_ref
  10.9 1.5 %collective-permute-done.1.link_ref = f32[48,128]{1,0:T(8,128)S(1)} collective-permute-done((f32[48,128]{1,0:T(8,128)S(1)}, f32[48,128]{1,0:T(8,128)S(1)}, u32[]{:S(2)}, u32[]{:S(2)}) %collective-permute-start.1) | collective-permute-done | bytes 24608 | tf_op jit(solution)/shard_map/ppermute | solution.py:171
  12.4 0.0 copy-done.6
  12.4 0.0 copy-start
  12.4 1.1 %copy-done = f32[3,16,32,128]{3,2,1,0:T(8,128)S(1)} copy-done((f32[3,16,32,128]{3,2,1,0:T(8,128)S(1)}, f32[3,16,32,128]{3,2,1,0:T(8,128)}, u32[]{:S(2)}) %copy-start) | copy-done | bytes 786456
  13.5 0.0 copy-start.2
  13.5 1.0 %copy-done.2 = f32[2,16,32,128]{3,2,1,0:T(8,128)S(1)} copy-done((f32[2,16,32,128]{3,2,1,0:T(8,128)S(1)}, f32[2,16,32,128]{3,2,1,0:T(8,128)}, u32[]{:S(2)}) %copy-start.2) | copy-done | bytes 524312
  14.6 0.0 copy-start.4
  14.6 1.1 %copy-done.4 = f32[3,16,32,128]{3,2,1,0:T(8,128)S(1)} copy-done((f32[3,16,32,128]{3,2,1,0:T(8,128)S(1)}, f32[3,16,32,128]{3,2,1,0:T(8,128)}, u32[]{:S(2)}) %copy-start.4) | copy-done | bytes 786456
  15.7 0.0 copy-start.5
  15.7 0.0 copy-start.3
  15.7 1.6 %maps.1 = (f32[3,16,32,128]{3,2,1,0:T(8,128)S(1)}, f32[3,16,32,128]{3,2,1,0:T(8,128)S(1)}, f32[512,128]{1,0:T(8,128)}) custom-call(s32[1]{0:T(128)} %bitcast.1.core_ref, f32[3,16,32,128]{3,2,1,0:T(8,128)S(1)} %copy-done.4, f32[3,16,32,128]{3,2,1,0:T(8,128)S(1)} %copy-done, f32[2,16,32,128]{3,2,1,0:T(8,128)S(1)} %copy-done.2, f32[32,128]{1,0:T(8,128)S(1)} %copy-done.6, ...), custom_call_target="tpu_custom_call" | custom-call | tf_op jit(solution)/shard_map/maps/pallas_call | solution.py:182
  17.3 12.5 %all-to-all-start = ((f32[64,8,128]{2,1,0:T(8,128)}), f32[64,8,128]{2,1,0:T(8,128)S(1)}, u32[]{:S(2)}, u32[]{:S(2)}) async-start(f32[64,8,128]{2,1,0:T(8,128)} %bitcast.4), calls=%async_computation | async-start | bytes 524288 | tf_op jit(solution)/shard_map/all_to_all | solution.py:190
  29.8 15.4 %all-to-all-done = f32[64,8,128]{2,1,0:T(8,128)S(1)} async-done(((f32[64,8,128]{2,1,0:T(8,128)}), f32[64,8,128]{2,1,0:T(8,128)S(1)}, u32[]{:S(2)}, u32[]{:S(2)}) %all-to-all-start) | async-done | bytes 262176 | tf_op jit(solution)/shard_map/all_to_all | solution.py:190
  45.2 0.0 copy-done.5
  45.2 0.3 relay.1
  45.5 16.4 %all_to_all.10 = f32[64,2,128]{2,1,0:T(2,128)S(1)} all-to-all(f32[64,2,128]{2,1,0:T(2,128)S(1)} %bitcast.10), channel_id=1, replica_groups=mesh['flow'=64,'lat'=8] {'flow'}, dimensions={0} | all-to-all | bytes 131072 | tf_op jit(solution)/shard_map/all_to_all | solution.py:201
  61.9 0.0 copy-done.3
  61.9 0.0 copy-done.1
  61.9 1.1 %fresh.1 = f32[3,16,32,128]{3,2,1,0:T(8,128)} custom-call(f32[128,128]{1,0:T(8,128)S(1)} %bitcast.9, f32[3,16,32,128]{3,2,1,0:T(8,128)S(1)} %get-tuple-element.9.src_ref, f32[3,16,32,128]{3,2,1,0:T(8,128)S(1)} %get-tuple-element.10.inv_ref, f32[3,16,32,128]{3,2,1,0:T(8,128)S(1)} %copy-done.1, f32[2,16,32,128]{3,2,1,0:T(8,128)S(1)} %copy-done.3), custom_call_target="tpu_custom_call" | custom-call | tf_op jit(solution)/shard_map/fresh/pallas_call | solution.py:202
  (1 shorter events, 0.0 us)
Async XLA Ops:
  0.0 12.4 %copy-start.6 = (f32[32,128]{1,0:T(8,128)S(1)}, f32[32,128]{1,0:T(8,128)}, u32[]{:S(2)}) copy-start(f32[32,128]{1,0:T(8,128)} %spread_ref.1) | copy-start | bytes 49156
  1.1 9.8 %collective-permute-start = (f32[48,128]{1,0:T(8,128)S(1)}, f32[48,128]{1,0:T(8,128)S(1)}, u32[]{:S(2)}, u32[]{:S(2)}) collective-permute-start(f32[48,128]{1,0:T(8,128)S(1)} %bitcast.12), channel_id=1, source_target_pairs={{0,1},{1,0},{2,3},{3,2},{4,5},{5,4},{6,7},{7,6},{8,9},{9,8},{10,11... | collective-permute-start | bytes 73736 | tf_op jit(solution)/shard_map/ppermute | solution.py:172
  3.0 9.4 %collective-permute-start.1 = (f32[48,128]{1,0:T(8,128)S(1)}, f32[48,128]{1,0:T(8,128)S(1)}, u32[]{:S(2)}, u32[]{:S(2)}) collective-permute-start(f32[48,128]{1,0:T(8,128)S(1)} %bitcast.11), channel_id=1, source_target_pairs={{1,2},{3,4},{5,6},{2,1},{4,3},{6,5},{9,10},{11,12},{13,14},{10,9},... | collective-permute-start | bytes 73736 | tf_op jit(solution)/shard_map/ppermute | solution.py:171
  12.4 1.1 %copy-start = (f32[3,16,32,128]{3,2,1,0:T(8,128)S(1)}, f32[3,16,32,128]{3,2,1,0:T(8,128)}, u32[]{:S(2)}) copy-start(f32[3,16,32,128]{3,2,1,0:T(8,128)} %cour_ref.3) | copy-start | bytes 2359300
  13.5 1.0 %copy-start.2 = (f32[2,16,32,128]{3,2,1,0:T(8,128)S(1)}, f32[2,16,32,128]{3,2,1,0:T(8,128)}, u32[]{:S(2)}) copy-start(f32[2,16,32,128]{3,2,1,0:T(8,128)} %rate_ref.3) | copy-start | bytes 1572868
  14.6 1.1 %copy-start.4 = (f32[3,16,32,128]{3,2,1,0:T(8,128)S(1)}, f32[3,16,32,128]{3,2,1,0:T(8,128)}, u32[]{:S(2)}) copy-start(f32[3,16,32,128]{3,2,1,0:T(8,128)} %conc_ref.1) | copy-start | bytes 2359300
  15.7 29.5 %copy-start.5 = (f32[3,32,128]{2,1,0:T(8,128)S(1)}, f32[3,32,128]{2,1,0:T(8,128)}, u32[]{:S(2)}) copy-start(f32[3,32,128]{2,1,0:T(8,128)} %inlet_ref.1) | copy-start | bytes 147460
  15.7 46.2 %copy-start.3 = (f32[2,16,32,128]{3,2,1,0:T(8,128)S(1)}, f32[2,16,32,128]{3,2,1,0:T(8,128)}, u32[]{:S(2)}) copy-start(f32[2,16,32,128]{3,2,1,0:T(8,128)} %rate_ref.3) | copy-start | bytes 1572868
  17.3 44.5 %copy-start.1 = (f32[3,16,32,128]{3,2,1,0:T(8,128)S(1)}, f32[3,16,32,128]{3,2,1,0:T(8,128)}, u32[]{:S(2)}) copy-start(f32[3,16,32,128]{3,2,1,0:T(8,128)} %cour_ref.3) | copy-start | bytes 2359300
  17.3 27.9 %all-to-all-start = ((f32[64,8,128]{2,1,0:T(8,128)}), f32[64,8,128]{2,1,0:T(8,128)S(1)}, u32[]{:S(2)}, u32[]{:S(2)}) async-start(f32[64,8,128]{2,1,0:T(8,128)} %bitcast.4), calls=%async_computation | async-start | bytes 524288 | tf_op jit(solution)/shard_map/all_to_all | solution.py:190

commit v2 on v1

--- a/solution.py
+++ b/solution.py
@@ -13,6 +13,10 @@
 SLOTS = 8
 
 
+def in_hbm(value):
+    return pltpu.with_memory_space_constraint(value, pltpu.HBM)
+
+
 def shifted(value, distance, axis, edge):
     size = value.shape[axis]
     position = lax.broadcasted_iota(jnp.int32, value.shape, axis)
@@ -28,27 +32,48 @@
     return first, second
 
 
+def load_kernel(core_ref, conc_ref, held_ref, link_ref, chip_ref, sems):
+    rows = conc_ref.shape[2]
+    copies = [pltpu.make_async_copy(conc_ref.at[c], held_ref.at[c], sems.at[c]) for c in range(3)]
+    for copy in copies:
+        copy.start()
+    even = core_ref[0] == 0
+    for c in range(3):
+        copies[c].wait()
+        low = held_ref[c, :, 0, :]
+        high = held_ref[c, :, rows - 1, :]
+        link_ref[c] = jnp.where(even, low, high)
+        chip_ref[c] = jnp.where(even, high, low)
+
+
 def maps_kernel(
-    core_ref, conc_ref, cour_ref, rate_ref, spread_ref, chip_ref, link_ref, src_ref, inv_ref, out_ref
+    conc_ref, cour_hbm, rate_hbm, spread_ref, src_ref, inv_ref, maps_ref, cour_ref, rate_ref, sems
 ):
     cells = conc_ref.shape[1]
-    rows = conc_ref.shape[2]
+    part = cells // 2
+    loads = []
+    for h in range(2):
+        span = pl.ds(h * part, part)
+        pair = [
+            pltpu.make_async_copy(cour_hbm.at[:, span], cour_ref.at[:, span], sems.at[0, h]),
+            pltpu.make_async_copy(rate_hbm.at[:, span], rate_ref.at[:, span], sems.at[1, h]),
+        ]
+        for copy in pair:
+            copy.start()
+        loads.append(pair)
     spread = spread_ref[...]
-    even = core_ref[0] == 0
+    for i in range(cells):
+        for c in range(3):
+            x = conc_ref[c, i]
+            beside = shifted(x, -1, 0, 0.0) + shifted(x, 1, 0, 0.0)
+            beside = beside + shifted(x, -1, 1, 0.0) + shifted(x, 1, 1, 0.0)
+            src_ref[c, i] = x + spread * (beside - 4.0 * x)
     maps = None
     for i in range(cells):
-        src = []
-        for c in range(3):
-            x = conc_ref[c, i]
-            chip = chip_ref[pl.ds(c * cells + i, 1), :]
-            link = link_ref[pl.ds(c * cells + i, 1), :]
-            below = jnp.broadcast_to(jnp.where(even, link, chip), x.shape)
-            above = jnp.broadcast_to(jnp.where(even, chip, link), x.shape)
-            beside = shifted(x, -1, 0, above) + shifted(x, 1, 0, below)
-            beside = beside + shifted(x, -1, 1, 0.0) + shifted(x, 1, 1, 0.0)
-            value = x + spread * (beside - 4.0 * x)
-            src_ref[c, i] = value
-            src.append(value)
+        if i % part == 0:
+            for copy in loads[i // part]:
+                copy.wait()
+        src = [src_ref[c, i] for c in range(3)]
         cour = [cour_ref[c, i] for c in range(3)]
         rate = [rate_ref[c, i] for c in range(2)]
         inv = [
@@ -91,15 +116,56 @@
             off_p = cour[1] * u1
             off_v = gain[2] * (src[2] + off_v + rate[1] * u1)
         maps = (aa, pa, pp, va, vp, vv, off_a, off_p, off_v)
-    listed = list(maps)
-    listed.append(jnp.zeros_like(spread))
-    for j in range(5):
-        first, second = halves(listed[2 * j], listed[2 * j + 1])
+    for j in range(9):
+        maps_ref[j] = maps[j]
+
+
+def seam_kernel(
+    core_ref, chip_ref, link_ref, spread_ref, cour_ref, rate_ref, inv_ref, maps_ref, src_in_ref, src_ref, out_ref
+):
+    cells, rows = src_ref.shape[1:3]
+    even = core_ref[0] == 0
+
+    def edge(ref, *index):
+        return jnp.concatenate([ref[(*index, pl.ds(0, 8))], ref[(*index, pl.ds(rows - 8, 8))]], axis=0)
+
+    spread = edge(spread_ref)
+    line = lax.broadcasted_iota(jnp.int32, spread.shape, 0)
+    lower = jnp.where(line == 0, spread, 0.0)
+    upper = jnp.where(line == 15, spread, 0.0)
+    for_chip = jnp.where(even, upper, lower)
+    for_link = jnp.where(even, lower, upper)
+    flux = None
+    for i in range(cells):
+        inv = [edge(inv_ref, c, i) for c in range(3)]
+        cour = [edge(cour_ref, c, i) for c in range(3)]
+        rate = [edge(rate_ref, c, i) for c in range(2)]
+        add = []
+        for c in range(3):
+            chip = chip_ref[pl.ds(c * cells + i, 1), :]
+            link = link_ref[pl.ds(c * cells + i, 1), :]
+            value = for_chip * chip + for_link * link
+            add.append(value)
+            src_ref[c, i, pl.ds(0, 8)] = src_in_ref[c, i, pl.ds(0, 8)] + value[:8]
+            src_ref[c, i, pl.ds(rows - 8, 8)] = src_in_ref[c, i, pl.ds(rows - 8, 8)] + value[8:]
+        if flux is not None:
+            add = [add[c] + flux[c] for c in range(3)]
+        u0 = inv[0] * add[0]
+        u1 = inv[1] * (add[1] + rate[0] * u0)
+        u2 = inv[2] * (add[2] + rate[1] * u1)
+        flux = [cour[0] * u0, cour[1] * u1, cour[2] * u2]
+    listed = [maps_ref[j] for j in range(9)]
+    for c in range(3):
+        own = listed[6 + c]
+        listed[6 + c] = jnp.concatenate(
+            [own[:8] + flux[c][:8], own[8:rows - 8], own[rows - 8:] + flux[c][8:]], axis=0
+        )
+    zeros = jnp.zeros_like(listed[0])
+    listed.append(zeros)
+    for j in range(SLOTS):
+        first, second = halves(listed[2 * j], listed[2 * j + 1]) if j < 5 else (zeros, zeros)
         out_ref[pl.ds(j, rows, stride=2 * SLOTS), :] = first
         out_ref[pl.ds(SLOTS + j, rows, stride=2 * SLOTS), :] = second
-    for j in range(5, SLOTS):
-        out_ref[pl.ds(j, rows, stride=2 * SLOTS), :] = listed[-1]
-        out_ref[pl.ds(SLOTS + j, rows, stride=2 * SLOTS), :] = listed[-1]
 
 
 def relay_kernel(place_ref, maps_ref, inlet_ref, out_ref, map_scr, flux_scr):
@@ -158,37 +224,55 @@
         flux = [cour_ref[c, i] * values[c] for c in range(3)]
 
 
-def halo(concentration):
-    _, cells, rows, lanes = concentration.shape
-    count = lax.axis_size("lat")
-    core = lax.axis_index("lat") % 2
-    low = concentration[:, :, 0, :].reshape(3 * cells, lanes)
-    high = concentration[:, :, rows - 1, :].reshape(3 * cells, lanes)
-    to_chip = jnp.where(core == 0, high, low)
-    to_link = jnp.where(core == 0, low, high)
-    links = [(i, i + 1) for i in range(1, count - 1, 2)]
-    links = links + [(b, a) for a, b in links]
-    link = lax.ppermute(to_link, "lat", links)
-    chip = lax.ppermute(to_chip, "lat", [(i, i ^ 1) for i in range(count)])
-    return core, chip, link
-
-
 def per_device(concentration, courant, rates, spread, inlet):
     _, cells, rows, lanes = concentration.shape
     count = lax.axis_size("flow")
+    across = lax.axis_size("lat")
     f32 = jnp.float32
-    core, chip, link = halo(concentration)
+    core = (lax.axis_index("lat") % 2).reshape(1)
+    place = lax.axis_index("flow").reshape(1)
     block = jax.ShapeDtypeStruct(concentration.shape, f32)
-    src, inv, maps = pl.pallas_call(
+    lines = jax.ShapeDtypeStruct((3, cells, lanes), f32)
+    hbm = pl.BlockSpec(memory_space=pltpu.HBM)
+    conc, to_link, to_chip = pl.pallas_call(
+        load_kernel,
+        out_shape=(block, lines, lines),
+        in_specs=[SMEM, hbm],
+        out_specs=(VMEM,) * 3,
+        scratch_shapes=[pltpu.SemaphoreType.DMA((3,))],
+        compiler_params=PARAMS,
+        name="load",
+    )(core, in_hbm(concentration))
+    links = [(i, i + 1) for i in range(1, across - 1, 2)]
+    links = links + [(b, a) for a, b in links]
+    link = lax.ppermute(to_link.reshape(3 * cells, lanes), "lat", links)
+    chip = lax.ppermute(to_chip.reshape(3 * cells, lanes), "lat", [(i, i ^ 1) for i in range(across)])
+    src, inv, maps, cour, rate = pl.pallas_call(
         maps_kernel,
-        out_shape=(block, block, jax.ShapeDtypeStruct((count * SLOTS, lanes), f32)),
-        in_specs=[SMEM] + [VMEM] * 6,
-        out_specs=(VMEM,) * 3,
-        compiler_params=PARAMS,
+        out_shape=(
+            block,
+            block,
+            jax.ShapeDtypeStruct((9, rows, lanes), f32),
+            block,
+            jax.ShapeDtypeStruct(rates.shape, f32),
+        ),
+        in_specs=[VMEM, hbm, hbm, VMEM],
+        out_specs=(VMEM,) * 5,
+        scratch_shapes=[pltpu.SemaphoreType.DMA((2, 2))],
+        compiler_params=PARAMS,
+        cost_estimate=pl.CostEstimate(flops=0, bytes_accessed=8 * 1024 * 1024, transcendentals=0),
         name="maps",
-    )(core.reshape(1), concentration, courant, rates, spread, chip, link)
-    maps = lax.all_to_all(maps.reshape(count, SLOTS, lanes), "flow", 0, 0)
-    place = lax.axis_index("flow").reshape(1)
+    )(conc, in_hbm(courant), in_hbm(rates), spread)
+    src, packed = pl.pallas_call(
+        seam_kernel,
+        out_shape=(block, jax.ShapeDtypeStruct((count * SLOTS, lanes), f32)),
+        in_specs=[SMEM] + [VMEM] * 8,
+        out_specs=(VMEM, VMEM),
+        input_output_aliases={8: 0},
+        compiler_params=PARAMS,
+        name="seam",
+    )(core, chip, link, spread, cour, rate, inv, maps, src)
+    packed = lax.all_to_all(packed.reshape(count, SLOTS, lanes), "flow", 0, 0)
     flux = pl.pallas_call(
         relay_kernel,
         out_shape=jax.ShapeDtypeStruct((count * 2, lanes), f32),
@@ -197,7 +281,7 @@
         scratch_shapes=[pltpu.VMEM((10, count, lanes), f32), pltpu.VMEM((3, count, lanes), f32)],
         compiler_params=PARAMS,
         name="relay",
-    )(place, maps.reshape(count * SLOTS, lanes), inlet)
+    )(place, packed.reshape(count * SLOTS, lanes), inlet)
     flux = lax.all_to_all(flux.reshape(count, 2, lanes), "flow", 0, 0)
     return pl.pallas_call(
         fresh_kernel,
@@ -206,7 +290,7 @@
         out_specs=VMEM,
         compiler_params=PARAMS,
         name="fresh",
-    )(flux.reshape(count * 2, lanes), src, inv, courant, rates)
+    )(flux.reshape(count * 2, lanes), src, inv, cour, rate)
 
 
 def solution(mesh):

time: 63.3 us -> 59.1 us (0.934)
  local copies, waits for them, and re-layouts: 3.32 us -> 0.01 us
  Pallas kernels: 2.99 us -> 5.34 us
  waiting for transfers between devices: 16.9 us -> 15.1 us
  other arithmetic: 1.07 us -> 0 us
    ppermute x2, starting transfers between devices: 9.81 us -> 5.42 us  [the longest x1 3.5 us: per_device(): lax.ppermute(to_chip.reshape(3 * cells, lanes), 'lat', [(i, i ^ 1) for i...]
    all_to_all x1, starting transfers between devices: 12.5 us -> 16.7 us  [per_device(): packed = lax.all_to_all(packed.reshape(count, SLOTS, lanes), 'flow', 0, 0)]
    unnamed x14 -> x4, local copies, waits for them, and re-layouts: 3.32 us -> 0.01 us
    pallas_call x0 -> x2, Pallas kernels: none -> 2.31 us  [the longest x1 1.16 us: per_device(): pl.pallas_call(load_kernel, out_shape=(block, lines, lines), in_specs=[SM...]
    ppermute x2, waiting for transfers between devices: 1.49 us -> 0.01 us  [the longest x1 0.01 us: per_device(): link = lax.ppermute(to_link.reshape(3 * cells, lanes), 'lat', links)]
    select_n x1 -> x0, other arithmetic: 1.07 us -> none  [halo(): to_link = jnp.where(core == 0, low, high)]
  transfers between devices with their start and end apart: 3 -> 3, of which waited for: 2 -> 1; matrix products, arithmetic and copies ran while one was open for 0% -> 0% of each run, Pallas kernels for 0% -> 3%
where the time goes in v2:
time: 59.1 us; the launch traced here: 58.8 us
  starting transfers between devices  22.1 us (37%)
  blocking collectives  16.1 us (27%)
  waiting for transfers between devices  15.1 us (26%)
  Pallas kernels  5.34 us (9%)
    all_to_all x1, starting transfers between devices, per_device(): packed = lax.all_to_all(packed.reshape(count, SLOTS, lanes), 'flow', 0, 0)  16.7 us
    all_to_all x1, blocking collectives, per_device(): flux = lax.all_to_all(flux.reshape(count, 2, lanes), 'flow', 0, 0)  16.1 us
    all_to_all x1, waiting for transfers between devices, per_device(): packed = lax.all_to_all(packed.reshape(count, SLOTS, lanes), 'flow', 0, 0)  15.1 us
    ppermute x1, starting transfers between devices, per_device(): lax.ppermute(to_chip.reshape(3 * cells, lanes), 'lat', [(i, i ^ 1) for i...  3.5 us
    ppermute x1, starting transfers between devices, per_device(): link = lax.ppermute(to_link.reshape(3 * cells, lanes), 'lat', links)  1.92 us
    pallas_call x1, Pallas kernels, per_device(): pl.pallas_call(maps_kernel, out_shape=(block, block, jax.ShapeDtypeStruct...  1.65 us
  transfers between devices with their start and end apart: 3, of which 1 were waited for; matrix products, arithmetic and copies ran while one was open for 0% of the time, Pallas kernels for 3%

profile of v2, /device:TPU:2, one launch (start us, length us, event | category | flops | bytes accessed | tf_op | source)
XLA Modules:
  0.0 58.8 jit_solution(13036828851881094770)
XLA Ops:
  0.0 0.0 copy-start
  0.0 1.2 %load.1 = (f32[3,16,32,128]{3,2,1,0:T(8,128)S(1)}, f32[3,16,128]{2,1,0:T(8,128)S(1)}, f32[3,16,128]{2,1,0:T(8,128)S(1)}) custom-call(s32[1]{0:T(128)} %bitcast.1.core_ref, f32[3,16,32,128]{3,2,1,0:T(8,128)} %conc_ref.1), custom_call_target="tpu_custom_call" | custom-call | tf_op jit(solution)/shard_map/load/pallas_call | solution.py:237
  1.2 1.9 %collective-permute-start.1 = (f32[48,128]{1,0:T(8,128)S(1)}, f32[48,128]{1,0:T(8,128)S(1)}, u32[]{:S(2)}, u32[]{:S(2)}) collective-permute-start(f32[48,128]{1,0:T(8,128)S(1)} %bitcast.12), channel_id=1, source_target_pairs={{1,2},{3,4},{5,6},{2,1},{4,3},{6,5},{9,10},{11,12},{13,14},{10,9},... | collective-permute-start | bytes 73736 | tf_op jit(solution)/shard_map/ppermute | solution.py:248
  3.1 3.5 %collective-permute-start = (f32[48,128]{1,0:T(8,128)S(1)}, f32[48,128]{1,0:T(8,128)S(1)}, u32[]{:S(2)}, u32[]{:S(2)}) collective-permute-start(f32[48,128]{1,0:T(8,128)S(1)} %bitcast.11), channel_id=1, source_target_pairs={{0,1},{1,0},{2,3},{3,2},{4,5},{5,4},{6,7},{7,6},{8,9},{9,8},{10,11... | collective-permute-start | bytes 73736 | tf_op jit(solution)/shard_map/ppermute | solution.py:249
  6.6 0.0 copy-done
  6.6 1.7 %maps.1 = (f32[3,16,32,128]{3,2,1,0:T(8,128)S(1)}, f32[3,16,32,128]{3,2,1,0:T(8,128)S(1)}, f32[9,32,128]{2,1,0:T(8,128)S(1)}, f32[3,16,32,128]{3,2,1,0:T(8,128)S(1)}, f32[2,16,32,128]{3,2,1,0:T(8,128)S(1)}) custom-call(f32[3,16,32,128]{3,2,1,0:T(8,128)S(1)} %get-tuple-element.17.conc_ref, f32[3,16,32,128]{3,2,1,0:T(8,128)} %cour_hbm.1, ...), custom_call_target="tpu_custom_call" | custom-call | bytes 8388608 | tf_op jit(solution)/shard_map/maps/pallas_call | solution.py:250
  8.3 0.0 collective-permute-done.1.link_ref
  8.3 0.0 collective-permute-done.chip_ref
  8.3 1.2 %seam.1 = (f32[3,16,32,128]{3,2,1,0:T(8,128)S(1)}, f32[512,128]{1,0:T(8,128)}) custom-call(s32[1]{0:T(128)} %bitcast.1.core_ref, f32[48,128]{1,0:T(8,128)S(1)} %collective-permute-done.chip_ref, f32[48,128]{1,0:T(8,128)S(1)} %collective-permute-done.1.link_ref, f32[32,128]{1,0:T(8,128)S(1)} %copy-done, ...), custom_call_target="tpu_custom_call", output_to_operand_aliasing={{0}: (8, {})} | custom-call | tf_op jit(solution)/shard_map/seam/pallas_call | solution.py:266
  9.4 0.0 copy-start.1
  9.4 16.7 %all-to-all-start = ((f32[64,8,128]{2,1,0:T(8,128)}), f32[64,8,128]{2,1,0:T(8,128)S(1)}, u32[]{:S(2)}, u32[]{:S(2)}) async-start(f32[64,8,128]{2,1,0:T(8,128)} %bitcast.4), calls=%async_computation | async-start | bytes 524288 | tf_op jit(solution)/shard_map/all_to_all | solution.py:275
  26.2 15.1 %all-to-all-done = f32[64,8,128]{2,1,0:T(8,128)S(1)} async-done(((f32[64,8,128]{2,1,0:T(8,128)}), f32[64,8,128]{2,1,0:T(8,128)S(1)}, u32[]{:S(2)}, u32[]{:S(2)}) %all-to-all-start) | async-done | bytes 262176 | tf_op jit(solution)/shard_map/all_to_all | solution.py:275
  41.3 0.0 copy-done.1
  41.3 0.3 relay.1
  41.6 16.1 %all_to_all.10 = f32[64,2,128]{2,1,0:T(2,128)S(1)} all-to-all(f32[64,2,128]{2,1,0:T(2,128)S(1)} %bitcast.10), channel_id=1, replica_groups=mesh['flow'=64,'lat'=8] {'flow'}, dimensions={0} | all-to-all | bytes 131072 | tf_op jit(solution)/shard_map/all_to_all | solution.py:285
  57.7 1.1 %fresh.1 = f32[3,16,32,128]{3,2,1,0:T(8,128)} custom-call(f32[128,128]{1,0:T(8,128)S(1)} %bitcast.9, f32[3,16,32,128]{3,2,1,0:T(8,128)S(1)} %get-tuple-element.24.src_ref, f32[3,16,32,128]{3,2,1,0:T(8,128)S(1)} %get-tuple-element.20.inv_ref, f32[3,16,32,128]{3,2,1,0:T(8,128)S(1)} %get-tuple-element.18.cour_ref, f32[2,16,32,128]{3,2,1,0:T(8,128)S(1)} %get-tuple-element.19.rate_ref), custom_call_target="tpu_custom_call" | custom-call | tf_op jit(solution)/shard_map/fresh/pallas_call | solution.py:286
Async XLA Ops:
  0.0 6.6 %copy-start = (f32[32,128]{1,0:T(8,128)S(1)}, f32[32,128]{1,0:T(8,128)}, u32[]{:S(2)}) copy-start(f32[32,128]{1,0:T(8,128)} %spread_ref.3) | copy-start | bytes 49156
  1.2 7.1 %collective-permute-start.1 = (f32[48,128]{1,0:T(8,128)S(1)}, f32[48,128]{1,0:T(8,128)S(1)}, u32[]{:S(2)}, u32[]{:S(2)}) collective-permute-start(f32[48,128]{1,0:T(8,128)S(1)} %bitcast.12), channel_id=1, source_target_pairs={{1,2},{3,4},{5,6},{2,1},{4,3},{6,5},{9,10},{11,12},{13,14},{10,9},... | collective-permute-start | bytes 73736 | tf_op jit(solution)/shard_map/ppermute | solution.py:248
  3.1 5.2 %collective-permute-start = (f32[48,128]{1,0:T(8,128)S(1)}, f32[48,128]{1,0:T(8,128)S(1)}, u32[]{:S(2)}, u32[]{:S(2)}) collective-permute-start(f32[48,128]{1,0:T(8,128)S(1)} %bitcast.11), channel_id=1, source_target_pairs={{0,1},{1,0},{2,3},{3,2},{4,5},{5,4},{6,7},{7,6},{8,9},{9,8},{10,11... | collective-permute-start | bytes 73736 | tf_op jit(solution)/shard_map/ppermute | solution.py:249
  9.4 31.9 %copy-start.1 = (f32[3,32,128]{2,1,0:T(8,128)S(1)}, f32[3,32,128]{2,1,0:T(8,128)}, u32[]{:S(2)}) copy-start(f32[3,32,128]{2,1,0:T(8,128)} %inlet_ref.1) | copy-start | bytes 147460
  9.4 31.9 %all-to-all-start = ((f32[64,8,128]{2,1,0:T(8,128)}), f32[64,8,128]{2,1,0:T(8,128)S(1)}, u32[]{:S(2)}, u32[]{:S(2)}) async-start(f32[64,8,128]{2,1,0:T(8,128)} %bitcast.4), calls=%async_computation | async-start | bytes 524288 | tf_op jit(solution)/shard_map/all_to_all | solution.py:275

commit v3 on v2

--- a/solution.py
+++ b/solution.py
@@ -10,18 +10,15 @@
 VMEM = pl.BlockSpec(memory_space=pltpu.VMEM)
 SMEM = pl.BlockSpec(memory_space=pltpu.SMEM)
 PARAMS = pltpu.CompilerParams(vmem_limit_bytes=16 * 1024 * 1024)
-SLOTS = 8
+SLOTS = 5
 
 
 def in_hbm(value):
     return pltpu.with_memory_space_constraint(value, pltpu.HBM)
 
 
-def shifted(value, distance, axis, edge):
-    size = value.shape[axis]
-    position = lax.broadcasted_iota(jnp.int32, value.shape, axis)
-    moved = pltpu.roll(value, distance % size, axis)
-    return jnp.where(position == (0 if distance == 1 else size - 1), edge, moved)
+def in_vmem(value):
+    return pltpu.with_memory_space_constraint(value, pltpu.VMEM)
 
 
 def halves(low, high):
@@ -32,55 +29,67 @@
     return first, second
 
 
-def load_kernel(core_ref, conc_ref, held_ref, link_ref, chip_ref, sems):
+def even_core(place_ref):
+    return place_ref[0] % 2 == 0
+
+
+def load_kernel(
+    place_ref, conc_ref, spread_hbm, inlet_hbm, held_ref, link_ref, chip_ref, spread_ref, inlet_ref, sems
+):
     rows = conc_ref.shape[2]
-    copies = [pltpu.make_async_copy(conc_ref.at[c], held_ref.at[c], sems.at[c]) for c in range(3)]
+    copies = [
+        pltpu.make_async_copy(conc_ref.at[c], held_ref.at[c], sems.at[c]) for c in range(3)
+    ]
+    copies.append(pltpu.make_async_copy(spread_hbm, spread_ref, sems.at[3]))
+    copies.append(pltpu.make_async_copy(inlet_hbm, inlet_ref, sems.at[4]))
     for copy in copies:
         copy.start()
-    even = core_ref[0] == 0
+    even = even_core(place_ref)
     for c in range(3):
         copies[c].wait()
         low = held_ref[c, :, 0, :]
         high = held_ref[c, :, rows - 1, :]
         link_ref[c] = jnp.where(even, low, high)
         chip_ref[c] = jnp.where(even, high, low)
-
-
-def maps_kernel(
-    conc_ref, cour_hbm, rate_hbm, spread_ref, src_ref, inv_ref, maps_ref, cour_ref, rate_ref, sems
-):
-    cells = conc_ref.shape[1]
-    part = cells // 2
+    copies[3].wait()
+    copies[4].wait()
+
+
+def maps_kernel(conc_ref, cour_ref, rate_hbm, spread_ref, src_ref, inv_ref, maps_ref, rate_ref, sems):
+    cells = src_ref.shape[1]
+    part = cells // sems.shape[0]
     loads = []
-    for h in range(2):
+    for h in range(sems.shape[0]):
         span = pl.ds(h * part, part)
-        pair = [
-            pltpu.make_async_copy(cour_hbm.at[:, span], cour_ref.at[:, span], sems.at[0, h]),
-            pltpu.make_async_copy(rate_hbm.at[:, span], rate_ref.at[:, span], sems.at[1, h]),
-        ]
-        for copy in pair:
-            copy.start()
-        loads.append(pair)
+        loads.append(pltpu.make_async_copy(rate_hbm.at[:, span], rate_ref.at[:, span], sems.at[h]))
+        loads[h].start()
     spread = spread_ref[...]
+    rows, lanes = spread.shape
+    lane = lax.broadcasted_iota(jnp.int32, spread.shape, 1)
+    from_left = jnp.where(lane == 0, 0.0, spread)
+    from_right = jnp.where(lane == lanes - 1, 0.0, spread)
+    row = lax.broadcasted_iota(jnp.int32, spread.shape, 0)
+    from_below = jnp.where(row == 0, 0.0, spread)
+    from_above = jnp.where(row == rows - 1, 0.0, spread)
+    keep = 1.0 - 4.0 * spread
     for i in range(cells):
         for c in range(3):
             x = conc_ref[c, i]
-            beside = shifted(x, -1, 0, 0.0) + shifted(x, 1, 0, 0.0)
-            beside = beside + shifted(x, -1, 1, 0.0) + shifted(x, 1, 1, 0.0)
-            src_ref[c, i] = x + spread * (beside - 4.0 * x)
+            sides = from_left * pltpu.roll(x, 1, 1) + from_right * pltpu.roll(x, lanes - 1, 1)
+            ends = from_below * pltpu.roll(x, 1, 0) + from_above * pltpu.roll(x, rows - 1, 0)
+            src_ref[c, i] = keep * x + ends + sides
     maps = None
     for i in range(cells):
         if i % part == 0:
-            for copy in loads[i // part]:
-                copy.wait()
+            loads[i // part].wait()
         src = [src_ref[c, i] for c in range(3)]
         cour = [cour_ref[c, i] for c in range(3)]
         rate = [rate_ref[c, i] for c in range(2)]
-        inv = [
-            1.0 / (1.0 + cour[0] + rate[0]),
-            1.0 / (1.0 + cour[1] + rate[1]),
-            1.0 / (1.0 + cour[2]),
-        ]
+        under = [1.0 + cour[0] + rate[0], 1.0 + cour[1] + rate[1], 1.0 + cour[2]]
+        pair = under[0] * under[1]
+        whole = 1.0 / (pair * under[2])
+        both = whole * under[2]
+        inv = [both * under[1], both * under[0], whole * pair]
         for c in range(3):
             inv_ref[c, i] = inv[c]
         gain = [cour[c] * inv[c] for c in range(3)]
@@ -121,10 +130,10 @@
 
 
 def seam_kernel(
-    core_ref, chip_ref, link_ref, spread_ref, cour_ref, rate_ref, inv_ref, maps_ref, src_in_ref, src_ref, out_ref
+    place_ref, chip_ref, link_ref, spread_ref, cour_ref, rate_ref, inv_ref, maps_ref, src_in_ref, src_ref, out_ref
 ):
     cells, rows = src_ref.shape[1:3]
-    even = core_ref[0] == 0
+    even = even_core(place_ref)
 
     def edge(ref, *index):
         return jnp.concatenate([ref[(*index, pl.ds(0, 8))], ref[(*index, pl.ds(rows - 8, 8))]], axis=0)
@@ -160,10 +169,9 @@
         listed[6 + c] = jnp.concatenate(
             [own[:8] + flux[c][:8], own[8:rows - 8], own[rows - 8:] + flux[c][8:]], axis=0
         )
-    zeros = jnp.zeros_like(listed[0])
-    listed.append(zeros)
+    listed.append(listed[8])
     for j in range(SLOTS):
-        first, second = halves(listed[2 * j], listed[2 * j + 1]) if j < 5 else (zeros, zeros)
+        first, second = halves(listed[2 * j], listed[2 * j + 1])
         out_ref[pl.ds(j, rows, stride=2 * SLOTS), :] = first
         out_ref[pl.ds(SLOTS + j, rows, stride=2 * SLOTS), :] = second
 
@@ -177,9 +185,9 @@
         map_scr[2 * j] = pair
         if 2 * j + 1 < 9:
             map_scr[2 * j + 1] = pltpu.roll(pair, half, 1)
-    place = place_ref[0]
+    place = place_ref[0] // 2
     row = place // 2
-    odd = place - 2 * row
+    odd = place % 2
     flux = []
     for c in range(3):
         line = inlet_ref[c, pl.ds(row, 1), :]
@@ -199,7 +207,7 @@
     out_ref[pl.ds(1, count, stride=2), :] = flux_scr[2]
 
 
-def fresh_kernel(flux_ref, src_ref, inv_ref, cour_ref, rate_ref, out_ref):
+def fresh_kernel(flux_ref, src_ref, inv_ref, cour_ref, rate_ref, out_hbm, out_ref, sems):
     cells, rows, lanes = src_ref.shape[1:]
     half = lanes // 2
     lane = lax.broadcasted_iota(jnp.int32, (rows, lanes), 1)
@@ -214,6 +222,8 @@
         jnp.where(lane < half, pltpu.roll(pair_l, half, 1), pair_h),
         jnp.where(lane < half, third_l, pltpu.roll(third_h, half, 1)),
     ]
+    part = cells // sems.shape[0]
+    copies = []
     for i in range(cells):
         first = inv_ref[0, i] * (src_ref[0, i] + flux[0])
         second = inv_ref[1, i] * (src_ref[1, i] + flux[1] + rate_ref[0, i] * first)
@@ -222,6 +232,12 @@
         for c in range(3):
             out_ref[c, i] = values[c]
         flux = [cour_ref[c, i] * values[c] for c in range(3)]
+        if (i + 1) % part == 0:
+            span = pl.ds(i + 1 - part, part)
+            copies.append(pltpu.make_async_copy(out_ref.at[:, span], out_hbm.at[:, span], sems.at[i // part]))
+            copies[-1].start()
+    for copy in copies:
+        copy.wait()
 
 
 def per_device(concentration, courant, rates, spread, inlet):
@@ -229,40 +245,46 @@
     count = lax.axis_size("flow")
     across = lax.axis_size("lat")
     f32 = jnp.float32
-    core = (lax.axis_index("lat") % 2).reshape(1)
-    place = lax.axis_index("flow").reshape(1)
+    place = (lax.axis_index("flow") * 2 + lax.axis_index("lat") % 2).reshape(1)
     block = jax.ShapeDtypeStruct(concentration.shape, f32)
     lines = jax.ShapeDtypeStruct((3, cells, lanes), f32)
     hbm = pl.BlockSpec(memory_space=pltpu.HBM)
-    conc, to_link, to_chip = pl.pallas_call(
+    conc, to_link, to_chip, spread, inlet = pl.pallas_call(
         load_kernel,
-        out_shape=(block, lines, lines),
-        in_specs=[SMEM, hbm],
-        out_specs=(VMEM,) * 3,
-        scratch_shapes=[pltpu.SemaphoreType.DMA((3,))],
-        compiler_params=PARAMS,
+        out_shape=(
+            block,
+            lines,
+            lines,
+            jax.ShapeDtypeStruct(spread.shape, f32),
+            jax.ShapeDtypeStruct(inlet.shape, f32),
+        ),
+        in_specs=[SMEM, hbm, hbm, hbm],
+        out_specs=(VMEM,) * 5,
+        scratch_shapes=[pltpu.SemaphoreType.DMA((5,))],
+        compiler_params=PARAMS,
+        cost_estimate=pl.CostEstimate(flops=0, bytes_accessed=64 * 1024 * 1024, transcendentals=0),
         name="load",
-    )(core, in_hbm(concentration))
+    )(place, in_hbm(concentration), in_hbm(spread), in_hbm(inlet))
     links = [(i, i + 1) for i in range(1, across - 1, 2)]
     links = links + [(b, a) for a, b in links]
     link = lax.ppermute(to_link.reshape(3 * cells, lanes), "lat", links)
     chip = lax.ppermute(to_chip.reshape(3 * cells, lanes), "lat", [(i, i ^ 1) for i in range(across)])
-    src, inv, maps, cour, rate = pl.pallas_call(
+    cour = in_vmem(courant)
+    src, inv, maps, rate = pl.pallas_call(
         maps_kernel,
         out_shape=(
             block,
             block,
             jax.ShapeDtypeStruct((9, rows, lanes), f32),
-            block,
             jax.ShapeDtypeStruct(rates.shape, f32),
         ),
-        in_specs=[VMEM, hbm, hbm, VMEM],
-        out_specs=(VMEM,) * 5,
-        scratch_shapes=[pltpu.SemaphoreType.DMA((2, 2))],
+        in_specs=[VMEM, VMEM, hbm, VMEM],
+        out_specs=(VMEM,) * 4,
+        scratch_shapes=[pltpu.SemaphoreType.DMA((4,))],
         compiler_params=PARAMS,
         cost_estimate=pl.CostEstimate(flops=0, bytes_accessed=8 * 1024 * 1024, transcendentals=0),
         name="maps",
-    )(conc, in_hbm(courant), in_hbm(rates), spread)
+    )(conc, cour, in_hbm(rates), spread)
     src, packed = pl.pallas_call(
         seam_kernel,
         out_shape=(block, jax.ShapeDtypeStruct((count * SLOTS, lanes), f32)),
@@ -271,8 +293,8 @@
         input_output_aliases={8: 0},
         compiler_params=PARAMS,
         name="seam",
-    )(core, chip, link, spread, cour, rate, inv, maps, src)
-    packed = lax.all_to_all(packed.reshape(count, SLOTS, lanes), "flow", 0, 0)
+    )(place, chip, link, spread, cour, rate, inv, maps, src)
+    packed = lax.all_to_all(packed.reshape(count, SLOTS, 1, lanes), "flow", 0, 0)
     flux = pl.pallas_call(
         relay_kernel,
         out_shape=jax.ShapeDtypeStruct((count * 2, lanes), f32),
@@ -287,7 +309,8 @@
         fresh_kernel,
         out_shape=block,
         in_specs=[VMEM] * 5,
-        out_specs=VMEM,
+        out_specs=hbm,
+        scratch_shapes=[pltpu.VMEM(block.shape, f32), pltpu.SemaphoreType.DMA((4,))],
         compiler_params=PARAMS,
         name="fresh",
     )(flux.reshape(count * 2, lanes), src, inv, cour, rate)

time: 59.1 us -> 56.2 us (0.951)
  blocking collectives: 16.1 us -> 45.8 us
  starting transfers between devices: 22.1 us -> 5.42 us
  waiting for transfers between devices: 15.1 us -> 0.01 us
  Pallas kernels: 5.34 us -> 4.67 us
    all_to_all x0 -> x1, blocking collectives: none -> 29.7 us  [per_device(): lax.all_to_all(packed.reshape(count, SLOTS, 1, lanes), 'flow', 0, 0)]
    all_to_all x1 -> x0, starting transfers between devices: 16.7 us -> none  [per_device(): packed = lax.all_to_all(packed.reshape(count, SLOTS, lanes), 'flow', 0, 0)]
    all_to_all x1 -> x0, waiting for transfers between devices: 15.1 us -> none  [per_device(): packed = lax.all_to_all(packed.reshape(count, SLOTS, lanes), 'flow', 0, 0)]
    pallas_call x1, Pallas kernels: 1.15 us -> 0.38 us  [per_device(): pl.pallas_call(seam_kernel, out_shape=(block, jax.ShapeDtypeStruct((count...]
  transfers between devices with their start and end apart: 3 -> 2, of which waited for: 1 -> 0; matrix products, arithmetic and copies ran while one was open for 0% -> 0% of each run, Pallas kernels for 3% -> 3%
where the time goes in v3:
time: 56.2 us; the launch traced here: 55.9 us
  blocking collectives  45.8 us (81%)
  starting transfers between devices  5.42 us (10%)
  Pallas kernels  4.67 us (8%)
    all_to_all x1, blocking collectives, per_device(): lax.all_to_all(packed.reshape(count, SLOTS, 1, lanes), 'flow', 0, 0)  29.7 us
    all_to_all x1, blocking collectives, per_device(): flux = lax.all_to_all(flux.reshape(count, 2, lanes), 'flow', 0, 0)  16 us
    ppermute x1, starting transfers between devices, per_device(): lax.ppermute(to_chip.reshape(3 * cells, lanes), 'lat', [(i, i ^ 1) for i...  3.5 us
    ppermute x1, starting transfers between devices, per_device(): link = lax.ppermute(to_link.reshape(3 * cells, lanes), 'lat', links)  1.92 us
    pallas_call x1, Pallas kernels, per_device(): pl.pallas_call(maps_kernel, out_shape=(block, block, jax.ShapeDtypeStruct...  1.65 us
    pallas_call x1, Pallas kernels, per_device(): pl.pallas_call(load_kernel, out_shape=(block, lines, lines, jax.ShapeDtyp...  1.24 us
  transfers between devices with their start and end apart: 2, of which 0 were waited for; matrix products, arithmetic and copies ran while one was open for 0% of the time, Pallas kernels for 3%

profile of v3, /device:TPU:2, one launch (start us, length us, event | category | flops | bytes accessed | tf_op | source)
XLA Modules:
  0.0 55.9 jit_solution(6725943616453106190)
XLA Ops:
  0.0 0.0 copy-start
  0.0 1.2 %load.1 = (f32[3,16,32,128]{3,2,1,0:T(8,128)S(1)}, f32[3,16,128]{2,1,0:T(8,128)S(1)}, f32[3,16,128]{2,1,0:T(8,128)S(1)}, f32[32,128]{1,0:T(8,128)S(1)}, f32[3,32,128]{2,1,0:T(8,128)S(1)}) custom-call(s32[1]{0:T(128)} %bitcast.place_ref, f32[3,16,32,128]{3,2,1,0:T(8,128)} %conc_ref.1, f32[32,128]{1,0:T(8,128)} %spread_hbm.1, f32[3,32,128]{2,1,0:T(8,128)} %inlet_hbm.1), custom_call_target="tpu_custom_call" | custom-call | bytes 67108864 | tf_op jit(solution)/shard_map/load/pallas_call | solution.py:252
  1.3 1.9 %collective-permute-start.1 = (f32[48,128]{1,0:T(8,128)S(1)}, f32[48,128]{1,0:T(8,128)S(1)}, u32[]{:S(2)}, u32[]{:S(2)}) collective-permute-start(f32[48,128]{1,0:T(8,128)S(1)} %bitcast.12), channel_id=1, source_target_pairs={{1,2},{3,4},{5,6},{2,1},{4,3},{6,5},{9,10},{11,12},{13,14},{10,9},... | collective-permute-start | bytes 73736 | tf_op jit(solution)/shard_map/ppermute | solution.py:270
  3.2 3.5 %collective-permute-start = (f32[48,128]{1,0:T(8,128)S(1)}, f32[48,128]{1,0:T(8,128)S(1)}, u32[]{:S(2)}, u32[]{:S(2)}) collective-permute-start(f32[48,128]{1,0:T(8,128)S(1)} %bitcast.11), channel_id=1, source_target_pairs={{0,1},{1,0},{2,3},{3,2},{4,5},{5,4},{6,7},{7,6},{8,9},{9,8},{10,11... | collective-permute-start | bytes 73736 | tf_op jit(solution)/shard_map/ppermute | solution.py:271
  6.7 0.0 copy-done
  6.7 1.7 %maps.1 = (f32[3,16,32,128]{3,2,1,0:T(8,128)S(1)}, f32[3,16,32,128]{3,2,1,0:T(8,128)S(1)}, f32[9,32,128]{2,1,0:T(8,128)S(1)}, f32[2,16,32,128]{3,2,1,0:T(8,128)S(1)}) custom-call(f32[3,16,32,128]{3,2,1,0:T(8,128)S(1)} %get-tuple-element.19.conc_ref, f32[3,16,32,128]{3,2,1,0:T(8,128)S(1)} %copy-done, f32[2,16,32,128]{3,2,1,0:T(8,128)} %rate_hbm.1, ...), custom_call_target="tpu_custom_call" | custom-call | bytes 8388608 | tf_op jit(solution)/shard_map/maps/pallas_call | solution.py:273
  8.4 0.0 collective-permute-done.1.link_ref
  8.4 0.0 collective-permute-done.chip_ref
  8.4 0.4 seam.1
  8.8 29.7 %all_to_all.10 = f32[64,5,1,128]{3,2,1,0:T(1,128)S(1)} all-to-all(f32[64,5,1,128]{3,2,1,0:T(1,128)S(1)} %bitcast.10), channel_id=1, replica_groups=mesh['flow'=64,'lat'=8] {'flow'}, dimensions={0} | all-to-all | bytes 327680 | tf_op jit(solution)/shard_map/all_to_all | solution.py:297
  38.5 0.3 relay.1
  38.8 16.0 %all_to_all.11 = f32[64,2,128]{2,1,0:T(2,128)S(1)} all-to-all(f32[64,2,128]{2,1,0:T(2,128)S(1)} %bitcast.9), channel_id=1, replica_groups=mesh['flow'=64,'lat'=8] {'flow'}, dimensions={0} | all-to-all | bytes 131072 | tf_op jit(solution)/shard_map/all_to_all | solution.py:307
  54.8 1.1 %fresh.1 = f32[3,16,32,128]{3,2,1,0:T(8,128)} custom-call(f32[128,128]{1,0:T(8,128)S(1)} %bitcast.8, f32[3,16,32,128]{3,2,1,0:T(8,128)S(1)} %get-tuple-element.26.src_ref, f32[3,16,32,128]{3,2,1,0:T(8,128)S(1)} %get-tuple-element.21.inv_ref, f32[3,16,32,128]{3,2,1,0:T(8,128)S(1)} %copy-done, f32[2,16,32,128]{3,2,1,0:T(8,128)S(1)} %get-tuple-element.20.rate_ref), custom_call_target="tpu_custom_call" | custom-call | tf_op jit(solution)/shard_map/fresh/pallas_call | solution.py:308
Async XLA Ops:
  0.0 6.7 %copy-start = (f32[3,16,32,128]{3,2,1,0:T(8,128)S(1)}, f32[3,16,32,128]{3,2,1,0:T(8,128)}, u32[]{:S(2)}) copy-start(f32[3,16,32,128]{3,2,1,0:T(8,128)} %cour_ref.5) | copy-start | bytes 2359300
  1.3 7.1 %collective-permute-start.1 = (f32[48,128]{1,0:T(8,128)S(1)}, f32[48,128]{1,0:T(8,128)S(1)}, u32[]{:S(2)}, u32[]{:S(2)}) collective-permute-start(f32[48,128]{1,0:T(8,128)S(1)} %bitcast.12), channel_id=1, source_target_pairs={{1,2},{3,4},{5,6},{2,1},{4,3},{6,5},{9,10},{11,12},{13,14},{10,9},... | collective-permute-start | bytes 73736 | tf_op jit(solution)/shard_map/ppermute | solution.py:270
  3.2 5.2 %collective-permute-start = (f32[48,128]{1,0:T(8,128)S(1)}, f32[48,128]{1,0:T(8,128)S(1)}, u32[]{:S(2)}, u32[]{:S(2)}) collective-permute-start(f32[48,128]{1,0:T(8,128)S(1)} %bitcast.11), channel_id=1, source_target_pairs={{0,1},{1,0},{2,3},{3,2},{4,5},{5,4},{6,7},{7,6},{8,9},{9,8},{10,11... | collective-permute-start | bytes 73736 | tf_op jit(solution)/shard_map/ppermute | solution.py:271

commit v4 on v3

--- a/solution.py
+++ b/solution.py
@@ -34,35 +34,41 @@
 
 
 def load_kernel(
-    place_ref, conc_ref, spread_hbm, inlet_hbm, held_ref, link_ref, chip_ref, spread_ref, inlet_ref, sems
+    place_ref,
+    conc_hbm,
+    rate_hbm,
+    spread_hbm,
+    inlet_hbm,
+    conc_ref,
+    link_ref,
+    chip_ref,
+    rate_ref,
+    spread_ref,
+    inlet_ref,
+    sems,
 ):
-    rows = conc_ref.shape[2]
-    copies = [
-        pltpu.make_async_copy(conc_ref.at[c], held_ref.at[c], sems.at[c]) for c in range(3)
+    rows = conc_hbm.shape[2]
+    edges = [pltpu.make_async_copy(conc_hbm.at[c], conc_ref.at[c], sems.at[c]) for c in range(3)]
+    others = [
+        pltpu.make_async_copy(rate_hbm, rate_ref, sems.at[3]),
+        pltpu.make_async_copy(spread_hbm, spread_ref, sems.at[4]),
+        pltpu.make_async_copy(inlet_hbm, inlet_ref, sems.at[5]),
     ]
-    copies.append(pltpu.make_async_copy(spread_hbm, spread_ref, sems.at[3]))
-    copies.append(pltpu.make_async_copy(inlet_hbm, inlet_ref, sems.at[4]))
-    for copy in copies:
+    for copy in edges + others:
         copy.start()
     even = even_core(place_ref)
     for c in range(3):
-        copies[c].wait()
-        low = held_ref[c, :, 0, :]
-        high = held_ref[c, :, rows - 1, :]
+        edges[c].wait()
+        low = conc_ref[c, :, 0, :]
+        high = conc_ref[c, :, rows - 1, :]
         link_ref[c] = jnp.where(even, low, high)
         chip_ref[c] = jnp.where(even, high, low)
-    copies[3].wait()
-    copies[4].wait()
-
-
-def maps_kernel(conc_ref, cour_ref, rate_hbm, spread_ref, src_ref, inv_ref, maps_ref, rate_ref, sems):
+    for copy in others:
+        copy.wait()
+
+
+def maps_kernel(conc_ref, cour_ref, rate_ref, spread_ref, src_ref, inv_ref, maps_ref):
     cells = src_ref.shape[1]
-    part = cells // sems.shape[0]
-    loads = []
-    for h in range(sems.shape[0]):
-        span = pl.ds(h * part, part)
-        loads.append(pltpu.make_async_copy(rate_hbm.at[:, span], rate_ref.at[:, span], sems.at[h]))
-        loads[h].start()
     spread = spread_ref[...]
     rows, lanes = spread.shape
     lane = lax.broadcasted_iota(jnp.int32, spread.shape, 1)
@@ -80,8 +86,6 @@
             src_ref[c, i] = keep * x + ends + sides
     maps = None
     for i in range(cells):
-        if i % part == 0:
-            loads[i // part].wait()
         src = [src_ref[c, i] for c in range(3)]
         cour = [cour_ref[c, i] for c in range(3)]
         rate = [rate_ref[c, i] for c in range(2)]
@@ -249,42 +253,41 @@
     block = jax.ShapeDtypeStruct(concentration.shape, f32)
     lines = jax.ShapeDtypeStruct((3, cells, lanes), f32)
     hbm = pl.BlockSpec(memory_space=pltpu.HBM)
-    conc, to_link, to_chip, spread, inlet = pl.pallas_call(
+    conc, to_link, to_chip, rate, spread, inlet = pl.pallas_call(
         load_kernel,
         out_shape=(
             block,
             lines,
             lines,
+            jax.ShapeDtypeStruct(rates.shape, f32),
             jax.ShapeDtypeStruct(spread.shape, f32),
             jax.ShapeDtypeStruct(inlet.shape, f32),
         ),
-        in_specs=[SMEM, hbm, hbm, hbm],
-        out_specs=(VMEM,) * 5,
-        scratch_shapes=[pltpu.SemaphoreType.DMA((5,))],
+        in_specs=[SMEM] + [hbm] * 4,
+        out_specs=(VMEM,) * 6,
+        scratch_shapes=[pltpu.SemaphoreType.DMA((6,))],
         compiler_params=PARAMS,
         cost_estimate=pl.CostEstimate(flops=0, bytes_accessed=64 * 1024 * 1024, transcendentals=0),
         name="load",
-    )(place, in_hbm(concentration), in_hbm(spread), in_hbm(inlet))
+    )(place, in_hbm(concentration), in_hbm(rates), in_hbm(spread), in_hbm(inlet))
     links = [(i, i + 1) for i in range(1, across - 1, 2)]
     links = links + [(b, a) for a, b in links]
     link = lax.ppermute(to_link.reshape(3 * cells, lanes), "lat", links)
     chip = lax.ppermute(to_chip.reshape(3 * cells, lanes), "lat", [(i, i ^ 1) for i in range(across)])
     cour = in_vmem(courant)
-    src, inv, maps, rate = pl.pallas_call(
+    src, inv, maps = pl.pallas_call(
         maps_kernel,
         out_shape=(
             block,
             block,
             jax.ShapeDtypeStruct((9, rows, lanes), f32),
-            jax.ShapeDtypeStruct(rates.shape, f32),
         ),
-        in_specs=[VMEM, VMEM, hbm, VMEM],
-        out_specs=(VMEM,) * 4,
-        scratch_shapes=[pltpu.SemaphoreType.DMA((4,))],
+        in_specs=[VMEM] * 4,
+        out_specs=(VMEM,) * 3,
         compiler_params=PARAMS,
         cost_estimate=pl.CostEstimate(flops=0, bytes_accessed=8 * 1024 * 1024, transcendentals=0),
         name="maps",
-    )(conc, cour, in_hbm(rates), spread)
+    )(conc, cour, rate, spread)
     src, packed = pl.pallas_call(
         seam_kernel,
         out_shape=(block, jax.ShapeDtypeStruct((count * SLOTS, lanes), f32)),

time: 56.2 us -> 55.8 us (level)
  Pallas kernels: 4.67 us -> 4.04 us
    pallas_call x1, Pallas kernels: 1.65 us -> 0.86 us  [per_device(): pl.pallas_call(maps_kernel, out_shape=(block, block, jax.ShapeDtypeStruct...]
  transfers between devices with their start and end apart: 2 -> 2, of which waited for: 0 -> 0; matrix products, arithmetic and copies ran while one was open for 0% -> 0% of each run, Pallas kernels for 3% -> 2%
where the time goes in v4:
time: 55.8 us; the launch traced here: 55.6 us
  blocking collectives  46 us (82%)
  starting transfers between devices  5.42 us (10%)
  Pallas kernels  4.04 us (7%)
    all_to_all x1, blocking collectives, per_device(): lax.all_to_all(packed.reshape(count, SLOTS, 1, lanes), 'flow', 0, 0)  30 us
    all_to_all x1, blocking collectives, per_device(): flux = lax.all_to_all(flux.reshape(count, 2, lanes), 'flow', 0, 0)  16 us
    ppermute x1, starting transfers between devices, per_device(): lax.ppermute(to_chip.reshape(3 * cells, lanes), 'lat', [(i, i ^ 1) for i...  3.5 us
    ppermute x1, starting transfers between devices, per_device(): link = lax.ppermute(to_link.reshape(3 * cells, lanes), 'lat', links)  1.92 us
    pallas_call x1, Pallas kernels, per_device(): pl.pallas_call(load_kernel, out_shape=(block, lines, lines, jax.ShapeDtyp...  1.41 us
  transfers between devices with their start and end apart: 2, of which 0 were waited for; matrix products, arithmetic and copies ran while one was open for 0% of the time, Pallas kernels for 2%

profile of v4, /device:TPU:2, one launch (start us, length us, event | category | flops | bytes accessed | tf_op | source)
XLA Modules:
  0.0 55.6 jit_solution(9121803913180719962)
XLA Ops:
  0.0 0.0 copy-start
  0.0 1.4 %load.1 = (f32[3,16,32,128]{3,2,1,0:T(8,128)S(1)}, f32[3,16,128]{2,1,0:T(8,128)S(1)}, f32[3,16,128]{2,1,0:T(8,128)S(1)}, f32[2,16,32,128]{3,2,1,0:T(8,128)S(1)},...) custom-call(s32[1]{0:T(128)} %bitcast.place_ref, f32[3,16,32,128]{3,2,1,0:T(8,128)} %conc_hbm.1, ...), custom_call_target="tpu_custom_call" | custom-call | bytes 67108864 | tf_op jit(solution)/shard_map/load/pallas_call | solution.py:256
  1.4 1.9 %collective-permute-start.1 = (f32[48,128]{1,0:T(8,128)S(1)}, f32[48,128]{1,0:T(8,128)S(1)}, u32[]{:S(2)}, u32[]{:S(2)}) collective-permute-start(f32[48,128]{1,0:T(8,128)S(1)} %bitcast.12), channel_id=1, source_target_pairs={{1,2},{3,4},{5,6},{2,1},{4,3},{6,5},{9,10},{11,12},{13,14},{10,9},... | collective-permute-start | bytes 73736 | tf_op jit(solution)/shard_map/ppermute | solution.py:275
  3.3 3.5 %collective-permute-start = (f32[48,128]{1,0:T(8,128)S(1)}, f32[48,128]{1,0:T(8,128)S(1)}, u32[]{:S(2)}, u32[]{:S(2)}) collective-permute-start(f32[48,128]{1,0:T(8,128)S(1)} %bitcast.11), channel_id=1, source_target_pairs={{0,1},{1,0},{2,3},{3,2},{4,5},{5,4},{6,7},{7,6},{8,9},{9,8},{10,11... | collective-permute-start | bytes 73736 | tf_op jit(solution)/shard_map/ppermute | solution.py:276
  6.9 0.0 copy-done
  6.9 0.9 %maps.1 = (f32[3,16,32,128]{3,2,1,0:T(8,128)S(1)}, f32[3,16,32,128]{3,2,1,0:T(8,128)S(1)}, f32[9,32,128]{2,1,0:T(8,128)S(1)}) custom-call(f32[3,16,32,128]{3,2,1,0:T(8,128)S(1)} %get-tuple-element.20.conc_ref, f32[3,16,32,128]{3,2,1,0:T(8,128)S(1)} %copy-done, f32[2,16,32,128]{3,2,1,0:T(8,128)S(1)} %get-tuple-element.19.rate_ref, ...), custom_call_target="tpu_custom_call" | custom-call | bytes 8388608 | tf_op jit(solution)/shard_map/maps/pallas_call | solution.py:278
  7.7 0.0 collective-permute-done.1.link_ref
  7.7 0.0 collective-permute-done.chip_ref
  7.8 0.4 seam.1
  8.1 30.0 %all_to_all.10 = f32[64,5,1,128]{3,2,1,0:T(1,128)S(1)} all-to-all(f32[64,5,1,128]{3,2,1,0:T(1,128)S(1)} %bitcast.10), channel_id=1, replica_groups=mesh['flow'=64,'lat'=8] {'flow'}, dimensions={0} | all-to-all | bytes 327680 | tf_op jit(solution)/shard_map/all_to_all | solution.py:300
  38.1 0.3 relay.1
  38.5 16.0 %all_to_all.11 = f32[64,2,128]{2,1,0:T(2,128)S(1)} all-to-all(f32[64,2,128]{2,1,0:T(2,128)S(1)} %bitcast.9), channel_id=1, replica_groups=mesh['flow'=64,'lat'=8] {'flow'}, dimensions={0} | all-to-all | bytes 131072 | tf_op jit(solution)/shard_map/all_to_all | solution.py:310
  54.5 1.1 %fresh.1 = f32[3,16,32,128]{3,2,1,0:T(8,128)} custom-call(f32[128,128]{1,0:T(8,128)S(1)} %bitcast.8, f32[3,16,32,128]{3,2,1,0:T(8,128)S(1)} %get-tuple-element.26.src_ref, f32[3,16,32,128]{3,2,1,0:T(8,128)S(1)} %get-tuple-element.21.inv_ref, f32[3,16,32,128]{3,2,1,0:T(8,128)S(1)} %copy-done, f32[2,16,32,128]{3,2,1,0:T(8,128)S(1)} %get-tuple-element.19.rate_ref), custom_call_target="tpu_custom_call" | custom-call | tf_op jit(solution)/shard_map/fresh/pallas_call | solution.py:311
Async XLA Ops:
  0.0 6.9 %copy-start = (f32[3,16,32,128]{3,2,1,0:T(8,128)S(1)}, f32[3,16,32,128]{3,2,1,0:T(8,128)}, u32[]{:S(2)}) copy-start(f32[3,16,32,128]{3,2,1,0:T(8,128)} %cour_ref.5) | copy-start | bytes 2359300
  1.4 6.3 %collective-permute-start.1 = (f32[48,128]{1,0:T(8,128)S(1)}, f32[48,128]{1,0:T(8,128)S(1)}, u32[]{:S(2)}, u32[]{:S(2)}) collective-permute-start(f32[48,128]{1,0:T(8,128)S(1)} %bitcast.12), channel_id=1, source_target_pairs={{1,2},{3,4},{5,6},{2,1},{4,3},{6,5},{9,10},{11,12},{13,14},{10,9},... | collective-permute-start | bytes 73736 | tf_op jit(solution)/shard_map/ppermute | solution.py:275
  3.3 4.4 %collective-permute-start = (f32[48,128]{1,0:T(8,128)S(1)}, f32[48,128]{1,0:T(8,128)S(1)}, u32[]{:S(2)}, u32[]{:S(2)}) collective-permute-start(f32[48,128]{1,0:T(8,128)S(1)} %bitcast.11), channel_id=1, source_target_pairs={{0,1},{1,0},{2,3},{3,2},{4,5},{5,4},{6,7},{7,6},{8,9},{9,8},{10,11... | collective-permute-start | bytes 73736 | tf_op jit(solution)/shard_map/ppermute | solution.py:276

commit v5 on v4

--- a/solution.py
+++ b/solution.py
@@ -29,19 +29,14 @@
     return first, second
 
 
-def even_core(place_ref):
-    return place_ref[0] % 2 == 0
-
-
 def load_kernel(
-    place_ref,
     conc_hbm,
     rate_hbm,
     spread_hbm,
     inlet_hbm,
     conc_ref,
-    link_ref,
-    chip_ref,
+    low_ref,
+    high_ref,
     rate_ref,
     spread_ref,
     inlet_ref,
@@ -56,13 +51,10 @@
     ]
     for copy in edges + others:
         copy.start()
-    even = even_core(place_ref)
     for c in range(3):
         edges[c].wait()
-        low = conc_ref[c, :, 0, :]
-        high = conc_ref[c, :, rows - 1, :]
-        link_ref[c] = jnp.where(even, low, high)
-        chip_ref[c] = jnp.where(even, high, low)
+        low_ref[c] = conc_ref[c, :, 0, :]
+        high_ref[c] = conc_ref[c, :, rows - 1, :]
     for copy in others:
         copy.wait()
 
@@ -134,20 +126,18 @@
 
 
 def seam_kernel(
-    place_ref, chip_ref, link_ref, spread_ref, cour_ref, rate_ref, inv_ref, maps_ref, src_in_ref, src_ref, out_ref
+    across, place_ref, below_ref, above_ref, spread_ref, cour_ref, rate_ref, inv_ref, maps_ref, src_in_ref, src_ref, out_ref
 ):
     cells, rows = src_ref.shape[1:3]
-    even = even_core(place_ref)
+    side = place_ref[0] % across
 
     def edge(ref, *index):
         return jnp.concatenate([ref[(*index, pl.ds(0, 8))], ref[(*index, pl.ds(rows - 8, 8))]], axis=0)
 
     spread = edge(spread_ref)
     line = lax.broadcasted_iota(jnp.int32, spread.shape, 0)
-    lower = jnp.where(line == 0, spread, 0.0)
-    upper = jnp.where(line == 15, spread, 0.0)
-    for_chip = jnp.where(even, upper, lower)
-    for_link = jnp.where(even, lower, upper)
+    from_below = jnp.where(jnp.logical_and(line == 0, side > 0), spread, 0.0)
+    from_above = jnp.where(jnp.logical_and(line == 15, side < across - 1), spread, 0.0)
     flux = None
     for i in range(cells):
         inv = [edge(inv_ref, c, i) for c in range(3)]
@@ -155,9 +145,9 @@
         rate = [edge(rate_ref, c, i) for c in range(2)]
         add = []
         for c in range(3):
-            chip = chip_ref[pl.ds(c * cells + i, 1), :]
-            link = link_ref[pl.ds(c * cells + i, 1), :]
-            value = for_chip * chip + for_link * link
+            below = below_ref[pl.ds(c * cells + i, 1), :]
+            above = above_ref[pl.ds(c * cells + i, 1), :]
+            value = from_below * below + from_above * above
             add.append(value)
             src_ref[c, i, pl.ds(0, 8)] = src_in_ref[c, i, pl.ds(0, 8)] + value[:8]
             src_ref[c, i, pl.ds(rows - 8, 8)] = src_in_ref[c, i, pl.ds(rows - 8, 8)] + value[8:]
@@ -180,7 +170,7 @@
         out_ref[pl.ds(SLOTS + j, rows, stride=2 * SLOTS), :] = second
 
 
-def relay_kernel(place_ref, maps_ref, inlet_ref, out_ref, map_scr, flux_scr):
+def relay_kernel(across, place_ref, maps_ref, inlet_ref, out_ref, map_scr, flux_scr):
     count = out_ref.shape[0] // 2
     lanes = out_ref.shape[1]
     half = lanes // 2
@@ -189,7 +179,7 @@
         map_scr[2 * j] = pair
         if 2 * j + 1 < 9:
             map_scr[2 * j + 1] = pltpu.roll(pair, half, 1)
-    place = place_ref[0] // 2
+    place = place_ref[0] // across
     row = place // 2
     odd = place % 2
     flux = []
@@ -249,11 +239,11 @@
     count = lax.axis_size("flow")
     across = lax.axis_size("lat")
     f32 = jnp.float32
-    place = (lax.axis_index("flow") * 2 + lax.axis_index("lat") % 2).reshape(1)
+    place = (lax.axis_index("flow") * across + lax.axis_index("lat")).reshape(1)
     block = jax.ShapeDtypeStruct(concentration.shape, f32)
     lines = jax.ShapeDtypeStruct((3, cells, lanes), f32)
     hbm = pl.BlockSpec(memory_space=pltpu.HBM)
-    conc, to_link, to_chip, rate, spread, inlet = pl.pallas_call(
+    conc, low, high, rate, spread, inlet = pl.pallas_call(
         load_kernel,
         out_shape=(
             block,
@@ -263,17 +253,16 @@
             jax.ShapeDtypeStruct(spread.shape, f32),
             jax.ShapeDtypeStruct(inlet.shape, f32),
         ),
-        in_specs=[SMEM] + [hbm] * 4,
+        in_specs=[hbm] * 4,
         out_specs=(VMEM,) * 6,
         scratch_shapes=[pltpu.SemaphoreType.DMA((6,))],
         compiler_params=PARAMS,
         cost_estimate=pl.CostEstimate(flops=0, bytes_accessed=64 * 1024 * 1024, transcendentals=0),
         name="load",
-    )(place, in_hbm(concentration), in_hbm(rates), in_hbm(spread), in_hbm(inlet))
-    links = [(i, i + 1) for i in range(1, across - 1, 2)]
-    links = links + [(b, a) for a, b in links]
-    link = lax.ppermute(to_link.reshape(3 * cells, lanes), "lat", links)
-    chip = lax.ppermute(to_chip.reshape(3 * cells, lanes), "lat", [(i, i ^ 1) for i in range(across)])
+    )(in_hbm(concentration), in_hbm(rates), in_hbm(spread), in_hbm(inlet))
+    ring = [(i, (i + 1) % across) for i in range(across)]
+    below = lax.ppermute(high.reshape(3 * cells, lanes), "lat", ring)
+    above = lax.ppermute(low.reshape(3 * cells, lanes), "lat", [(b, a) for a, b in ring])
     cour = in_vmem(courant)
     src, inv, maps = pl.pallas_call(
         maps_kernel,
@@ -289,17 +278,17 @@
         name="maps",
     )(conc, cour, rate, spread)
     src, packed = pl.pallas_call(
-        seam_kernel,
+        functools.partial(seam_kernel, across),
         out_shape=(block, jax.ShapeDtypeStruct((count * SLOTS, lanes), f32)),
         in_specs=[SMEM] + [VMEM] * 8,
         out_specs=(VMEM, VMEM),
         input_output_aliases={8: 0},
         compiler_params=PARAMS,
         name="seam",
-    )(place, chip, link, spread, cour, rate, inv, maps, src)
+    )(place, below, above, spread, cour, rate, inv, maps, src)
     packed = lax.all_to_all(packed.reshape(count, SLOTS, 1, lanes), "flow", 0, 0)
     flux = pl.pallas_call(
-        relay_kernel,
+        functools.partial(relay_kernel, across),
         out_shape=jax.ShapeDtypeStruct((count * 2, lanes), f32),
         in_specs=[SMEM] + [VMEM] * 2,
         out_specs=VMEM,

time: 55.8 us -> 54.4 us (0.975)
  the two profiles are of different devices: /device:TPU:2 before, /device:TPU:8 now
where the time goes in v5:
time: 54.4 us; the launch traced here: 54.2 us
  blocking collectives  44.4 us (82%)
  Pallas kernels  3.95 us (7%)
  waiting for transfers between devices  3.65 us (7%)
  starting transfers between devices  2.21 us (4%)
    all_to_all x1, blocking collectives, per_device(): lax.all_to_all(packed.reshape(count, SLOTS, 1, lanes), 'flow', 0, 0)  28.1 us
    all_to_all x1, blocking collectives, per_device(): flux = lax.all_to_all(flux.reshape(count, 2, lanes), 'flow', 0, 0)  16.2 us
    ppermute x1, waiting for transfers between devices, per_device(): below = lax.ppermute(high.reshape(3 * cells, lanes), 'lat', ring)  2.94 us
    ppermute x1, starting transfers between devices, per_device(): lax.ppermute(low.reshape(3 * cells, lanes), 'lat', [(b, a) for a, b in ri...  2.21 us
    pallas_call x1, Pallas kernels, per_device(): pl.pallas_call(load_kernel, out_shape=(block, lines, lines, jax.ShapeDtyp...  1.41 us
    pallas_call x1, Pallas kernels, per_device(): pl.pallas_call(fresh_kernel, out_shape=block, in_specs=[VMEM] * 5, out_sp...  1.09 us
  transfers between devices with their start and end apart: 2, of which 2 were waited for; matrix products, arithmetic and copies ran while one was open for 0% of the time, Pallas kernels for 1%

profile of v5, /device:TPU:8, one launch (start us, length us, event | category | flops | bytes accessed | tf_op | source)
XLA Modules:
  0.0 54.2 jit_solution(9195847603157627821)
XLA Ops:
  0.0 0.0 copy-start
  0.0 1.4 %load.1 = (f32[3,16,32,128]{3,2,1,0:T(8,128)S(1)}, f32[3,16,128]{2,1,0:T(8,128)S(1)}, f32[3,16,128]{2,1,0:T(8,128)S(1)}, f32[2,16,32,128]{3,2,1,0:T(8,128)S(1)},...) custom-call(f32[3,16,32,128]{3,2,1,0:T(8,128)} %conc_hbm.1, f32[2,16,32,128]{3,2,1,0:T(8,128)} %rate_hbm.1, ...), custom_call_target="tpu_custom_call" | custom-call | bytes 67108864 | tf_op jit(solution)/shard_map/load/pallas_call | solution.py:246
  1.4 2.2 %collective-permute-start.1 = (f32[48,128]{1,0:T(8,128)S(1)}, f32[48,128]{1,0:T(8,128)S(1)}, u32[]{:S(2)}, u32[]{:S(2)}) collective-permute-start(f32[48,128]{1,0:T(8,128)S(1)} %bitcast.12), channel_id=1, source_target_pairs={{1,0},{2,1},{3,2},{4,3},{5,4},{6,5},{7,6},{0,7},{9,8},{10,9},{11,1... | collective-permute-start | bytes 73736 | tf_op jit(solution)/shard_map/ppermute | solution.py:265
  3.6 0.0 collective-permute-start
  3.6 0.0 copy-done
  3.6 0.8 %maps.1 = (f32[3,16,32,128]{3,2,1,0:T(8,128)S(1)}, f32[3,16,32,128]{3,2,1,0:T(8,128)S(1)}, f32[9,32,128]{2,1,0:T(8,128)S(1)}) custom-call(f32[3,16,32,128]{3,2,1,0:T(8,128)S(1)} %get-tuple-element.20.conc_ref, f32[3,16,32,128]{3,2,1,0:T(8,128)S(1)} %copy-done, f32[2,16,32,128]{3,2,1,0:T(8,128)S(1)} %get-tuple-element.19.rate_ref, ...), custom_call_target="tpu_custom_call" | custom-call | bytes 8388608 | tf_op jit(solution)/shard_map/maps/pallas_call | solution.py:267
  4.4 0.7 %collective-permute-done.1.above_ref = f32[48,128]{1,0:T(8,128)S(1)} collective-permute-done((f32[48,128]{1,0:T(8,128)S(1)}, f32[48,128]{1,0:T(8,128)S(1)}, u32[]{:S(2)}, u32[]{:S(2)}) %collective-permute-start.1) | collective-permute-done | bytes 24608 | tf_op jit(solution)/shard_map/ppermute | solution.py:265
  5.1 2.9 %collective-permute-done.below_ref = f32[48,128]{1,0:T(8,128)S(1)} collective-permute-done((f32[48,128]{1,0:T(8,128)S(1)}, f32[48,128]{1,0:T(8,128)S(1)}, u32[]{:S(2)}, u32[]{:S(2)}) %collective-permute-start) | collective-permute-done | bytes 24608 | tf_op jit(solution)/shard_map/ppermute | solution.py:264
  8.1 0.3 seam.1
  8.4 28.1 %all_to_all.10 = f32[64,5,1,128]{3,2,1,0:T(1,128)S(1)} all-to-all(f32[64,5,1,128]{3,2,1,0:T(1,128)S(1)} %bitcast.10), channel_id=1, replica_groups=mesh['flow'=64,'lat'=8] {'flow'}, dimensions={0} | all-to-all | bytes 327680 | tf_op jit(solution)/shard_map/all_to_all | solution.py:289
  36.6 0.3 relay.1
  36.9 16.2 %all_to_all.11 = f32[64,2,128]{2,1,0:T(2,128)S(1)} all-to-all(f32[64,2,128]{2,1,0:T(2,128)S(1)} %bitcast.9), channel_id=1, replica_groups=mesh['flow'=64,'lat'=8] {'flow'}, dimensions={0} | all-to-all | bytes 131072 | tf_op jit(solution)/shard_map/all_to_all | solution.py:299
  53.1 1.1 %fresh.1 = f32[3,16,32,128]{3,2,1,0:T(8,128)} custom-call(f32[128,128]{1,0:T(8,128)S(1)} %bitcast.8, f32[3,16,32,128]{3,2,1,0:T(8,128)S(1)} %get-tuple-element.26.src_ref, f32[3,16,32,128]{3,2,1,0:T(8,128)S(1)} %get-tuple-element.21.inv_ref, f32[3,16,32,128]{3,2,1,0:T(8,128)S(1)} %copy-done, f32[2,16,32,128]{3,2,1,0:T(8,128)S(1)} %get-tuple-element.19.rate_ref), custom_call_target="tpu_custom_call" | custom-call | tf_op jit(solution)/shard_map/fresh/pallas_call | solution.py:300
Async XLA Ops:
  0.0 3.6 %copy-start = (f32[3,16,32,128]{3,2,1,0:T(8,128)S(1)}, f32[3,16,32,128]{3,2,1,0:T(8,128)}, u32[]{:S(2)}) copy-start(f32[3,16,32,128]{3,2,1,0:T(8,128)} %cour_ref.5) | copy-start | bytes 2359300
  1.4 3.7 %collective-permute-start.1 = (f32[48,128]{1,0:T(8,128)S(1)}, f32[48,128]{1,0:T(8,128)S(1)}, u32[]{:S(2)}, u32[]{:S(2)}) collective-permute-start(f32[48,128]{1,0:T(8,128)S(1)} %bitcast.12), channel_id=1, source_target_pairs={{1,0},{2,1},{3,2},{4,3},{5,4},{6,5},{7,6},{0,7},{9,8},{10,9},{11,1... | collective-permute-start | bytes 73736 | tf_op jit(solution)/shard_map/ppermute | solution.py:265
  3.6 4.5 %collective-permute-start = (f32[48,128]{1,0:T(8,128)S(1)}, f32[48,128]{1,0:T(8,128)S(1)}, u32[]{:S(2)}, u32[]{:S(2)}) collective-permute-start(f32[48,128]{1,0:T(8,128)S(1)} %bitcast.11), channel_id=1, source_target_pairs={{0,1},{1,2},{2,3},{3,4},{4,5},{5,6},{6,7},{7,0},{8,9},{9,10},{10,1... | collective-permute-start | bytes 73736 | tf_op jit(solution)/shard_map/ppermute | solution.py:264

commit v6 on v5

--- a/solution.py
+++ b/solution.py
@@ -126,7 +126,7 @@
 
 
 def seam_kernel(
-    across, place_ref, below_ref, above_ref, spread_ref, cour_ref, rate_ref, inv_ref, maps_ref, src_in_ref, src_ref, out_ref
+    across, place_ref, above_ref, below_ref, spread_ref, cour_ref, rate_ref, inv_ref, maps_ref, src_in_ref, src_ref, out_ref
 ):
     cells, rows = src_ref.shape[1:3]
     side = place_ref[0] % across
@@ -261,8 +261,8 @@
         name="load",
     )(in_hbm(concentration), in_hbm(rates), in_hbm(spread), in_hbm(inlet))
     ring = [(i, (i + 1) % across) for i in range(across)]
+    above = lax.ppermute(low.reshape(3 * cells, lanes), "lat", [(b, a) for a, b in ring])
     below = lax.ppermute(high.reshape(3 * cells, lanes), "lat", ring)
-    above = lax.ppermute(low.reshape(3 * cells, lanes), "lat", [(b, a) for a, b in ring])
     cour = in_vmem(courant)
     src, inv, maps = pl.pallas_call(
         maps_kernel,
@@ -285,7 +285,7 @@
         input_output_aliases={8: 0},
         compiler_params=PARAMS,
         name="seam",
-    )(place, below, above, spread, cour, rate, inv, maps, src)
+    )(place, above, below, spread, cour, rate, inv, maps, src)
     packed = lax.all_to_all(packed.reshape(count, SLOTS, 1, lanes), "flow", 0, 0)
     flux = pl.pallas_call(
         functools.partial(relay_kernel, across),

time: 54.4 us -> 53.2 us (0.978)
  the two profiles are of different devices: /device:TPU:8 before, /device:TPU:2 now
where the time goes in v6:
time: 53.2 us; the launch traced here: 52.9 us
  blocking collectives  46.5 us (87%)
  Pallas kernels  3.95 us (7%)
  starting transfers between devices  1.75 us (3%)
  waiting for transfers between devices  0.71 us (1%)
    all_to_all x1, blocking collectives, per_device(): lax.all_to_all(packed.reshape(count, SLOTS, 1, lanes), 'flow', 0, 0)  29.8 us
    all_to_all x1, blocking collectives, per_device(): flux = lax.all_to_all(flux.reshape(count, 2, lanes), 'flow', 0, 0)  16.7 us
    ppermute x1, starting transfers between devices, per_device(): lax.ppermute(low.reshape(3 * cells, lanes), 'lat', [(b, a) for a, b in ri...  1.73 us
    pallas_call x1, Pallas kernels, per_device(): pl.pallas_call(load_kernel, out_shape=(block, lines, lines, jax.ShapeDtyp...  1.41 us
    pallas_call x1, Pallas kernels, per_device(): pl.pallas_call(fresh_kernel, out_shape=block, in_specs=[VMEM] * 5, out_sp...  1.09 us
  transfers between devices with their start and end apart: 2, of which 1 were waited for; matrix products, arithmetic and copies ran while one was open for 0% of the time, Pallas kernels for 2%

profile of v6, /device:TPU:2, one launch (start us, length us, event | category | flops | bytes accessed | tf_op | source)
XLA Modules:
  0.0 52.9 jit_solution(15819092640008119042)
XLA Ops:
  0.0 0.0 copy-start
  0.0 1.4 %load.1 = (f32[3,16,32,128]{3,2,1,0:T(8,128)S(1)}, f32[3,16,128]{2,1,0:T(8,128)S(1)}, f32[3,16,128]{2,1,0:T(8,128)S(1)}, f32[2,16,32,128]{3,2,1,0:T(8,128)S(1)},...) custom-call(f32[3,16,32,128]{3,2,1,0:T(8,128)} %conc_hbm.1, f32[2,16,32,128]{3,2,1,0:T(8,128)} %rate_hbm.1, ...), custom_call_target="tpu_custom_call" | custom-call | bytes 67108864 | tf_op jit(solution)/shard_map/load/pallas_call | solution.py:246
  1.4 0.0 collective-permute-start.1
  1.4 1.7 %collective-permute-start = (f32[48,128]{1,0:T(8,128)S(1)}, f32[48,128]{1,0:T(8,128)S(1)}, u32[]{:S(2)}, u32[]{:S(2)}) collective-permute-start(f32[48,128]{1,0:T(8,128)S(1)} %bitcast.11), channel_id=1, source_target_pairs={{1,0},{2,1},{3,2},{4,3},{5,4},{6,5},{7,6},{0,7},{9,8},{10,9},{11,1... | collective-permute-start | bytes 73736 | tf_op jit(solution)/shard_map/ppermute | solution.py:264
  3.2 0.0 copy-done
  3.2 0.8 %maps.1 = (f32[3,16,32,128]{3,2,1,0:T(8,128)S(1)}, f32[3,16,32,128]{3,2,1,0:T(8,128)S(1)}, f32[9,32,128]{2,1,0:T(8,128)S(1)}) custom-call(f32[3,16,32,128]{3,2,1,0:T(8,128)S(1)} %get-tuple-element.20.conc_ref, f32[3,16,32,128]{3,2,1,0:T(8,128)S(1)} %copy-done, f32[2,16,32,128]{3,2,1,0:T(8,128)S(1)} %get-tuple-element.19.rate_ref, ...), custom_call_target="tpu_custom_call" | custom-call | bytes 8388608 | tf_op jit(solution)/shard_map/maps/pallas_call | solution.py:267
  4.0 0.7 %collective-permute-done.1.below_ref = f32[48,128]{1,0:T(8,128)S(1)} collective-permute-done((f32[48,128]{1,0:T(8,128)S(1)}, f32[48,128]{1,0:T(8,128)S(1)}, u32[]{:S(2)}, u32[]{:S(2)}) %collective-permute-start.1) | collective-permute-done | bytes 24608 | tf_op jit(solution)/shard_map/ppermute | solution.py:265
  4.7 0.0 collective-permute-done.above_ref
  4.7 0.3 seam.1
  5.0 29.8 %all_to_all.10 = f32[64,5,1,128]{3,2,1,0:T(1,128)S(1)} all-to-all(f32[64,5,1,128]{3,2,1,0:T(1,128)S(1)} %bitcast.10), channel_id=1, replica_groups=mesh['flow'=64,'lat'=8] {'flow'}, dimensions={0} | all-to-all | bytes 327680 | tf_op jit(solution)/shard_map/all_to_all | solution.py:289
  34.8 0.3 relay.1
  35.1 16.7 %all_to_all.11 = f32[64,2,128]{2,1,0:T(2,128)S(1)} all-to-all(f32[64,2,128]{2,1,0:T(2,128)S(1)} %bitcast.9), channel_id=1, replica_groups=mesh['flow'=64,'lat'=8] {'flow'}, dimensions={0} | all-to-all | bytes 131072 | tf_op jit(solution)/shard_map/all_to_all | solution.py:299
  51.8 1.1 %fresh.1 = f32[3,16,32,128]{3,2,1,0:T(8,128)} custom-call(f32[128,128]{1,0:T(8,128)S(1)} %bitcast.8, f32[3,16,32,128]{3,2,1,0:T(8,128)S(1)} %get-tuple-element.26.src_ref, f32[3,16,32,128]{3,2,1,0:T(8,128)S(1)} %get-tuple-element.21.inv_ref, f32[3,16,32,128]{3,2,1,0:T(8,128)S(1)} %copy-done, f32[2,16,32,128]{3,2,1,0:T(8,128)S(1)} %get-tuple-element.19.rate_ref), custom_call_target="tpu_custom_call" | custom-call | tf_op jit(solution)/shard_map/fresh/pallas_call | solution.py:300
Async XLA Ops:
  0.0 3.2 %copy-start = (f32[3,16,32,128]{3,2,1,0:T(8,128)S(1)}, f32[3,16,32,128]{3,2,1,0:T(8,128)}, u32[]{:S(2)}) copy-start(f32[3,16,32,128]{3,2,1,0:T(8,128)} %cour_ref.5) | copy-start | bytes 2359300
  1.4 3.3 %collective-permute-start.1 = (f32[48,128]{1,0:T(8,128)S(1)}, f32[48,128]{1,0:T(8,128)S(1)}, u32[]{:S(2)}, u32[]{:S(2)}) collective-permute-start(f32[48,128]{1,0:T(8,128)S(1)} %bitcast.12), channel_id=1, source_target_pairs={{0,1},{1,2},{2,3},{3,4},{4,5},{5,6},{6,7},{7,0},{8,9},{9,10},{10,1... | collective-permute-start | bytes 73736 | tf_op jit(solution)/shard_map/ppermute | solution.py:265
  1.4 3.3 %collective-permute-start = (f32[48,128]{1,0:T(8,128)S(1)}, f32[48,128]{1,0:T(8,128)S(1)}, u32[]{:S(2)}, u32[]{:S(2)}) collective-permute-start(f32[48,128]{1,0:T(8,128)S(1)} %bitcast.11), channel_id=1, source_target_pairs={{1,0},{2,1},{3,2},{4,3},{5,4},{6,5},{7,6},{0,7},{9,8},{10,9},{11,1... | collective-permute-start | bytes 73736 | tf_op jit(solution)/shard_map/ppermute | solution.py:264

commit v7 on v6

--- a/solution.py
+++ b/solution.py
@@ -10,6 +10,7 @@
 VMEM = pl.BlockSpec(memory_space=pltpu.VMEM)
 SMEM = pl.BlockSpec(memory_space=pltpu.SMEM)
 PARAMS = pltpu.CompilerParams(vmem_limit_bytes=16 * 1024 * 1024)
+GROUP = 8
 SLOTS = 5
 
 
@@ -29,37 +30,24 @@
     return first, second
 
 
-def load_kernel(
-    conc_hbm,
-    rate_hbm,
-    spread_hbm,
-    inlet_hbm,
-    conc_ref,
-    low_ref,
-    high_ref,
-    rate_ref,
-    spread_ref,
-    inlet_ref,
-    sems,
-):
+def edges_kernel(conc_hbm, low_ref, high_ref, sems):
     rows = conc_hbm.shape[2]
-    edges = [pltpu.make_async_copy(conc_hbm.at[c], conc_ref.at[c], sems.at[c]) for c in range(3)]
-    others = [
-        pltpu.make_async_copy(rate_hbm, rate_ref, sems.at[3]),
-        pltpu.make_async_copy(spread_hbm, spread_ref, sems.at[4]),
-        pltpu.make_async_copy(inlet_hbm, inlet_ref, sems.at[5]),
-    ]
-    for copy in edges + others:
-        copy.start()
-    for c in range(3):
-        edges[c].wait()
-        low_ref[c] = conc_ref[c, :, 0, :]
-        high_ref[c] = conc_ref[c, :, rows - 1, :]
-    for copy in others:
-        copy.wait()
-
-
-def maps_kernel(conc_ref, cour_ref, rate_ref, spread_ref, src_ref, inv_ref, maps_ref):
+    low_copy = pltpu.make_async_copy(conc_hbm.at[:, :, 0, :], low_ref, sems.at[0])
+    high_copy = pltpu.make_async_copy(conc_hbm.at[:, :, rows - 1, :], high_ref, sems.at[1])
+    low_copy.start()
+    high_copy.start()
+    low_copy.wait()
+    high_copy.wait()
+
+
+def pack(out_ref, row, low, high):
+    rows = low.shape[0]
+    first, second = halves(low, high)
+    out_ref[pl.ds(row, rows, stride=2 * SLOTS), :] = first
+    out_ref[pl.ds(SLOTS + row, rows, stride=2 * SLOTS), :] = second
+
+
+def maps_kernel(conc_ref, cour_ref, rate_ref, spread_ref, src_ref, inv_ref, off_ref, out_ref):
     cells = src_ref.shape[1]
     spread = spread_ref[...]
     rows, lanes = spread.shape
@@ -121,13 +109,27 @@
             off_p = cour[1] * u1
             off_v = gain[2] * (src[2] + off_v + rate[1] * u1)
         maps = (aa, pa, pp, va, vp, vv, off_a, off_p, off_v)
-    for j in range(9):
-        maps_ref[j] = maps[j]
+    for j in range(3):
+        pack(out_ref, j, maps[2 * j], maps[2 * j + 1])
+        off_ref[j] = maps[6 + j]
 
 
 def seam_kernel(
-    across, place_ref, above_ref, below_ref, spread_ref, cour_ref, rate_ref, inv_ref, maps_ref, src_in_ref, src_ref, out_ref
+    across,
+    place_ref,
+    above_ref,
+    below_ref,
+    spread_ref,
+    cour_ref,
+    rate_ref,
+    inv_ref,
+    off_ref,
+    src_in_ref,
+    out_in_ref,
+    src_ref,
+    out_ref,
 ):
+    del out_in_ref
     cells, rows = src_ref.shape[1:3]
     side = place_ref[0] % across
 
@@ -157,28 +159,56 @@
         u1 = inv[1] * (add[1] + rate[0] * u0)
         u2 = inv[2] * (add[2] + rate[1] * u1)
         flux = [cour[0] * u0, cour[1] * u1, cour[2] * u2]
-    listed = [maps_ref[j] for j in range(9)]
+    offset = []
     for c in range(3):
-        own = listed[6 + c]
-        listed[6 + c] = jnp.concatenate(
-            [own[:8] + flux[c][:8], own[8:rows - 8], own[rows - 8:] + flux[c][8:]], axis=0
+        own = off_ref[c]
+        offset.append(
+            jnp.concatenate([own[:8] + flux[c][:8], own[8:rows - 8], own[rows - 8:] + flux[c][8:]], axis=0)
         )
-    listed.append(listed[8])
-    for j in range(SLOTS):
-        first, second = halves(listed[2 * j], listed[2 * j + 1])
-        out_ref[pl.ds(j, rows, stride=2 * SLOTS), :] = first
-        out_ref[pl.ds(SLOTS + j, rows, stride=2 * SLOTS), :] = second
-
-
-def relay_kernel(across, place_ref, maps_ref, inlet_ref, out_ref, map_scr, flux_scr):
-    count = out_ref.shape[0] // 2
+    pack(out_ref, 3, offset[0], offset[1])
+    pack(out_ref, 4, offset[2], offset[2])
+
+
+def chained(later, earlier):
+    la, pa, pp, va, vp, vv, oa, op, ov = later
+    ea, fa, fp, ga, gp, gv, xa, xp, xv = earlier
+    return (
+        la * ea,
+        pa * ea + pp * fa,
+        pp * fp,
+        (va * ea + vp * fa) + vv * ga,
+        vp * fp + vv * gp,
+        vv * gv,
+        la * xa + oa,
+        (pa * xa + op) + pp * xp,
+        (va * xa + ov) + (vp * xp + vv * xv),
+    )
+
+
+def applied(m, flux):
+    return [
+        m[0] * flux[0] + m[6],
+        (m[1] * flux[0] + m[7]) + m[2] * flux[1],
+        (m[3] * flux[0] + m[8]) + (m[4] * flux[1] + m[5] * flux[2]),
+    ]
+
+
+def relay_kernel(across, place_ref, maps_ref, inlet_ref, out_ref, total_scr, flux_scr):
     lanes = out_ref.shape[1]
     half = lanes // 2
-    for j in range(5):
-        pair = maps_ref[pl.ds(j, count, stride=SLOTS), :]
-        map_scr[2 * j] = pair
-        if 2 * j + 1 < 9:
-            map_scr[2 * j + 1] = pltpu.roll(pair, half, 1)
+    chains = out_ref.shape[0] // (2 * GROUP)
+    before = []
+    total = None
+    for step in range(GROUP):
+        pairs = [maps_ref[pl.ds(step * SLOTS + j, chains, stride=GROUP * SLOTS), :] for j in range(SLOTS)]
+        turned = [pltpu.roll(pair, half, 1) for pair in pairs[:-1]]
+        one = (
+            pairs[0], turned[0], pairs[1], turned[1], pairs[2], turned[2], pairs[3], turned[3], pairs[4]
+        )
+        before.append(total)
+        total = one if total is None else chained(one, total)
+    for j in range(9):
+        total_scr[j] = total[j]
     place = place_ref[0] // across
     row = place // 2
     odd = place % 2
@@ -186,19 +216,18 @@
     for c in range(3):
         line = inlet_ref[c, pl.ds(row, 1), :]
         flux.append(jnp.where(odd == 1, pltpu.roll(line, half, 1), line))
-    for f in range(count):
-        for c in range(3):
-            flux_scr[c, pl.ds(f, 1), :] = flux[c]
-        m = [map_scr[j, pl.ds(f, 1), :] for j in range(9)]
-        flux = [
-            m[0] * flux[0] + m[6],
-            (m[1] * flux[0] + m[7]) + m[2] * flux[1],
-            (m[3] * flux[0] + m[8]) + (m[4] * flux[1] + m[5] * flux[2]),
-        ]
-    lane = lax.broadcasted_iota(jnp.int32, (count, lanes), 1)
-    first = jnp.where(lane < half, flux_scr[0], pltpu.roll(flux_scr[1], half, 1))
-    out_ref[pl.ds(0, count, stride=2), :] = first
-    out_ref[pl.ds(1, count, stride=2), :] = flux_scr[2]
+    for chain in range(chains):
+        for c in range(3):
+            flux_scr[c, pl.ds(chain, 1), :] = flux[c]
+        if chain + 1 < chains:
+            flux = applied([total_scr[j, pl.ds(chain, 1), :] for j in range(9)], flux)
+    heads = [flux_scr[c] for c in range(3)]
+    lane = lax.broadcasted_iota(jnp.int32, (chains, lanes), 1)
+    for step in range(GROUP):
+        flux = heads if step == 0 else applied(before[step], heads)
+        first = jnp.where(lane < half, flux[0], pltpu.roll(flux[1], half, 1))
+        out_ref[pl.ds(2 * step, chains, stride=2 * GROUP), :] = first
+        out_ref[pl.ds(2 * step + 1, chains, stride=2 * GROUP), :] = flux[2]
 
 
 def fresh_kernel(flux_ref, src_ref, inv_ref, cour_ref, rate_ref, out_hbm, out_ref, sems):
@@ -243,59 +272,53 @@
     block = jax.ShapeDtypeStruct(concentration.shape, f32)
     lines = jax.ShapeDtypeStruct((3, cells, lanes), f32)
     hbm = pl.BlockSpec(memory_space=pltpu.HBM)
-    conc, low, high, rate, spread, inlet = pl.pallas_call(
-        load_kernel,
-        out_shape=(
-            block,
-            lines,
-            lines,
-            jax.ShapeDtypeStruct(rates.shape, f32),
-            jax.ShapeDtypeStruct(spread.shape, f32),
-            jax.ShapeDtypeStruct(inlet.shape, f32),
-        ),
-        in_specs=[hbm] * 4,
-        out_specs=(VMEM,) * 6,
-        scratch_shapes=[pltpu.SemaphoreType.DMA((6,))],
-        compiler_params=PARAMS,
-        cost_estimate=pl.CostEstimate(flops=0, bytes_accessed=64 * 1024 * 1024, transcendentals=0),
-        name="load",
-    )(in_hbm(concentration), in_hbm(rates), in_hbm(spread), in_hbm(inlet))
+    low, high = pl.pallas_call(
+        edges_kernel,
+        out_shape=(lines, lines),
+        in_specs=[hbm],
+        out_specs=(VMEM, VMEM),
+        scratch_shapes=[pltpu.SemaphoreType.DMA((2,))],
+        compiler_params=PARAMS,
+        cost_estimate=pl.CostEstimate(flops=10**11, bytes_accessed=1024, transcendentals=0),
+        name="edges",
+    )(in_hbm(concentration))
     ring = [(i, (i + 1) % across) for i in range(across)]
     above = lax.ppermute(low.reshape(3 * cells, lanes), "lat", [(b, a) for a, b in ring])
     below = lax.ppermute(high.reshape(3 * cells, lanes), "lat", ring)
-    cour = in_vmem(courant)
-    src, inv, maps = pl.pallas_call(
+    conc, cour, rate = in_vmem(concentration), in_vmem(courant), in_vmem(rates)
+    spread = in_vmem(spread)
+    table = jax.ShapeDtypeStruct((count * SLOTS, lanes), f32)
+    src, inv, offset, packed = pl.pallas_call(
         maps_kernel,
-        out_shape=(
-            block,
-            block,
-            jax.ShapeDtypeStruct((9, rows, lanes), f32),
-        ),
+        out_shape=(block, block, jax.ShapeDtypeStruct((3, rows, lanes), f32), table),
         in_specs=[VMEM] * 4,
-        out_specs=(VMEM,) * 3,
+        out_specs=(VMEM,) * 4,
         compiler_params=PARAMS,
         cost_estimate=pl.CostEstimate(flops=0, bytes_accessed=8 * 1024 * 1024, transcendentals=0),
         name="maps",
     )(conc, cour, rate, spread)
     src, packed = pl.pallas_call(
         functools.partial(seam_kernel, across),
-        out_shape=(block, jax.ShapeDtypeStruct((count * SLOTS, lanes), f32)),
-        in_specs=[SMEM] + [VMEM] * 8,
+        out_shape=(block, table),
+        in_specs=[SMEM] + [VMEM] * 9,
         out_specs=(VMEM, VMEM),
-        input_output_aliases={8: 0},
+        input_output_aliases={8: 0, 9: 1},
         compiler_params=PARAMS,
         name="seam",
-    )(place, above, below, spread, cour, rate, inv, maps, src)
+    )(place, above, below, spread, cour, rate, inv, offset, src, packed)
     packed = lax.all_to_all(packed.reshape(count, SLOTS, 1, lanes), "flow", 0, 0)
     flux = pl.pallas_call(
         functools.partial(relay_kernel, across),
         out_shape=jax.ShapeDtypeStruct((count * 2, lanes), f32),
         in_specs=[SMEM] + [VMEM] * 2,
         out_specs=VMEM,
-        scratch_shapes=[pltpu.VMEM((10, count, lanes), f32), pltpu.VMEM((3, count, lanes), f32)],
+        scratch_shapes=[
+            pltpu.VMEM((9, count // GROUP, lanes), f32),
+            pltpu.VMEM((3, count // GROUP, lanes), f32),
+        ],
         compiler_params=PARAMS,
         name="relay",
-    )(place, packed.reshape(count * SLOTS, lanes), inlet)
+    )(place, packed.reshape(count * SLOTS, lanes), in_vmem(inlet))
     flux = lax.all_to_all(flux.reshape(count, 2, lanes), "flow", 0, 0)
     return pl.pallas_call(
         fresh_kernel,

time: 53.2 us -> 52.7 us (level)
  the two profiles are of different devices: /device:TPU:2 before, /device:TPU:4 now
where the time goes in v7:
time: 52.7 us; the launch traced here: 52.5 us
  blocking collectives  46.7 us (89%)
  Pallas kernels  3.3 us (6%)
  starting transfers between devices  1.75 us (3%)
  waiting for transfers between devices  0.63 us (1%)
    all_to_all x1, blocking collectives, per_device(): lax.all_to_all(packed.reshape(count, SLOTS, 1, lanes), 'flow', 0, 0)  30.4 us
    all_to_all x1, blocking collectives, per_device(): flux = lax.all_to_all(flux.reshape(count, 2, lanes), 'flow', 0, 0)  16.3 us
    ppermute x1, starting transfers between devices, per_device(): lax.ppermute(low.reshape(3 * cells, lanes), 'lat', [(b, a) for a, b in ri...  1.73 us
    pallas_call x1, Pallas kernels, per_device(): pl.pallas_call(fresh_kernel, out_shape=block, in_specs=[VMEM] * 5, out_sp...  1.09 us
  transfers between devices with their start and end apart: 2, of which 1 were waited for; matrix products, arithmetic and copies ran while one was open for 0% of the time, Pallas kernels for 2%

profile of v7, /device:TPU:4, one launch (start us, length us, event | category | flops | bytes accessed | tf_op | source)
XLA Modules:
  0.0 52.5 jit_solution(18264297114725685108)
XLA Ops:
  0.0 0.0 copy-start.2
  0.0 0.0 copy-start.1
  0.0 0.0 copy-start
  0.0 0.9 %edges.1 = (f32[3,16,128]{2,1,0:T(8,128)S(1)}, f32[3,16,128]{2,1,0:T(8,128)S(1)}) custom-call(f32[3,16,32,128]{3,2,1,0:T(8,128)} %conc_ref.1), custom_call_target="tpu_custom_call" | custom-call | flops 99999997952 | bytes 1024 | tf_op jit(solution)/shard_map/edges/pallas_call | solution.py:275
  0.9 0.0 copy-start.3
  0.9 0.0 collective-permute-start.1
  1.0 1.7 %collective-permute-start = (f32[48,128]{1,0:T(8,128)S(1)}, f32[48,128]{1,0:T(8,128)S(1)}, u32[]{:S(2)}, u32[]{:S(2)}) collective-permute-start(f32[48,128]{1,0:T(8,128)S(1)} %bitcast.11), channel_id=1, source_target_pairs={{1,0},{2,1},{3,2},{4,3},{5,4},{6,5},{7,6},{0,7},{9,8},{10,9},{11,1... | collective-permute-start | bytes 73736 | tf_op jit(solution)/shard_map/ppermute | solution.py:286
  2.7 0.0 copy-done.2
  2.7 0.0 copy-done.1
  2.7 0.0 copy-done
  2.7 0.0 copy-done.3
  2.7 0.9 %maps.1 = (f32[3,16,32,128]{3,2,1,0:T(8,128)S(1)}, f32[3,16,32,128]{3,2,1,0:T(8,128)S(1)}, f32[3,32,128]{2,1,0:T(8,128)S(1)}, f32[320,128]{1,0:T(8,128)S(1)}) custom-call(f32[3,16,32,128]{3,2,1,0:T(8,128)S(1)} %copy-done.2, f32[3,16,32,128]{3,2,1,0:T(8,128)S(1)} %copy-done, f32[2,16,32,128]{3,2,1,0:T(8,128)S(1)} %copy-done.1, f32[32,128]{1,0:T(8,128)S(1)} %copy-done.3), custom_call_target="tpu_custom_call" | custom-call | bytes 8388608 | tf_op jit(solution)/shard_map/maps/pallas_call | solution.py:291
  3.6 0.6 %collective-permute-done.1.below_ref = f32[48,128]{1,0:T(8,128)S(1)} collective-permute-done((f32[48,128]{1,0:T(8,128)S(1)}, f32[48,128]{1,0:T(8,128)S(1)}, u32[]{:S(2)}, u32[]{:S(2)}) %collective-permute-start.1) | collective-permute-done | bytes 24608 | tf_op jit(solution)/shard_map/ppermute | solution.py:287
  4.2 0.0 collective-permute-done.above_ref
  4.2 0.2 seam.1
  4.4 0.0 copy-start.4
  4.5 30.4 %all_to_all.10 = f32[64,5,1,128]{3,2,1,0:T(1,128)S(1)} all-to-all(f32[64,5,1,128]{3,2,1,0:T(1,128)S(1)} %bitcast.8), channel_id=1, replica_groups=mesh['flow'=64,'lat'=8] {'flow'}, dimensions={0} | all-to-all | bytes 327680 | tf_op jit(solution)/shard_map/all_to_all | solution.py:309
  34.9 0.0 copy-done.4
  34.9 0.2 relay.1
  35.1 16.3 %all_to_all.11 = f32[64,2,128]{2,1,0:T(2,128)S(1)} all-to-all(f32[64,2,128]{2,1,0:T(2,128)S(1)} %bitcast.10), channel_id=1, replica_groups=mesh['flow'=64,'lat'=8] {'flow'}, dimensions={0} | all-to-all | bytes 131072 | tf_op jit(solution)/shard_map/all_to_all | solution.py:322
  51.4 1.1 %fresh.1 = f32[3,16,32,128]{3,2,1,0:T(8,128)} custom-call(f32[128,128]{1,0:T(8,128)S(1)} %bitcast.9, f32[3,16,32,128]{3,2,1,0:T(8,128)S(1)} %get-tuple-element.20.src_ref, f32[3,16,32,128]{3,2,1,0:T(8,128)S(1)} %get-tuple-element.15.inv_ref, f32[3,16,32,128]{3,2,1,0:T(8,128)S(1)} %copy-done, f32[2,16,32,128]{3,2,1,0:T(8,128)S(1)} %copy-done.1), custom_call_target="tpu_custom_call" | custom-call | tf_op jit(solution)/shard_map/fresh/pallas_call | solution.py:323
Async XLA Ops:
  0.0 2.7 %copy-start.2 = (f32[3,16,32,128]{3,2,1,0:T(8,128)S(1)}, f32[3,16,32,128]{3,2,1,0:T(8,128)}, u32[]{:S(2)}) copy-start(f32[3,16,32,128]{3,2,1,0:T(8,128)} %conc_ref.1) | copy-start | bytes 2359300
  0.0 2.7 %copy-start.1 = (f32[2,16,32,128]{3,2,1,0:T(8,128)S(1)}, f32[2,16,32,128]{3,2,1,0:T(8,128)}, u32[]{:S(2)}) copy-start(f32[2,16,32,128]{3,2,1,0:T(8,128)} %rate_ref.5) | copy-start | bytes 1572868
  0.0 2.7 %copy-start = (f32[3,16,32,128]{3,2,1,0:T(8,128)S(1)}, f32[3,16,32,128]{3,2,1,0:T(8,128)}, u32[]{:S(2)}) copy-start(f32[3,16,32,128]{3,2,1,0:T(8,128)} %cour_ref.5) | copy-start | bytes 2359300
  0.9 1.8 %copy-start.3 = (f32[32,128]{1,0:T(8,128)S(1)}, f32[32,128]{1,0:T(8,128)}, u32[]{:S(2)}) copy-start(f32[32,128]{1,0:T(8,128)} %spread_ref.3) | copy-start | bytes 49156
  0.9 3.3 %collective-permute-start.1 = (f32[48,128]{1,0:T(8,128)S(1)}, f32[48,128]{1,0:T(8,128)S(1)}, u32[]{:S(2)}, u32[]{:S(2)}) collective-permute-start(f32[48,128]{1,0:T(8,128)S(1)} %bitcast.12), channel_id=1, source_target_pairs={{0,1},{1,2},{2,3},{3,4},{4,5},{5,6},{6,7},{7,0},{8,9},{9,10},{10,1... | collective-permute-start | bytes 73736 | tf_op jit(solution)/shard_map/ppermute | solution.py:287
  1.0 3.3 %collective-permute-start = (f32[48,128]{1,0:T(8,128)S(1)}, f32[48,128]{1,0:T(8,128)S(1)}, u32[]{:S(2)}, u32[]{:S(2)}) collective-permute-start(f32[48,128]{1,0:T(8,128)S(1)} %bitcast.11), channel_id=1, source_target_pairs={{1,0},{2,1},{3,2},{4,3},{5,4},{6,5},{7,6},{0,7},{9,8},{10,9},{11,1... | collective-permute-start | bytes 73736 | tf_op jit(solution)/shard_map/ppermute | solution.py:286
  4.4 30.4 %copy-start.4 = (f32[3,32,128]{2,1,0:T(8,128)S(1)}, f32[3,32,128]{2,1,0:T(8,128)}, u32[]{:S(2)}) copy-start(f32[3,32,128]{2,1,0:T(8,128)} %inlet_ref.1) | copy-start | bytes 147460

commit v8 on v7

--- a/solution.py
+++ b/solution.py
@@ -11,7 +11,7 @@
 SMEM = pl.BlockSpec(memory_space=pltpu.SMEM)
 PARAMS = pltpu.CompilerParams(vmem_limit_bytes=16 * 1024 * 1024)
 GROUP = 8
-SLOTS = 5
+SLOTS = 9
 
 
 def in_hbm(value):
@@ -20,14 +20,6 @@
 
 def in_vmem(value):
     return pltpu.with_memory_space_constraint(value, pltpu.VMEM)
-
-
-def halves(low, high):
-    lane = lax.broadcasted_iota(jnp.int32, low.shape, 1)
-    half = low.shape[1] // 2
-    first = jnp.where(lane < half, low, pltpu.roll(high, half, 1))
-    second = jnp.where(lane < half, pltpu.roll(low, half, 1), high)
-    return first, second
 
 
 def edges_kernel(conc_hbm, low_ref, high_ref, sems):
@@ -40,11 +32,10 @@
     high_copy.wait()
 
 
-def pack(out_ref, row, low, high):
-    rows = low.shape[0]
-    first, second = halves(low, high)
-    out_ref[pl.ds(row, rows, stride=2 * SLOTS), :] = first
-    out_ref[pl.ds(SLOTS + row, rows, stride=2 * SLOTS), :] = second
+def pack(out_ref, slot, value):
+    rows = value.shape[0]
+    for team in range(out_ref.shape[0] // (SLOTS * rows)):
+        out_ref[pl.ds(team * rows * SLOTS + slot, rows, stride=SLOTS), :] = value
 
 
 def maps_kernel(conc_ref, cour_ref, rate_ref, spread_ref, src_ref, inv_ref, off_ref, out_ref):
@@ -109,9 +100,10 @@
             off_p = cour[1] * u1
             off_v = gain[2] * (src[2] + off_v + rate[1] * u1)
         maps = (aa, pa, pp, va, vp, vv, off_a, off_p, off_v)
-    for j in range(3):
-        pack(out_ref, j, maps[2 * j], maps[2 * j + 1])
-        off_ref[j] = maps[6 + j]
+    for j in range(6):
+        pack(out_ref, j, maps[j])
+    for c in range(3):
+        off_ref[c] = maps[6 + c]
 
 
 def seam_kernel(
@@ -159,14 +151,10 @@
         u1 = inv[1] * (add[1] + rate[0] * u0)
         u2 = inv[2] * (add[2] + rate[1] * u1)
         flux = [cour[0] * u0, cour[1] * u1, cour[2] * u2]
-    offset = []
     for c in range(3):
         own = off_ref[c]
-        offset.append(
-            jnp.concatenate([own[:8] + flux[c][:8], own[8:rows - 8], own[rows - 8:] + flux[c][8:]], axis=0)
-        )
-    pack(out_ref, 3, offset[0], offset[1])
-    pack(out_ref, 4, offset[2], offset[2])
+        total = [own[:8] + flux[c][:8], own[8:rows - 8], own[rows - 8:] + flux[c][8:]]
+        pack(out_ref, 6 + c, jnp.concatenate(total, axis=0))
 
 
 def chained(later, earlier):
@@ -193,58 +181,40 @@
     ]
 
 
-def relay_kernel(across, place_ref, maps_ref, inlet_ref, out_ref, total_scr, flux_scr):
-    lanes = out_ref.shape[1]
-    half = lanes // 2
-    chains = out_ref.shape[0] // (2 * GROUP)
+def relay_kernel(across, place_ref, maps_ref, inlet_ref, out_ref, total_scr, head_scr, flux_scr):
+    rows = inlet_ref.shape[1]
+    chains = total_scr.shape[1]
     before = []
     total = None
     for step in range(GROUP):
-        pairs = [maps_ref[pl.ds(step * SLOTS + j, chains, stride=GROUP * SLOTS), :] for j in range(SLOTS)]
-        turned = [pltpu.roll(pair, half, 1) for pair in pairs[:-1]]
-        one = (
-            pairs[0], turned[0], pairs[1], turned[1], pairs[2], turned[2], pairs[3], turned[3], pairs[4]
+        one = tuple(
+            maps_ref[pl.ds(step * SLOTS + j, chains, stride=GROUP * SLOTS), :] for j in range(SLOTS)
         )
         before.append(total)
         total = one if total is None else chained(one, total)
     for j in range(9):
         total_scr[j] = total[j]
     place = place_ref[0] // across
-    row = place // 2
-    odd = place % 2
-    flux = []
-    for c in range(3):
-        line = inlet_ref[c, pl.ds(row, 1), :]
-        flux.append(jnp.where(odd == 1, pltpu.roll(line, half, 1), line))
+    team = place // rows
+    row = place % rows
+    flux = [inlet_ref[c, pl.ds(row, 1), :] for c in range(3)]
     for chain in range(chains):
         for c in range(3):
-            flux_scr[c, pl.ds(chain, 1), :] = flux[c]
+            head_scr[c, pl.ds(chain, 1), :] = flux[c]
         if chain + 1 < chains:
             flux = applied([total_scr[j, pl.ds(chain, 1), :] for j in range(9)], flux)
-    heads = [flux_scr[c] for c in range(3)]
-    lane = lax.broadcasted_iota(jnp.int32, (chains, lanes), 1)
+    heads = [head_scr[c] for c in range(3)]
     for step in range(GROUP):
         flux = heads if step == 0 else applied(before[step], heads)
-        first = jnp.where(lane < half, flux[0], pltpu.roll(flux[1], half, 1))
-        out_ref[pl.ds(2 * step, chains, stride=2 * GROUP), :] = first
-        out_ref[pl.ds(2 * step + 1, chains, stride=2 * GROUP), :] = flux[2]
+        for c in range(3):
+            flux_scr[pl.ds(3 * step + c, chains, stride=3 * GROUP), :] = flux[c]
+    size = out_ref.shape[0]
+    out_ref[...] = flux_scr[pl.ds(pl.multiple_of(team * size, 8), size), :]
 
 
 def fresh_kernel(flux_ref, src_ref, inv_ref, cour_ref, rate_ref, out_hbm, out_ref, sems):
-    cells, rows, lanes = src_ref.shape[1:]
-    half = lanes // 2
-    lane = lax.broadcasted_iota(jnp.int32, (rows, lanes), 1)
-
-    def half_row(h, j):
-        return flux_ref[pl.ds(2 * h + j, rows, stride=4), :]
-
-    pair_l, pair_h = half_row(0, 0), half_row(1, 0)
-    third_l, third_h = half_row(0, 1), half_row(1, 1)
-    flux = [
-        jnp.where(lane < half, pair_l, pltpu.roll(pair_h, half, 1)),
-        jnp.where(lane < half, pltpu.roll(pair_l, half, 1), pair_h),
-        jnp.where(lane < half, third_l, pltpu.roll(third_h, half, 1)),
-    ]
+    cells, rows = src_ref.shape[1:3]
+    flux = [flux_ref[pl.ds(c, rows, stride=3), :] for c in range(3)]
     part = cells // sems.shape[0]
     copies = []
     for i in range(cells):
@@ -309,17 +279,19 @@
     packed = lax.all_to_all(packed.reshape(count, SLOTS, 1, lanes), "flow", 0, 0)
     flux = pl.pallas_call(
         functools.partial(relay_kernel, across),
-        out_shape=jax.ShapeDtypeStruct((count * 2, lanes), f32),
+        out_shape=jax.ShapeDtypeStruct((rows * 3, lanes), f32),
         in_specs=[SMEM] + [VMEM] * 2,
         out_specs=VMEM,
         scratch_shapes=[
             pltpu.VMEM((9, count // GROUP, lanes), f32),
             pltpu.VMEM((3, count // GROUP, lanes), f32),
+            pltpu.VMEM((count * 3, lanes), f32),
         ],
         compiler_params=PARAMS,
         name="relay",
     )(place, packed.reshape(count * SLOTS, lanes), in_vmem(inlet))
-    flux = lax.all_to_all(flux.reshape(count, 2, lanes), "flow", 0, 0)
+    teams = [list(range(first, first + rows)) for first in range(0, count, rows)]
+    flux = lax.all_to_all(flux.reshape(rows, 3, 1, lanes), "flow", 0, 0, axis_index_groups=teams)
     return pl.pallas_call(
         fresh_kernel,
         out_shape=block,
@@ -328,7 +300,7 @@
         scratch_shapes=[pltpu.VMEM(block.shape, f32), pltpu.SemaphoreType.DMA((4,))],
         compiler_params=PARAMS,
         name="fresh",
-    )(flux.reshape(count * 2, lanes), src, inv, cour, rate)
+    )(flux.reshape(rows * 3, lanes), src, inv, cour, rate)
 
 
 def solution(mesh):

time: 52.7 us -> 52.7 us (level)
    all_to_all x1, blocking collectives: 30.4 us -> 32.3 us  [per_device(): lax.all_to_all(packed.reshape(count, SLOTS, 1, lanes), 'flow', 0, 0)]
    all_to_all x1, blocking collectives: 16.3 us -> 14.6 us  [per_device(): lax.all_to_all(flux.reshape(rows, 3, 1, lanes), 'flow', 0, 0, axis_index_...]
where the time goes in v8:
time: 52.7 us; the launch traced here: 52.5 us
  blocking collectives  46.9 us (89%)
  Pallas kernels  3.02 us (6%)
  starting transfers between devices  1.75 us (3%)
  waiting for transfers between devices  0.69 us (1%)
    all_to_all x1, blocking collectives, per_device(): lax.all_to_all(packed.reshape(count, SLOTS, 1, lanes), 'flow', 0, 0)  32.3 us
    all_to_all x1, blocking collectives, per_device(): lax.all_to_all(flux.reshape(rows, 3, 1, lanes), 'flow', 0, 0, axis_index_...  14.6 us
    ppermute x1, starting transfers between devices, per_device(): lax.ppermute(low.reshape(3 * cells, lanes), 'lat', [(b, a) for a, b in ri...  1.73 us
  transfers between devices with their start and end apart: 2, of which 1 were waited for; matrix products, arithmetic and copies ran while one was open for 0% of the time, Pallas kernels for 2%

profile of v8, /device:TPU:4, one launch (start us, length us, event | category | flops | bytes accessed | tf_op | source)
XLA Modules:
  0.0 52.5 jit_solution(2416175239257553487)
XLA Ops:
  0.0 0.0 copy-start.2
  0.0 0.0 copy-start.1
  0.0 0.0 copy-start
  0.0 0.9 %edges.1 = (f32[3,16,128]{2,1,0:T(8,128)S(1)}, f32[3,16,128]{2,1,0:T(8,128)S(1)}) custom-call(f32[3,16,32,128]{3,2,1,0:T(8,128)} %conc_ref.1), custom_call_target="tpu_custom_call" | custom-call | flops 99999997952 | bytes 1024 | tf_op jit(solution)/shard_map/edges/pallas_call | solution.py:245
  0.9 0.0 copy-start.3
  0.9 0.0 collective-permute-start.1
  1.0 1.7 %collective-permute-start = (f32[48,128]{1,0:T(8,128)S(1)}, f32[48,128]{1,0:T(8,128)S(1)}, u32[]{:S(2)}, u32[]{:S(2)}) collective-permute-start(f32[48,128]{1,0:T(8,128)S(1)} %bitcast.11), channel_id=1, source_target_pairs={{1,0},{2,1},{3,2},{4,3},{5,4},{6,5},{7,6},{0,7},{9,8},{10,9},{11,1... | collective-permute-start | bytes 73736 | tf_op jit(solution)/shard_map/ppermute | solution.py:256
  2.7 0.0 copy-done.2
  2.7 0.0 copy-done.1
  2.7 0.0 copy-done
  2.7 0.0 copy-done.3
  2.7 0.8 %maps.1 = (f32[3,16,32,128]{3,2,1,0:T(8,128)S(1)}, f32[3,16,32,128]{3,2,1,0:T(8,128)S(1)}, f32[3,32,128]{2,1,0:T(8,128)S(1)}, f32[576,128]{1,0:T(8,128)S(1)}) custom-call(f32[3,16,32,128]{3,2,1,0:T(8,128)S(1)} %copy-done.2, f32[3,16,32,128]{3,2,1,0:T(8,128)S(1)} %copy-done, f32[2,16,32,128]{3,2,1,0:T(8,128)S(1)} %copy-done.1, f32[32,128]{1,0:T(8,128)S(1)} %copy-done.3), custom_call_target="tpu_custom_call" | custom-call | bytes 8388608 | tf_op jit(solution)/shard_map/maps/pallas_call | solution.py:261
  3.5 0.7 %collective-permute-done.1.below_ref = f32[48,128]{1,0:T(8,128)S(1)} collective-permute-done((f32[48,128]{1,0:T(8,128)S(1)}, f32[48,128]{1,0:T(8,128)S(1)}, u32[]{:S(2)}, u32[]{:S(2)}) %collective-permute-start.1) | collective-permute-done | bytes 24608 | tf_op jit(solution)/shard_map/ppermute | solution.py:257
  4.2 0.0 collective-permute-done.above_ref
  4.2 0.2 seam.1
  4.5 0.0 copy-start.4
  4.5 32.3 %all_to_all.10 = f32[64,9,1,128]{3,2,1,0:T(1,128)S(1)} all-to-all(f32[64,9,1,128]{3,2,1,0:T(1,128)S(1)} %bitcast.8), channel_id=1, replica_groups=mesh['flow'=64,'lat'=8] {'flow'}, dimensions={0} | all-to-all | bytes 589824 | tf_op jit(solution)/shard_map/all_to_all | solution.py:279
  36.8 0.0 copy-done.4
  36.8 0.1 relay.1
  36.9 14.6 %all_to_all.11 = f32[32,3,1,128]{3,2,1,0:T(1,128)S(1)} all-to-all(f32[32,3,1,128]{3,2,1,0:T(1,128)S(1)} %bitcast.10), channel_id=1, replica_groups={{0,8,16,24,32,40,48,56,64,72,80,88,96,104,112,120,128,136,144,152,160,1..., dimensions={0} | all-to-all | bytes 98304 | tf_op jit(solution)/shard_map/all_to_all | solution.py:294
  51.5 0.9 %fresh.1 = f32[3,16,32,128]{3,2,1,0:T(8,128)} custom-call(f32[96,128]{1,0:T(8,128)S(1)} %bitcast.9, f32[3,16,32,128]{3,2,1,0:T(8,128)S(1)} %get-tuple-element.20.src_ref, f32[3,16,32,128]{3,2,1,0:T(8,128)S(1)} %get-tuple-element.15.inv_ref, f32[3,16,32,128]{3,2,1,0:T(8,128)S(1)} %copy-done, f32[2,16,32,128]{3,2,1,0:T(8,128)S(1)} %copy-done.1), custom_call_target="tpu_custom_call" | custom-call | tf_op jit(solution)/shard_map/fresh/pallas_call | solution.py:295
Async XLA Ops:
  0.0 2.7 %copy-start.2 = (f32[3,16,32,128]{3,2,1,0:T(8,128)S(1)}, f32[3,16,32,128]{3,2,1,0:T(8,128)}, u32[]{:S(2)}) copy-start(f32[3,16,32,128]{3,2,1,0:T(8,128)} %conc_ref.1) | copy-start | bytes 2359300
  0.0 2.7 %copy-start.1 = (f32[2,16,32,128]{3,2,1,0:T(8,128)S(1)}, f32[2,16,32,128]{3,2,1,0:T(8,128)}, u32[]{:S(2)}) copy-start(f32[2,16,32,128]{3,2,1,0:T(8,128)} %rate_ref.5) | copy-start | bytes 1572868
  0.0 2.7 %copy-start = (f32[3,16,32,128]{3,2,1,0:T(8,128)S(1)}, f32[3,16,32,128]{3,2,1,0:T(8,128)}, u32[]{:S(2)}) copy-start(f32[3,16,32,128]{3,2,1,0:T(8,128)} %cour_ref.5) | copy-start | bytes 2359300
  0.9 1.8 %copy-start.3 = (f32[32,128]{1,0:T(8,128)S(1)}, f32[32,128]{1,0:T(8,128)}, u32[]{:S(2)}) copy-start(f32[32,128]{1,0:T(8,128)} %spread_ref.3) | copy-start | bytes 49156
  0.9 3.3 %collective-permute-start.1 = (f32[48,128]{1,0:T(8,128)S(1)}, f32[48,128]{1,0:T(8,128)S(1)}, u32[]{:S(2)}, u32[]{:S(2)}) collective-permute-start(f32[48,128]{1,0:T(8,128)S(1)} %bitcast.12), channel_id=1, source_target_pairs={{0,1},{1,2},{2,3},{3,4},{4,5},{5,6},{6,7},{7,0},{8,9},{9,10},{10,1... | collective-permute-start | bytes 73736 | tf_op jit(solution)/shard_map/ppermute | solution.py:257
  1.0 3.3 %collective-permute-start = (f32[48,128]{1,0:T(8,128)S(1)}, f32[48,128]{1,0:T(8,128)S(1)}, u32[]{:S(2)}, u32[]{:S(2)}) collective-permute-start(f32[48,128]{1,0:T(8,128)S(1)} %bitcast.11), channel_id=1, source_target_pairs={{1,0},{2,1},{3,2},{4,3},{5,4},{6,5},{7,6},{0,7},{9,8},{10,9},{11,1... | collective-permute-start | bytes 73736 | tf_op jit(solution)/shard_map/ppermute | solution.py:256
  4.5 32.3 %copy-start.4 = (f32[3,32,128]{2,1,0:T(8,128)S(1)}, f32[3,32,128]{2,1,0:T(8,128)}, u32[]{:S(2)}) copy-start(f32[3,32,128]{2,1,0:T(8,128)} %inlet_ref.1) | copy-start | bytes 147460

commit v9 on v8

--- a/solution.py
+++ b/solution.py
@@ -10,7 +10,7 @@
 VMEM = pl.BlockSpec(memory_space=pltpu.VMEM)
 SMEM = pl.BlockSpec(memory_space=pltpu.SMEM)
 PARAMS = pltpu.CompilerParams(vmem_limit_bytes=16 * 1024 * 1024)
-GROUP = 8
+GROUP = 4
 SLOTS = 9
 
 
@@ -33,9 +33,7 @@
 
 
 def pack(out_ref, slot, value):
-    rows = value.shape[0]
-    for team in range(out_ref.shape[0] // (SLOTS * rows)):
-        out_ref[pl.ds(team * rows * SLOTS + slot, rows, stride=SLOTS), :] = value
+    out_ref[pl.ds(slot, value.shape[0], stride=SLOTS), :] = value
 
 
 def maps_kernel(conc_ref, cour_ref, rate_ref, spread_ref, src_ref, inv_ref, off_ref, out_ref):
@@ -181,8 +179,7 @@
     ]
 
 
-def relay_kernel(across, place_ref, maps_ref, inlet_ref, out_ref, total_scr, head_scr, flux_scr):
-    rows = inlet_ref.shape[1]
+def chains_of(maps_ref, total_scr):
     chains = total_scr.shape[1]
     before = []
     total = None
@@ -194,22 +191,46 @@
         total = one if total is None else chained(one, total)
     for j in range(9):
         total_scr[j] = total[j]
-    place = place_ref[0] // across
-    team = place // rows
-    row = place % rows
-    flux = [inlet_ref[c, pl.ds(row, 1), :] for c in range(3)]
-    for chain in range(chains):
+    return before
+
+
+def chain_at(total_scr, chain):
+    return [total_scr[j, pl.ds(chain, 1), :] for j in range(9)]
+
+
+def own_row(across, place_ref, inlet_ref):
+    rows = inlet_ref.shape[1]
+    row = (place_ref[0] // across) % rows
+    return [inlet_ref[c, pl.ds(row, 1), :] for c in range(3)]
+
+
+def middle_kernel(across, place_ref, maps_ref, inlet_ref, out_ref, total_scr):
+    chains_of(maps_ref, total_scr)
+    flux = own_row(across, place_ref, inlet_ref)
+    for chain in range(total_scr.shape[1]):
+        flux = applied(chain_at(total_scr, chain), flux)
+    for c in range(3):
+        out_ref[pl.ds(c, 1), :] = flux[c]
+
+
+def relay_kernel(across, place_ref, maps_ref, inlet_ref, middle_ref, out_ref, total_scr, head_scr):
+    chains = total_scr.shape[1]
+    before = chains_of(maps_ref, total_scr)
+    leading = place_ref[0] // across < inlet_ref.shape[1]
+    inlet = own_row(across, place_ref, inlet_ref)
+    flux = [jnp.where(leading, inlet[c], middle_ref[pl.ds(c, 1), :]) for c in range(3)]
+    shift = jnp.where(leading, 0, chains // 2)
+    for step in range(chains):
+        chain = (step + shift) % chains
         for c in range(3):
             head_scr[c, pl.ds(chain, 1), :] = flux[c]
-        if chain + 1 < chains:
-            flux = applied([total_scr[j, pl.ds(chain, 1), :] for j in range(9)], flux)
+        if step + 1 < chains:
+            flux = applied(chain_at(total_scr, chain), flux)
     heads = [head_scr[c] for c in range(3)]
     for step in range(GROUP):
         flux = heads if step == 0 else applied(before[step], heads)
         for c in range(3):
-            flux_scr[pl.ds(3 * step + c, chains, stride=3 * GROUP), :] = flux[c]
-    size = out_ref.shape[0]
-    out_ref[...] = flux_scr[pl.ds(pl.multiple_of(team * size, 8), size), :]
+            out_ref[pl.ds(3 * step + c, chains, stride=3 * GROUP), :] = flux[c]
 
 
 def fresh_kernel(flux_ref, src_ref, inv_ref, cour_ref, rate_ref, out_hbm, out_ref, sems):
@@ -257,7 +278,7 @@
     below = lax.ppermute(high.reshape(3 * cells, lanes), "lat", ring)
     conc, cour, rate = in_vmem(concentration), in_vmem(courant), in_vmem(rates)
     spread = in_vmem(spread)
-    table = jax.ShapeDtypeStruct((count * SLOTS, lanes), f32)
+    table = jax.ShapeDtypeStruct((rows * SLOTS, lanes), f32)
     src, inv, offset, packed = pl.pallas_call(
         maps_kernel,
         out_shape=(block, block, jax.ShapeDtypeStruct((3, rows, lanes), f32), table),
@@ -276,21 +297,32 @@
         compiler_params=PARAMS,
         name="seam",
     )(place, above, below, spread, cour, rate, inv, offset, src, packed)
-    packed = lax.all_to_all(packed.reshape(count, SLOTS, 1, lanes), "flow", 0, 0)
+    assert count == 2 * rows
+    middle = rows + rows // 2
+    teams = [list(range(rows)), [*range(middle, count), *range(rows, middle)]]
+    packed = lax.all_to_all(packed.reshape(rows, SLOTS, 1, lanes), "flow", 0, 0, axis_index_groups=teams)
+    packed = packed.reshape(rows * SLOTS, lanes)
+    inlet = in_vmem(inlet)
+    totals = pltpu.VMEM((9, rows // GROUP, lanes), f32)
+    middle = pl.pallas_call(
+        functools.partial(middle_kernel, across),
+        out_shape=jax.ShapeDtypeStruct((3, lanes), f32),
+        in_specs=[SMEM] + [VMEM] * 2,
+        out_specs=VMEM,
+        scratch_shapes=[totals],
+        compiler_params=PARAMS,
+        name="middle",
+    )(place, packed, inlet)
+    middle = lax.ppermute(middle, "flow", list(zip(*teams)))
     flux = pl.pallas_call(
         functools.partial(relay_kernel, across),
         out_shape=jax.ShapeDtypeStruct((rows * 3, lanes), f32),
-        in_specs=[SMEM] + [VMEM] * 2,
+        in_specs=[SMEM] + [VMEM] * 3,
         out_specs=VMEM,
-        scratch_shapes=[
-            pltpu.VMEM((9, count // GROUP, lanes), f32),
-            pltpu.VMEM((3, count // GROUP, lanes), f32),
-            pltpu.VMEM((count * 3, lanes), f32),
-        ],
+        scratch_shapes=[totals, pltpu.VMEM((3, rows // GROUP, lanes), f32)],
         compiler_params=PARAMS,
         name="relay",
-    )(place, packed.reshape(count * SLOTS, lanes), in_vmem(inlet))
-    teams = [list(range(first, first + rows)) for first in range(0, count, rows)]
+    )(place, packed, inlet, middle)
     flux = lax.all_to_all(flux.reshape(rows, 3, 1, lanes), "flow", 0, 0, axis_index_groups=teams)
     return pl.pallas_call(
         fresh_kernel,

time: 52.7 us -> 50.6 us (0.960)
  the two profiles are of different devices: /device:TPU:4 before, /device:TPU:56 now
where the time goes in v9:
time: 50.6 us; the launch traced here: 50.3 us
  blocking collectives  36 us (71%)
  waiting for transfers between devices  6.98 us (14%)
  starting transfers between devices  4.25 us (8%)
  Pallas kernels  3.02 us (6%)
    all_to_all x1, blocking collectives, per_device(): lax.all_to_all(packed.reshape(rows, SLOTS, 1, lanes), 'flow', 0, 0, axis_...  23.2 us
    all_to_all x1, blocking collectives, per_device(): lax.all_to_all(flux.reshape(rows, 3, 1, lanes), 'flow', 0, 0, axis_index_...  12.8 us
    ppermute x1, waiting for transfers between devices, per_device(): middle = lax.ppermute(middle, 'flow', list(zip(*teams)))  6.29 us
    ppermute x1, starting transfers between devices, per_device(): lax.ppermute(low.reshape(3 * cells, lanes), 'lat', [(b, a) for a, b in ri...  2.94 us
    ppermute x1, starting transfers between devices, per_device(): middle = lax.ppermute(middle, 'flow', list(zip(*teams)))  1.29 us
  transfers between devices with their start and end apart: 3, of which 2 were waited for; matrix products, arithmetic and copies ran while one was open for 0% of the time, Pallas kernels for 2%

profile of v9, /device:TPU:56, one launch (start us, length us, event | category | flops | bytes accessed | tf_op | source)
XLA Modules:
  0.0 50.3 jit_solution(1265295356613136392)
XLA Ops:
  0.0 0.0 copy-start.2
  0.0 0.0 copy-start.1
  0.0 0.0 copy-start
  0.0 0.9 %edges.1 = (f32[3,16,128]{2,1,0:T(8,128)S(1)}, f32[3,16,128]{2,1,0:T(8,128)S(1)}) custom-call(f32[3,16,32,128]{3,2,1,0:T(8,128)} %conc_ref.1), custom_call_target="tpu_custom_call" | custom-call | flops 99999997952 | bytes 1024 | tf_op jit(solution)/shard_map/edges/pallas_call | solution.py:266
  0.9 0.0 copy-start.4
  0.9 0.0 collective-permute-start.1
  1.0 2.9 %collective-permute-start = (f32[48,128]{1,0:T(8,128)S(1)}, f32[48,128]{1,0:T(8,128)S(1)}, u32[]{:S(2)}, u32[]{:S(2)}) collective-permute-start(f32[48,128]{1,0:T(8,128)S(1)} %bitcast.12), channel_id=1, source_target_pairs={{1,0},{2,1},{3,2},{4,3},{5,4},{6,5},{7,6},{0,7},{9,8},{10,9},{11,1... | collective-permute-start | bytes 73736 | tf_op jit(solution)/shard_map/ppermute | solution.py:277
  3.9 0.0 copy-done.2
  3.9 0.0 copy-done.1
  3.9 0.0 copy-done
  3.9 0.0 copy-done.4
  3.9 0.8 %maps.1 = (f32[3,16,32,128]{3,2,1,0:T(8,128)S(1)}, f32[3,16,32,128]{3,2,1,0:T(8,128)S(1)}, f32[3,32,128]{2,1,0:T(8,128)S(1)}, f32[288,128]{1,0:T(8,128)S(1)}) custom-call(f32[3,16,32,128]{3,2,1,0:T(8,128)S(1)} %copy-done.2, f32[3,16,32,128]{3,2,1,0:T(8,128)S(1)} %copy-done, f32[2,16,32,128]{3,2,1,0:T(8,128)S(1)} %copy-done.1, f32[32,128]{1,0:T(8,128)S(1)} %copy-done.4), custom_call_target="tpu_custom_call" | custom-call | bytes 8388608 | tf_op jit(solution)/shard_map/maps/pallas_call | solution.py:282
  4.7 0.7 %collective-permute-done.1.below_ref = f32[48,128]{1,0:T(8,128)S(1)} collective-permute-done((f32[48,128]{1,0:T(8,128)S(1)}, f32[48,128]{1,0:T(8,128)S(1)}, u32[]{:S(2)}, u32[]{:S(2)}) %collective-permute-start.1) | collective-permute-done | bytes 24608 | tf_op jit(solution)/shard_map/ppermute | solution.py:278
  5.4 0.0 collective-permute-done.above_ref
  5.4 0.2 seam.1
  5.7 0.0 copy-start.3
  5.7 23.2 %all_to_all.10 = f32[32,9,1,128]{3,2,1,0:T(1,128)S(1)} all-to-all(f32[32,9,1,128]{3,2,1,0:T(1,128)S(1)} %bitcast.9), channel_id=1, replica_groups={{0,8,16,24,32,40,48,56,64,72,80,88,96,104,112,120,128,136,144,152,160,1..., dimensions={0} | all-to-all | bytes 294912 | tf_op jit(solution)/shard_map/all_to_all | solution.py:303
  28.9 0.0 copy-done.3
  28.9 1.3 %collective-permute-start.2 = (f32[3,128]{1,0:T(4,128)S(1)}, f32[3,128]{1,0:T(4,128)S(1)}, u32[]{:S(2)}, u32[]{:S(2)}) collective-permute-start(f32[3,128]{1,0:T(4,128)S(1)} %middle.1), channel_id=1, source_target_pairs={{0,384},{8,392},{16,400},{24,408},{32,416},{40,424},{48,432},{56,4... | collective-permute-start | bytes 4616 | tf_op jit(solution)/shard_map/ppermute | solution.py:316
  30.2 6.3 %collective-permute-done.2.middle_ref = f32[3,128]{1,0:T(4,128)S(1)} collective-permute-done((f32[3,128]{1,0:T(4,128)S(1)}, f32[3,128]{1,0:T(4,128)S(1)}, u32[]{:S(2)}, u32[]{:S(2)}) %collective-permute-start.2) | collective-permute-done | bytes 1568 | tf_op jit(solution)/shard_map/ppermute | solution.py:316
  36.5 0.1 relay.1
  36.6 12.8 %all_to_all.11 = f32[32,3,1,128]{3,2,1,0:T(1,128)S(1)} all-to-all(f32[32,3,1,128]{3,2,1,0:T(1,128)S(1)} %bitcast.11), channel_id=1, replica_groups={{0,8,16,24,32,40,48,56,64,72,80,88,96,104,112,120,128,136,144,152,160,1..., dimensions={0} | all-to-all | bytes 98304 | tf_op jit(solution)/shard_map/all_to_all | solution.py:326
  49.4 0.9 %fresh.1 = f32[3,16,32,128]{3,2,1,0:T(8,128)} custom-call(f32[96,128]{1,0:T(8,128)S(1)} %bitcast.10, f32[3,16,32,128]{3,2,1,0:T(8,128)S(1)} %get-tuple-element.20.src_ref, f32[3,16,32,128]{3,2,1,0:T(8,128)S(1)} %get-tuple-element.15.inv_ref, f32[3,16,32,128]{3,2,1,0:T(8,128)S(1)} %copy-done, f32[2,16,32,128]{3,2,1,0:T(8,128)S(1)} %copy-done.1), custom_call_target="tpu_custom_call" | custom-call | tf_op jit(solution)/shard_map/fresh/pallas_call | solution.py:327
  (1 shorter events, 0.0 us)
Async XLA Ops:
  0.0 3.9 %copy-start.2 = (f32[3,16,32,128]{3,2,1,0:T(8,128)S(1)}, f32[3,16,32,128]{3,2,1,0:T(8,128)}, u32[]{:S(2)}) copy-start(f32[3,16,32,128]{3,2,1,0:T(8,128)} %conc_ref.1) | copy-start | bytes 2359300
  0.0 3.9 %copy-start.1 = (f32[2,16,32,128]{3,2,1,0:T(8,128)S(1)}, f32[2,16,32,128]{3,2,1,0:T(8,128)}, u32[]{:S(2)}) copy-start(f32[2,16,32,128]{3,2,1,0:T(8,128)} %rate_ref.5) | copy-start | bytes 1572868
  0.0 3.9 %copy-start = (f32[3,16,32,128]{3,2,1,0:T(8,128)S(1)}, f32[3,16,32,128]{3,2,1,0:T(8,128)}, u32[]{:S(2)}) copy-start(f32[3,16,32,128]{3,2,1,0:T(8,128)} %cour_ref.5) | copy-start | bytes 2359300
  0.9 3.0 %copy-start.4 = (f32[32,128]{1,0:T(8,128)S(1)}, f32[32,128]{1,0:T(8,128)}, u32[]{:S(2)}) copy-start(f32[32,128]{1,0:T(8,128)} %spread_ref.3) | copy-start | bytes 49156
  0.9 4.5 %collective-permute-start.1 = (f32[48,128]{1,0:T(8,128)S(1)}, f32[48,128]{1,0:T(8,128)S(1)}, u32[]{:S(2)}, u32[]{:S(2)}) collective-permute-start(f32[48,128]{1,0:T(8,128)S(1)} %bitcast.13), channel_id=1, source_target_pairs={{0,1},{1,2},{2,3},{3,4},{4,5},{5,6},{6,7},{7,0},{8,9},{9,10},{10,1... | collective-permute-start | bytes 73736 | tf_op jit(solution)/shard_map/ppermute | solution.py:278
  1.0 4.5 %collective-permute-start = (f32[48,128]{1,0:T(8,128)S(1)}, f32[48,128]{1,0:T(8,128)S(1)}, u32[]{:S(2)}, u32[]{:S(2)}) collective-permute-start(f32[48,128]{1,0:T(8,128)S(1)} %bitcast.12), channel_id=1, source_target_pairs={{1,0},{2,1},{3,2},{4,3},{5,4},{6,5},{7,6},{0,7},{9,8},{10,9},{11,1... | collective-permute-start | bytes 73736 | tf_op jit(solution)/shard_map/ppermute | solution.py:277
  5.7 23.2 %copy-start.3 = (f32[3,32,128]{2,1,0:T(8,128)S(1)}, f32[3,32,128]{2,1,0:T(8,128)}, u32[]{:S(2)}) copy-start(f32[3,32,128]{2,1,0:T(8,128)} %inlet_ref.3) | copy-start | bytes 147460
  28.9 7.6 %collective-permute-start.2 = (f32[3,128]{1,0:T(4,128)S(1)}, f32[3,128]{1,0:T(4,128)S(1)}, u32[]{:S(2)}, u32[]{:S(2)}) collective-permute-start(f32[3,128]{1,0:T(4,128)S(1)} %middle.1), channel_id=1, source_target_pairs={{0,384},{8,392},{16,400},{24,408},{32,416},{40,424},{48,432},{56,4... | collective-permute-start | bytes 4616 | tf_op jit(solution)/shard_map/ppermute | solution.py:316

commit v10 on v9

--- a/solution.py
+++ b/solution.py
@@ -24,12 +24,14 @@
 
 def edges_kernel(conc_hbm, low_ref, high_ref, sems):
     rows = conc_hbm.shape[2]
-    low_copy = pltpu.make_async_copy(conc_hbm.at[:, :, 0, :], low_ref, sems.at[0])
-    high_copy = pltpu.make_async_copy(conc_hbm.at[:, :, rows - 1, :], high_ref, sems.at[1])
-    low_copy.start()
-    high_copy.start()
-    low_copy.wait()
-    high_copy.wait()
+    copies = []
+    for c in range(3):
+        copies.append(pltpu.make_async_copy(conc_hbm.at[c, :, rows - 1, :], high_ref.at[c], sems.at[0, c]))
+        copies.append(pltpu.make_async_copy(conc_hbm.at[c, :, 0, :], low_ref.at[c], sems.at[1, c]))
+    for copy in copies:
+        copy.start()
+    for copy in copies:
+        copy.wait()
 
 
 def pack(out_ref, slot, value):
@@ -268,7 +270,7 @@
         out_shape=(lines, lines),
         in_specs=[hbm],
         out_specs=(VMEM, VMEM),
-        scratch_shapes=[pltpu.SemaphoreType.DMA((2,))],
+        scratch_shapes=[pltpu.SemaphoreType.DMA((2, 3))],
         compiler_params=PARAMS,
         cost_estimate=pl.CostEstimate(flops=10**11, bytes_accessed=1024, transcendentals=0),
         name="edges",

time: 50.6 us -> 50.6 us (level)
  no operation moved by 1% of the time
where the time goes in v10:
time: 50.6 us; the launch traced here: 50.4 us
  blocking collectives  36 us (71%)
  waiting for transfers between devices  6.98 us (14%)
  starting transfers between devices  4.25 us (8%)
  Pallas kernels  3.08 us (6%)
    all_to_all x1, blocking collectives, per_device(): lax.all_to_all(packed.reshape(rows, SLOTS, 1, lanes), 'flow', 0, 0, axis_...  23.2 us
    all_to_all x1, blocking collectives, per_device(): lax.all_to_all(flux.reshape(rows, 3, 1, lanes), 'flow', 0, 0, axis_index_...  12.8 us
    ppermute x1, waiting for transfers between devices, per_device(): middle = lax.ppermute(middle, 'flow', list(zip(*teams)))  6.29 us
    ppermute x1, starting transfers between devices, per_device(): lax.ppermute(low.reshape(3 * cells, lanes), 'lat', [(b, a) for a, b in ri...  2.94 us
    ppermute x1, starting transfers between devices, per_device(): middle = lax.ppermute(middle, 'flow', list(zip(*teams)))  1.29 us
  transfers between devices with their start and end apart: 3, of which 2 were waited for; matrix products, arithmetic and copies ran while one was open for 0% of the time, Pallas kernels for 2%

profile of v10, /device:TPU:56, one launch (start us, length us, event | category | flops | bytes accessed | tf_op | source)
XLA Modules:
  0.0 50.4 jit_solution(7918295483215011003)
XLA Ops:
  0.0 0.0 copy-start.2
  0.0 0.0 copy-start.1
  0.0 0.0 copy-start
  0.0 1.0 %edges.1 = (f32[3,16,128]{2,1,0:T(8,128)S(1)}, f32[3,16,128]{2,1,0:T(8,128)S(1)}) custom-call(f32[3,16,32,128]{3,2,1,0:T(8,128)} %conc_ref.1), custom_call_target="tpu_custom_call" | custom-call | flops 99999997952 | bytes 1024 | tf_op jit(solution)/shard_map/edges/pallas_call | solution.py:268
  1.0 0.0 copy-start.4
  1.0 0.0 collective-permute-start.1
  1.0 2.9 %collective-permute-start = (f32[48,128]{1,0:T(8,128)S(1)}, f32[48,128]{1,0:T(8,128)S(1)}, u32[]{:S(2)}, u32[]{:S(2)}) collective-permute-start(f32[48,128]{1,0:T(8,128)S(1)} %bitcast.12), channel_id=1, source_target_pairs={{1,0},{2,1},{3,2},{4,3},{5,4},{6,5},{7,6},{0,7},{9,8},{10,9},{11,1... | collective-permute-start | bytes 73736 | tf_op jit(solution)/shard_map/ppermute | solution.py:279
  4.0 0.0 copy-done.2
  4.0 0.0 copy-done.1
  4.0 0.0 copy-done
  4.0 0.0 copy-done.4
  4.0 0.8 %maps.1 = (f32[3,16,32,128]{3,2,1,0:T(8,128)S(1)}, f32[3,16,32,128]{3,2,1,0:T(8,128)S(1)}, f32[3,32,128]{2,1,0:T(8,128)S(1)}, f32[288,128]{1,0:T(8,128)S(1)}) custom-call(f32[3,16,32,128]{3,2,1,0:T(8,128)S(1)} %copy-done.2, f32[3,16,32,128]{3,2,1,0:T(8,128)S(1)} %copy-done, f32[2,16,32,128]{3,2,1,0:T(8,128)S(1)} %copy-done.1, f32[32,128]{1,0:T(8,128)S(1)} %copy-done.4), custom_call_target="tpu_custom_call" | custom-call | bytes 8388608 | tf_op jit(solution)/shard_map/maps/pallas_call | solution.py:284
  4.8 0.7 %collective-permute-done.1.below_ref = f32[48,128]{1,0:T(8,128)S(1)} collective-permute-done((f32[48,128]{1,0:T(8,128)S(1)}, f32[48,128]{1,0:T(8,128)S(1)}, u32[]{:S(2)}, u32[]{:S(2)}) %collective-permute-start.1) | collective-permute-done | bytes 24608 | tf_op jit(solution)/shard_map/ppermute | solution.py:280
  5.5 0.0 collective-permute-done.above_ref
  5.5 0.2 seam.1
  5.7 0.0 copy-start.3
  5.8 23.2 %all_to_all.10 = f32[32,9,1,128]{3,2,1,0:T(1,128)S(1)} all-to-all(f32[32,9,1,128]{3,2,1,0:T(1,128)S(1)} %bitcast.9), channel_id=1, replica_groups={{0,8,16,24,32,40,48,56,64,72,80,88,96,104,112,120,128,136,144,152,160,1..., dimensions={0} | all-to-all | bytes 294912 | tf_op jit(solution)/shard_map/all_to_all | solution.py:305
  28.9 0.0 copy-done.3
  29.0 1.3 %collective-permute-start.2 = (f32[3,128]{1,0:T(4,128)S(1)}, f32[3,128]{1,0:T(4,128)S(1)}, u32[]{:S(2)}, u32[]{:S(2)}) collective-permute-start(f32[3,128]{1,0:T(4,128)S(1)} %middle.1), channel_id=1, source_target_pairs={{0,384},{8,392},{16,400},{24,408},{32,416},{40,424},{48,432},{56,4... | collective-permute-start | bytes 4616 | tf_op jit(solution)/shard_map/ppermute | solution.py:318
  30.3 6.3 %collective-permute-done.2.middle_ref = f32[3,128]{1,0:T(4,128)S(1)} collective-permute-done((f32[3,128]{1,0:T(4,128)S(1)}, f32[3,128]{1,0:T(4,128)S(1)}, u32[]{:S(2)}, u32[]{:S(2)}) %collective-permute-start.2) | collective-permute-done | bytes 1568 | tf_op jit(solution)/shard_map/ppermute | solution.py:318
  36.6 0.1 relay.1
  36.6 12.8 %all_to_all.11 = f32[32,3,1,128]{3,2,1,0:T(1,128)S(1)} all-to-all(f32[32,3,1,128]{3,2,1,0:T(1,128)S(1)} %bitcast.11), channel_id=1, replica_groups={{0,8,16,24,32,40,48,56,64,72,80,88,96,104,112,120,128,136,144,152,160,1..., dimensions={0} | all-to-all | bytes 98304 | tf_op jit(solution)/shard_map/all_to_all | solution.py:328
  49.4 0.9 %fresh.1 = f32[3,16,32,128]{3,2,1,0:T(8,128)} custom-call(f32[96,128]{1,0:T(8,128)S(1)} %bitcast.10, f32[3,16,32,128]{3,2,1,0:T(8,128)S(1)} %get-tuple-element.20.src_ref, f32[3,16,32,128]{3,2,1,0:T(8,128)S(1)} %get-tuple-element.15.inv_ref, f32[3,16,32,128]{3,2,1,0:T(8,128)S(1)} %copy-done, f32[2,16,32,128]{3,2,1,0:T(8,128)S(1)} %copy-done.1), custom_call_target="tpu_custom_call" | custom-call | tf_op jit(solution)/shard_map/fresh/pallas_call | solution.py:329
  (1 shorter events, 0.0 us)
Async XLA Ops:
  0.0 4.0 %copy-start.2 = (f32[3,16,32,128]{3,2,1,0:T(8,128)S(1)}, f32[3,16,32,128]{3,2,1,0:T(8,128)}, u32[]{:S(2)}) copy-start(f32[3,16,32,128]{3,2,1,0:T(8,128)} %conc_ref.1) | copy-start | bytes 2359300
  0.0 4.0 %copy-start.1 = (f32[2,16,32,128]{3,2,1,0:T(8,128)S(1)}, f32[2,16,32,128]{3,2,1,0:T(8,128)}, u32[]{:S(2)}) copy-start(f32[2,16,32,128]{3,2,1,0:T(8,128)} %rate_ref.5) | copy-start | bytes 1572868
  0.0 4.0 %copy-start = (f32[3,16,32,128]{3,2,1,0:T(8,128)S(1)}, f32[3,16,32,128]{3,2,1,0:T(8,128)}, u32[]{:S(2)}) copy-start(f32[3,16,32,128]{3,2,1,0:T(8,128)} %cour_ref.5) | copy-start | bytes 2359300
  1.0 3.0 %copy-start.4 = (f32[32,128]{1,0:T(8,128)S(1)}, f32[32,128]{1,0:T(8,128)}, u32[]{:S(2)}) copy-start(f32[32,128]{1,0:T(8,128)} %spread_ref.3) | copy-start | bytes 49156
  1.0 4.5 %collective-permute-start.1 = (f32[48,128]{1,0:T(8,128)S(1)}, f32[48,128]{1,0:T(8,128)S(1)}, u32[]{:S(2)}, u32[]{:S(2)}) collective-permute-start(f32[48,128]{1,0:T(8,128)S(1)} %bitcast.13), channel_id=1, source_target_pairs={{0,1},{1,2},{2,3},{3,4},{4,5},{5,6},{6,7},{7,0},{8,9},{9,10},{10,1... | collective-permute-start | bytes 73736 | tf_op jit(solution)/shard_map/ppermute | solution.py:280
  1.0 4.5 %collective-permute-start = (f32[48,128]{1,0:T(8,128)S(1)}, f32[48,128]{1,0:T(8,128)S(1)}, u32[]{:S(2)}, u32[]{:S(2)}) collective-permute-start(f32[48,128]{1,0:T(8,128)S(1)} %bitcast.12), channel_id=1, source_target_pairs={{1,0},{2,1},{3,2},{4,3},{5,4},{6,5},{7,6},{0,7},{9,8},{10,9},{11,1... | collective-permute-start | bytes 73736 | tf_op jit(solution)/shard_map/ppermute | solution.py:279
  5.7 23.2 %copy-start.3 = (f32[3,32,128]{2,1,0:T(8,128)S(1)}, f32[3,32,128]{2,1,0:T(8,128)}, u32[]{:S(2)}) copy-start(f32[3,32,128]{2,1,0:T(8,128)} %inlet_ref.3) | copy-start | bytes 147460
  29.0 7.6 %collective-permute-start.2 = (f32[3,128]{1,0:T(4,128)S(1)}, f32[3,128]{1,0:T(4,128)S(1)}, u32[]{:S(2)}, u32[]{:S(2)}) collective-permute-start(f32[3,128]{1,0:T(4,128)S(1)} %middle.1), channel_id=1, source_target_pairs={{0,384},{8,392},{16,400},{24,408},{32,416},{40,424},{48,432},{56,4... | collective-permute-start | bytes 4616 | tf_op jit(solution)/shard_map/ppermute | solution.py:318
